TPU v7x, 32 devices: a whole 2x2x4 slice. The times are simulated.
32 devices in a mesh: member: 8 (over y, x, core), lat: 4 (over z).
Axes of the slice: x: 2, y: 2, z: 4, core: 2. Of those that a mesh axis runs over, the one named last changes fastest.
Arguments:
- state: float32 [32, 32, 8, 256], P('member', 'lat'), may hold values from -6 to 6
- zonal_wind: float32 [32, 8, 256], P('lat'), may hold values from -5 to 5
- meridional_wind: float32 [32, 8, 256], P('lat'), may hold values from -5 to 5
- obs_cell: int32 [32, 8, 128], P('lat'), may hold values from 0 to 255
- obs_value: float32 [32, 8, 128], P('lat'), may hold values from -10 to 10
- obs_weight: float32 [32, 8, 128], P('lat'), may hold values from 1 to 1024
Outputs:
- analysis: float32 [32, 32, 8, 256], P('member', 'lat')
All inputs are finite; a program needn't handle non-finite values.
Results may differ from a plain program's by a relative error of at most 0.00014.
Values sent between devices are 32-bit elements; how exact they have to be, the bound alone decides.
No kernel may reach another device: no remote copies, remote signals or barrier semaphores. Data moves between devices by JAX's collectives and lax.ppermute only.
A program may use at most 64 MiB of HBM per device.

v0:
```python
import jax
import jax.numpy as jnp
from jax import lax
from jax.sharding import PartitionSpec as P

SWEEPS = 3


step_size = 0.3


def extended_2(block, sides, width):
    for axis, dim in sides:
        count = lax.axis_size(axis)
        forward = [(i, i + 1) for i in range(count - 1)]
        backward = [(target, source) for source, target in forward]
        low = lax.ppermute(
            lax.slice_in_dim(block, block.shape[dim] - width, None, axis=dim), axis, forward
        )
        high = lax.ppermute(lax.slice_in_dim(block, 0, width, axis=dim), axis, backward)
        block = jnp.concatenate([low, block, high], axis=dim)
    return block


def advance(padded, zonal, meridional):
    middle = padded[:, 1:-1]
    north_row = padded[:, 2:]
    south_row = padded[:, :-2]
    east_cell = jnp.roll(middle, -1, axis=3)
    west_cell = jnp.roll(middle, 1, axis=3)
    return middle - step_size * (
        (zonal + middle) * (east_cell - west_cell) * 0.5
        + meridional * (north_row - south_row) * 0.5
    )


def analyse(ensemble, observed, values, weights):
    highest = lax.Precision.HIGHEST
    count = ensemble.shape[0]
    obs_mean = jnp.mean(observed, axis=0)
    perturb = observed - obs_mean
    innovation = values - obs_mean
    gram = jnp.einsum("kro,lro->rkl", perturb * weights, perturb, precision=highest)
    identity = jnp.eye(count, dtype=jnp.float32)
    system = gram + (count - 1.0) * identity
    frobenius = jnp.sqrt(jnp.sum(system * system, axis=(1, 2)))
    iterate = system / frobenius[:, None, None]
    inverse = jnp.broadcast_to(identity, system.shape)
    for sweep in range(SWEEPS):
        product = jnp.einsum("rij,rjk->rik", inverse, iterate, precision=highest)
        factor = 1.5 * identity - 0.5 * product
        iterate = jnp.einsum("rij,rjk->rik", iterate, factor, precision=highest)
        inverse = jnp.einsum("rij,rjk->rik", factor, inverse, precision=highest)
    root = inverse / jnp.sqrt(frobenius)[:, None, None]
    covariance = jnp.einsum("rij,rjk->rik", root, root, precision=highest)
    projected = jnp.einsum("kro,ro->rk", perturb, weights * innovation, precision=highest)
    mean_weights = jnp.einsum("rkl,rl->rk", covariance, projected, precision=highest)
    transform = mean_weights[:, :, None] + jnp.sqrt(count - 1.0) * root
    state_mean = jnp.mean(ensemble, axis=0)
    state_pert = ensemble - state_mean
    return state_mean + jnp.einsum("rkm,krn->mrn", transform, state_pert, precision=highest)


def pick_columns(rows, cells):
    return jax.vmap(
        lambda block, index: jnp.take(block, index, axis=1), in_axes=(1, 0), out_axes=1
    )(rows, cells)


def body(state, zonal_wind, meridional_wind, obs_cell, obs_value, obs_weight):
    members_dev, lat_dev, levels, longitudes = state.shape
    groups = lax.axis_size("member")
    regions = lat_dev * levels // groups
    count = members_dev * groups
    stacked = jnp.concatenate([state, zonal_wind[None], meridional_wind[None]], axis=0)
    extended = extended_2(stacked, (("lat", 1),), 2)
    first = advance(
        extended[:members_dev], extended[members_dev, 1:-1], extended[members_dev + 1, 1:-1]
    )
    field = advance(first, zonal_wind, meridional_wind)
    flat = field.reshape(members_dev, lat_dev * levels, longitudes)
    all_cells = obs_cell.reshape(lat_dev * levels, -1)
    start = lax.axis_index("member") * regions
    cells = lax.dynamic_slice_in_dim(all_cells, start, regions, 0)
    values = lax.dynamic_slice_in_dim(obs_value.reshape(lat_dev * levels, -1), start, regions, 0)
    weights = lax.dynamic_slice_in_dim(obs_weight.reshape(lat_dev * levels, -1), start, regions, 0)
    ensemble = lax.all_to_all(
        flat.reshape(members_dev, groups, regions, longitudes),
        "member",
        split_axis=1,
        concat_axis=0,
        tiled=True,
    ).reshape(count, regions, longitudes)
    observed = pick_columns(ensemble, cells)
    analysed = analyse(ensemble, observed, values, weights)
    returned = lax.all_to_all(
        analysed.reshape(count, 1, regions, longitudes),
        "member",
        split_axis=0,
        concat_axis=1,
        tiled=True,
    )
    return returned.reshape(state.shape)


def solution(mesh):
    in_specs = (
        P("member", "lat", None, None),
        P("lat", None, None),
        P("lat", None, None),
        P("lat", None, None),
        P("lat", None, None),
        P("lat", None, None),
    )
    out_specs = P("member", "lat", None, None)
    return jax.shard_map(body, mesh=mesh, in_specs=in_specs, out_specs=out_specs, check_vma=False)
```

profile of v0, /device:TPU:0, one launch (start us, length us, event | category | flops | bytes accessed | tf_op | source)
XLA Modules:
  0.0 47.4 jit_solution(7783131057567353832)
XLA Ops:
  0.0 0.0 copy-start
  0.0 0.0 copy-start.1
  0.0 0.0 copy-start.2
  0.0 1.0 %pad_maximum_fusion.7 = (f32[6,2,8,256]{3,2,0,1:T(8,128)S(1)}, f32[6,2,8,256]{3,2,0,1:T(8,128)S(1)}) fusion(f32[1,8,8,256]{3,2,0,1:T(8,128)} %bitcast.75, f32[1,8,8,256]{3,2,0,1:T(8,128)} %bitcast.79, f32[4,8,8,256]{3,2,1,0:T(8,128)} %param.6), kind=kLoop, calls=%fused_computation.45 | loop fusion | flops 98304 | bytes 589824 | tf_op jit(solution)/shard_map/concatenate | solution.py:75
  1.0 5.0 %collective-permute-start = (f32[6,2,8,256]{3,2,0,1:T(8,128)S(1)}, f32[6,2,8,256]{3,2,0,1:T(8,128)S(1)}, u32[]{:S(2)}, u32[]{:S(2)}) collective-permute-start(f32[6,2,8,256]{3,2,0,1:T(8,128)S(1)} %get-tuple-element.12), channel_id=1, source_target_pairs={{0,1},{1,2},{2,3},{4,5},{5,6},{6,7},{8,9},{9,10},{10,11},{12,13},{... | collective-permute-start | bytes 294920 | tf_op jit(solution)/shard_map/ppermute | solution.py:17
  6.0 1.3 %collective-permute-start.1 = (f32[6,2,8,256]{3,2,0,1:T(8,128)S(1)}, f32[6,2,8,256]{3,2,0,1:T(8,128)S(1)}, u32[]{:S(2)}, u32[]{:S(2)}) collective-permute-start(f32[6,2,8,256]{3,2,0,1:T(8,128)S(1)} %get-tuple-element.11), channel_id=1, source_target_pairs={{1,0},{2,1},{3,2},{5,4},{6,5},{7,6},{9,8},{10,9},{11,10},{13,12},{... | collective-permute-start | bytes 294920 | tf_op jit(solution)/shard_map/ppermute | solution.py:20
  7.3 0.7 %fusion.37 = s32[1024]{0:T(1024)S(1)} fusion(s32[64,128]{1,0:T(8,128)} %bitcast.87, s32[]{:T(128)S(6)} %select_n.18), kind=kLoop, calls=%fused_computation.70 | loop fusion | flops 8192 | bytes 8196 | tf_op jit(solution)/shard_map/vmap(jit(_take))/gather | solution.py:66
  8.0 0.2 collective-permute-done
  8.2 4.3 %collective-permute-done.1 = f32[6,2,8,256]{3,2,0,1:T(8,128)S(1)} collective-permute-done((f32[6,2,8,256]{3,2,0,1:T(8,128)S(1)}, f32[6,2,8,256]{3,2,0,1:T(8,128)S(1)}, u32[]{:S(2)}, u32[]{:S(2)}) %collective-permute-start.1) | collective-permute-done | bytes 98336 | tf_op jit(solution)/shard_map/ppermute | solution.py:20
  12.5 0.0 copy-done
  12.5 0.0 copy-done.1
  12.5 0.0 copy-done.2
  12.6 0.2 fusion.42
  12.7 0.1 fusion.41
  12.9 0.2 fusion.8
  13.1 0.1 fusion.44
  13.3 0.1 fusion.43
  13.4 0.9 %fusion.13 = f32[4,8,8,256]{3,2,0,1:T(8,128)} fusion(f32[4,10,8,256]{3,2,0,1:T(8,128)S(1)} %fusion.8, f32[4,8,8,1]{3,2,0,1:T(8,128)S(1)} %get-tuple-element.14, f32[4,8,8,255]{3,2,0,1:T(8,128)S(1)} %get-tuple-element.16, f32[4,8,8,255]{3,2,0,1:T(8,128)S(1)} %get-tuple-element.15, f32[4,8,8,1]{3,2,0,1:T(8,128)S(1)} %get-tuple-element.13, ...), kind=kLoop, calls=%fused_computation.30 | loop fusion | flops 655360 | bytes 1703936 | tf_op jit(solution)/shard_map/sub | solution.py:31
  14.3 3.7 %all-to-all-start = ((f32[4,8,8,256]{3,2,0,1:T(8,128)}), f32[4,8,8,256]{3,2,0,1:T(8,128)S(1)}, u32[]{:S(2)}, u32[]{:S(2)}) async-start(f32[4,8,8,256]{3,2,0,1:T(8,128)} %fusion.13), calls=%async_computation | async-start | bytes 524288 | tf_op jit(solution)/shard_map/all_to_all | solution.py:87
  18.0 0.7 %compare_and_fusion = pred[8,128]{1,0:T(8,128)(4,1)S(1)} fusion(s32[64,128]{1,0:T(8,128)} %bitcast.88, s32[]{:T(128)S(6)} %select_n.18), kind=kLoop, calls=%fused_computation.73 | loop fusion | flops 6144 | bytes 5124 | tf_op jit(solution)/shard_map/vmap(jit(_take))/and | solution.py:66
  18.7 6.2 %all-to-all-done = f32[4,8,8,256]{3,2,0,1:T(8,128)S(1)} async-done(((f32[4,8,8,256]{3,2,0,1:T(8,128)}), f32[4,8,8,256]{3,2,0,1:T(8,128)S(1)}, u32[]{:S(2)}, u32[]{:S(2)}) %all-to-all-start) | async-done | bytes 262176 | tf_op jit(solution)/shard_map/all_to_all | solution.py:87
  24.9 0.4 copy.19
  25.3 6.8 %gather_fusion = f32[1024,32]{1,0:T(8,128)S(1)} fusion(f32[8,32,256]{1,2,0:T(8,128)S(1)} %bitcast.74, s32[1024]{0:T(1024)S(1)} %fusion.37), kind=kCustom, calls=%fused_computation | custom fusion | bytes 270336 | tf_op jit(solution)/shard_map/vmap(jit(_take))/gather | solution.py:66
  32.1 0.2 copy.20
  32.3 0.7 %subtract_multiply_fusion = (f32[8,128]{1,0:T(8,128)S(1)}, f32[8,128]{1,0:T(8,128)S(1)}, f32[8,128]{1,0:T(8,128)S(1)}) fusion(f32[64,128]{1,0:T(8,128)} %bitcast.89, s32[]{:T(128)S(6)} %select_n.18, f32[64,128]{1,0:T(8,128)} %bitcast.90, f32[8,128]{1,0:T(8,128)S(1)} %bitcast_reduce_fusion.1), kind=kLoop, calls=%fused_computation.71 | loop fusion | flops 3072 | bytes 24580 | tf_op jit(solution)/shard_map/mul | solution.py:56
  33.0 0.4 multiply_reduce_fusion
  33.4 0.3 fusion.3
  33.8 0.3 fusion.33
  34.1 0.3 fusion.28
  34.4 0.3 fusion.2
  34.6 0.3 fusion.46
  34.9 0.3 fusion.45
  35.2 0.3 convolution_bitcast_fusion
  35.5 0.3 fusion.1
  35.7 0.3 convolution_divide_fusion
  36.0 0.3 fusion.47
  36.3 0.3 fusion.48
  36.7 0.5 %fusion = f32[32,1,8,256]{3,0,2,1:T(8,128)S(1)} fusion(f32[32,8,256]{2,1,0:T(8,128)S(1)} %broadcast_subtract_fusion, f32[8,32,32]{2,1,0:T(8,128)S(1)} %convolution_divide_fusion, f32[8,256]{1,0:T(8,128)S(1)} %broadcast_multiply_fusion, f32[8,32]{1,0:T(8,128)S(1)} %bitcast.85), kind=kOutput, calls=%fused_computation.2 | convolution fusion | flops 25247744 | bytes 566272 | tf_op jit(solution)/shard_map/rkm,krn->mrn/dot_general | solution.py:61
  37.2 0.2 copy.23
  37.3 9.3 %all_to_all.33 = f32[32,1,8,256]{3,2,1,0:T(8,128)S(1)} all-to-all(f32[32,1,8,256]{3,2,1,0:T(8,128)S(1)} %copy.23), channel_id=1, replica_groups=mesh['member'=8,'lat'=4] {'member'}, dimensions={0} | all-to-all | bytes 524288 | tf_op jit(solution)/shard_map/all_to_all | solution.py:96
  46.7 0.7 %copy.41 = f32[8,4,1,8,256]{4,3,0,1,2:T(8,128)} copy(f32[8,4,1,8,256]{4,3,1,0,2:T(8,128)S(1)} %bitcast.83) | data formatting | bytes 524288 | tf_op jit(solution)/shard_map/all_to_all | solution.py:96
  (10 shorter events, 0.2 us)
Async XLA Ops:
  0.0 12.5 %copy-start = (f32[4,8,8,256]{3,2,1,0:T(8,128)S(1)}, f32[4,8,8,256]{3,2,1,0:T(8,128)}, u32[]{:S(2)}) copy-start(f32[4,8,8,256]{3,2,1,0:T(8,128)} %param.6) | copy-start | bytes 786436
  0.0 12.5 %copy-start.1 = (f32[8,8,256]{2,1,0:T(8,128)S(1)}, f32[8,8,256]{2,1,0:T(8,128)}, u32[]{:S(2)}) copy-start(f32[8,8,256]{2,1,0:T(8,128)} %param.8) | copy-start | bytes 196612
  0.0 12.5 %copy-start.2 = (f32[8,8,256]{2,1,0:T(8,128)S(1)}, f32[8,8,256]{2,1,0:T(8,128)}, u32[]{:S(2)}) copy-start(f32[8,8,256]{2,1,0:T(8,128)} %param.7) | copy-start | bytes 196612
  1.0 7.2 %collective-permute-start = (f32[6,2,8,256]{3,2,0,1:T(8,128)S(1)}, f32[6,2,8,256]{3,2,0,1:T(8,128)S(1)}, u32[]{:S(2)}, u32[]{:S(2)}) collective-permute-start(f32[6,2,8,256]{3,2,0,1:T(8,128)S(1)} %get-tuple-element.12), channel_id=1, source_target_pairs={{0,1},{1,2},{2,3},{4,5},{5,6},{6,7},{8,9},{9,10},{10,11},{12,13},{... | collective-permute-start | bytes 294920 | tf_op jit(solution)/shard_map/ppermute | solution.py:17
  6.0 6.5 %collective-permute-start.1 = (f32[6,2,8,256]{3,2,0,1:T(8,128)S(1)}, f32[6,2,8,256]{3,2,0,1:T(8,128)S(1)}, u32[]{:S(2)}, u32[]{:S(2)}) collective-permute-start(f32[6,2,8,256]{3,2,0,1:T(8,128)S(1)} %get-tuple-element.11), channel_id=1, source_target_pairs={{1,0},{2,1},{3,2},{5,4},{6,5},{7,6},{9,8},{10,9},{11,10},{13,12},{... | collective-permute-start | bytes 294920 | tf_op jit(solution)/shard_map/ppermute | solution.py:20
  14.3 10.6 %all-to-all-start = ((f32[4,8,8,256]{3,2,0,1:T(8,128)}), f32[4,8,8,256]{3,2,0,1:T(8,128)S(1)}, u32[]{:S(2)}, u32[]{:S(2)}) async-start(f32[4,8,8,256]{3,2,0,1:T(8,128)} %fusion.13), calls=%async_computation | async-start | bytes 524288 | tf_op jit(solution)/shard_map/all_to_all | solution.py:87
where the time goes:
time: 47.8 us; the launch traced here: 47.4 us
  waiting for transfers between devices  10.7 us (22%)
  starting transfers between devices  9.98 us (21%)
  blocking collectives  9.32 us (19%)
  local copies, waits for them, and re-layouts  8.71 us (18%)
  other arithmetic  4.47 us (9%)
  matrix products  4.01 us (8%)
    all_to_all x1, blocking collectives, body(): lax.all_to_all(analysed.reshape(count, 1, regions, longitudes), 'member',...  9.32 us
    gather x2, local copies, waits for them, and re-layouts, pick_columns(): jnp.take(block, index, axis=1)  6.96 us
    all_to_all x1, waiting for transfers between devices, body(): lax.all_to_all(flat.reshape(members_dev, groups, regions, longitudes), 'm...  6.19 us
    ppermute x1, starting transfers between devices, extended_2(): lax.ppermute(lax.slice_in_dim(block, block.shape[dim] - width, None, axis...  4.97 us
    ppermute x1, waiting for transfers between devices, extended_2(): lax.ppermute(lax.slice_in_dim(block, 0, width, axis=dim), axis, backward)  4.32 us
    all_to_all x1, starting transfers between devices, body(): lax.all_to_all(flat.reshape(members_dev, groups, regions, longitudes), 'm...  3.72 us
    ppermute x1, starting transfers between devices, extended_2(): lax.ppermute(lax.slice_in_dim(block, 0, width, axis=dim), axis, backward)  1.29 us
    sub x2, other arithmetic, advance(): middle - step_size * ((zonal + middle) * (east_cell - west_cell) * 0.5 +...  1.16 us
  transfers between devices with their start and end apart: 3, of which 3 were waited for; matrix products, arithmetic and copies ran while one was open for 3% of the time, Pallas kernels for 0%

commit v1 on v0

v1 whole, which is shorter than its diff:
```python
import functools

import jax
import jax.numpy as jnp
from jax import lax
from jax.experimental import pallas as pl
from jax.experimental.pallas import tpu as pltpu
from jax.sharding import PartitionSpec as P

SWEEPS = 3
step_size = 0.3
VM = pltpu.VMEM


def whole(n):
    return [pl.BlockSpec(memory_space=VM)] * n


def pair_rounds(count):
    def pairs(first):
        partner = list(range(count))
        for i in range(first, count - 1, 2):
            partner[i], partner[i + 1] = i + 1, i
        return [(i, partner[i]) for i in range(count)]

    return pairs(0), pairs(1)


def edge_message(state, zonal, meridional, at_high):
    members, rows, levels, lon = state.shape
    start = jnp.where(at_high, rows - 2, 0)
    row = jnp.where(at_high, rows - 1, 0)
    fields = lax.dynamic_slice_in_dim(state, start, 2, 1)
    winds = [lax.dynamic_slice_in_dim(w, row, 1, 0) for w in (zonal, meridional)]
    return jnp.concatenate([fields.reshape(members * 2, levels, lon), *winds], axis=0)


def advance(south, middle, north, zonal, meridional):
    lon = middle.shape[-1]
    axis = middle.ndim - 1
    east = pltpu.roll(middle, lon - 1, axis)
    west = pltpu.roll(middle, 1, axis)
    return middle - step_size * (
        (zonal + middle) * (east - west) * 0.5 + meridional * (north - south) * 0.5
    )


def forecast_kernel(where_ref, state_ref, e_ref, o_ref, zonal_ref, merid_ref, out_ref):
    members, rows, levels, lon = state_ref.shape
    even = where_ref[0] == 1
    has_low = where_ref[1].astype(jnp.float32)
    has_high = where_ref[2].astype(jnp.float32)

    def halo(i):
        e, o = e_ref[i], o_ref[i]
        low = jnp.where(even, o, e) * has_low
        high = jnp.where(even, e, o) * has_high
        return low, high

    z_low, z_high = halo(members * 2)
    m_low, m_high = halo(members * 2 + 1)
    zonal = [z_low] + [zonal_ref[r] for r in range(rows)] + [z_high]
    merid = [m_low] + [merid_ref[r] for r in range(rows)] + [m_high]
    for m in range(members):
        low0, high0 = halo(2 * m)
        low1, high1 = halo(2 * m + 1)
        q = [low0, low1] + [state_ref[m, r] for r in range(rows)] + [high0, high1]
        first = [
            advance(q[r], q[r + 1], q[r + 2], zonal[r], merid[r]) for r in range(rows + 2)
        ]
        for r in range(rows):
            out_ref[r, m] = advance(
                first[r], first[r + 1], first[r + 2], zonal[r + 1], merid[r + 1]
            )


def forecast(where, state, e_msg, o_msg, zonal, merid):
    members, rows, levels, lon = state.shape
    size = state.size
    return pl.pallas_call(
        forecast_kernel,
        out_shape=jax.ShapeDtypeStruct((rows, members, levels, lon), jnp.float32),
        in_specs=[pl.BlockSpec(memory_space=pltpu.SMEM)] + whole(5),
        out_specs=pl.BlockSpec(memory_space=VM),
        cost_estimate=pl.CostEstimate(
            flops=24 * size, bytes_accessed=8 * size, transcendentals=0
        ),
        name="forecast",
    )(where, state, e_msg, o_msg, zonal, merid)


def cells_kernel(cell_ref, value_ref, weight_ref, dsum_ref, vsum_ref):
    regions, obs = cell_ref.shape
    lon = dsum_ref.shape[1]
    weight = weight_ref[...]
    cell_t = cell_ref[...].T
    weight_t = weight.T
    value_t = (weight * value_ref[...]).T
    index = lax.broadcasted_iota(jnp.int32, (obs, lon), 1)
    for r in range(regions):
        hit = jnp.broadcast_to(cell_t[:, r : r + 1], (obs, lon)) == index
        w = jnp.broadcast_to(weight_t[:, r : r + 1], (obs, lon))
        v = jnp.broadcast_to(value_t[:, r : r + 1], (obs, lon))
        dsum_ref[r : r + 1, :] = jnp.sum(jnp.where(hit, w, 0.0), axis=0, keepdims=True)
        vsum_ref[r : r + 1, :] = jnp.sum(jnp.where(hit, v, 0.0), axis=0, keepdims=True)


def per_cell(cells, values, weights, lon):
    regions, obs = cells.shape
    shape = jax.ShapeDtypeStruct((regions, lon), jnp.float32)
    return pl.pallas_call(
        cells_kernel,
        out_shape=(shape, shape),
        in_specs=whole(3),
        out_specs=tuple(whole(2)),
        cost_estimate=pl.CostEstimate(
            flops=4 * regions * obs * lon,
            bytes_accessed=4 * (3 * regions * obs + 2 * regions * lon),
            transcendentals=0,
        ),
        name="per_cell",
    )(cells, values, weights)


def split(x):
    high = x.astype(jnp.bfloat16)
    low = (x - high.astype(jnp.float32)).astype(jnp.bfloat16)
    return high, low


def product(a, b, dims=((1,), (0,))):
    def dot(x, y):
        return lax.dot_general(x, y, (dims, ((), ())), preferred_element_type=jnp.float32)

    return dot(a[0], b[0]) + (dot(a[0], b[1]) + dot(a[1], b[0]))


def analysis_kernel(regions, ens_ref, dsum_ref, vsum_ref, out_ref):
    size, lon = ens_ref.shape
    count = size // regions

    def over_members(x):
        if regions == 1:
            return jnp.sum(x, axis=0, keepdims=True)
        return jnp.sum(x.reshape(count, regions, x.shape[-1]), axis=0)

    def spread(x):
        if regions == 1:
            return jnp.broadcast_to(x, (size, x.shape[-1]))
        x = jnp.broadcast_to(x[None], (count, regions, x.shape[-1]))
        return x.reshape(size, x.shape[-1])

    ens = ens_ref[...]
    dsum = dsum_ref[...]
    mean = over_members(ens) * (1.0 / count)
    pert = ens - spread(mean)
    pull = vsum_ref[...] - dsum * mean

    row = lax.broadcasted_iota(jnp.int32, (size, size), 0)
    col = lax.broadcasted_iota(jnp.int32, (size, size), 1)
    same = lax.rem(row, regions) == lax.rem(col, regions)
    one = jnp.where(row == col, 1.0, 0.0)

    pert_s = split(pert)
    gram = product(split(pert * spread(dsum)), pert_s, ((1,), (1,)))
    system = jnp.where(same, gram, 0.0) + (count - 1.0) * one
    total = over_members(jnp.sum(system * system, axis=1, keepdims=True))
    frob = jnp.sqrt(total)
    iterate = system * spread(1.0 / frob)
    iterate_s = split(iterate)
    inverse_s = None
    for sweep in range(SWEEPS):
        step = iterate if inverse_s is None else product(inverse_s, iterate_s)
        factor_s = split(1.5 * one - 0.5 * step)
        if sweep == SWEEPS - 1:
            break
        iterate_s = split(product(iterate_s, factor_s))
        inverse_s = factor_s if inverse_s is None else split(product(factor_s, inverse_s))
    part_s = split(product(inverse_s, pert_s))
    update = product(factor_s, part_s) * spread(lax.rsqrt(frob))
    gain = jnp.sum(update * spread(pull), axis=1, keepdims=True)
    shift = mean + over_members(update * gain)
    out_ref[...] = spread(shift) + jnp.sqrt(count - 1.0) * update


def analysis(ens, dsum, vsum):
    size, lon = ens.shape
    regions = dsum.shape[0]
    return pl.pallas_call(
        functools.partial(analysis_kernel, regions),
        out_shape=jax.ShapeDtypeStruct((size, lon), jnp.float32),
        in_specs=whole(3),
        out_specs=pl.BlockSpec(memory_space=VM),
        cost_estimate=pl.CostEstimate(
            flops=48 * size * size * lon, bytes_accessed=8 * size * lon, transcendentals=0
        ),
        name="analysis",
    )(ens, dsum, vsum)


def body(state, zonal_wind, meridional_wind, obs_cell, obs_value, obs_weight):
    members_dev, lat_dev, levels, longitudes = state.shape
    groups = lax.axis_size("member")
    bands = lax.axis_size("lat")
    regions = lat_dev * levels // groups
    count = members_dev * groups
    band = lax.axis_index("lat")
    even = lax.rem(band, 2) == 0

    first_round, second_round = pair_rounds(bands)
    e_msg = lax.ppermute(
        edge_message(state, zonal_wind, meridional_wind, even), "lat", first_round
    )
    o_msg = lax.ppermute(
        edge_message(state, zonal_wind, meridional_wind, jnp.logical_not(even)),
        "lat",
        second_round,
    )

    def mine(x):
        x = x.reshape(groups, regions, x.shape[-1])
        return lax.dynamic_index_in_dim(x, lax.axis_index("member"), 0, keepdims=False)

    dsum, vsum = per_cell(mine(obs_cell), mine(obs_value), mine(obs_weight), longitudes)

    where = jnp.stack([even, band > 0, band < bands - 1]).astype(jnp.int32)
    field = forecast(where, state, e_msg, o_msg, zonal_wind, meridional_wind)
    blocks = field.transpose(1, 0, 2, 3).reshape(members_dev, groups, regions, longitudes)
    ensemble = lax.all_to_all(
        blocks.transpose(1, 0, 2, 3), "member", split_axis=0, concat_axis=0, tiled=True
    )
    analysed = analysis(ensemble.reshape(count * regions, longitudes), dsum, vsum)
    returned = lax.all_to_all(
        analysed.reshape(groups, members_dev, regions, longitudes),
        "member",
        split_axis=0,
        concat_axis=0,
        tiled=True,
    )
    return returned.transpose(1, 0, 2, 3).reshape(state.shape)


def solution(mesh):
    in_specs = (
        P("member", "lat", None, None),
        P("lat", None, None),
        P("lat", None, None),
        P("lat", None, None),
        P("lat", None, None),
        P("lat", None, None),
    )
    out_specs = P("member", "lat", None, None)
    return jax.shard_map(body, mesh=mesh, in_specs=in_specs, out_specs=out_specs, check_vma=False)
```

time: 47.8 us -> 40.3 us (0.84)
  Pallas kernels: 0 us -> 8.05 us
  waiting for transfers between devices: 10.7 us -> 4.92 us
  matrix products: 4.01 us -> 0 us
  other arithmetic: 4.47 us -> 0.62 us
  local copies, waits for them, and re-layouts: 8.71 us -> 5.6 us
  blocking collectives: 9.32 us -> 10.2 us
    pallas_call x0 -> x3, Pallas kernels: none -> 8.05 us  [the longest x1 3.88 us: analysis(): pl.pallas_call(functools.partial(analysis_kernel, regions), out_shape=jax...]
    gather x2 -> x0, local copies, waits for them, and re-layouts: 6.96 us -> none  [pick_columns(): jnp.take(block, index, axis=1)]
    dot_general x13 -> x0, matrix products: 4.01 us -> none  [the longest x3 0.85 us: analyse(): product = jnp.einsum('rij,rjk->rik', inverse, iterate, precision=highest)]
    all_to_all x1, waiting for transfers between devices: 6.19 us -> 3.1 us  [body(): lax.all_to_all(blocks.transpose(1, 0, 2, 3), 'member', split_axis=0, conc...]
    ppermute x2, waiting for transfers between devices: 4.49 us -> 1.82 us  [the longest x1 1.81 us: body(): lax.ppermute(edge_message(state, zonal_wind, meridional_wind, even), 'lat...]
    squeeze x0 -> x2, local copies, waits for them, and re-layouts: none -> 1.89 us  [mine(): lax.dynamic_index_in_dim(x, lax.axis_index('member'), 0, keepdims=False)]
    dynamic_slice x0 -> x2, local copies, waits for them, and re-layouts: none -> 1.65 us  [the longest x1 0.89 us: edge_message(): fields = lax.dynamic_slice_in_dim(state, start, 2, 1)]
    unnamed x6 -> x8, local copies, waits for them, and re-layouts: 0.01 us -> 1.34 us
  transfers between devices with their start and end apart: 3 -> 3, of which waited for: 3 -> 2; matrix products, arithmetic and copies ran while one was open for 3% -> 6% of each run, Pallas kernels for 0% -> 5%
where the time goes in v1:
time: 40.3 us; the launch traced here: 39.8 us
  starting transfers between devices  10.3 us (26%)
  blocking collectives  10.2 us (25%)
  Pallas kernels  8.05 us (20%)
  local copies, waits for them, and re-layouts  5.6 us (14%)
  waiting for transfers between devices  4.92 us (12%)
  other arithmetic  0.62 us (2%)
    all_to_all x1, blocking collectives, body(): lax.all_to_all(analysed.reshape(groups, members_dev, regions, longitudes)...  10.2 us
    ppermute x1, starting transfers between devices, body(): lax.ppermute(edge_message(state, zonal_wind, meridional_wind, even), 'lat...  5.94 us
    pallas_call x1, Pallas kernels, analysis(): pl.pallas_call(functools.partial(analysis_kernel, regions), out_shape=jax...  3.88 us
    all_to_all x1, starting transfers between devices, body(): lax.all_to_all(blocks.transpose(1, 0, 2, 3), 'member', split_axis=0, conc...  3.72 us
    all_to_all x1, waiting for transfers between devices, body(): lax.all_to_all(blocks.transpose(1, 0, 2, 3), 'member', split_axis=0, conc...  3.1 us
    pallas_call x1, Pallas kernels, forecast(): pl.pallas_call(forecast_kernel, out_shape=jax.ShapeDtypeStruct((rows, mem...  2.27 us
    pallas_call x1, Pallas kernels, per_cell(): pl.pallas_call(cells_kernel, out_shape=(shape, shape), in_specs=whole(3),...  1.9 us
    squeeze x2, local copies, waits for them, and re-layouts, mine(): lax.dynamic_index_in_dim(x, lax.axis_index('member'), 0, keepdims=False)  1.89 us
  transfers between devices with their start and end apart: 3, of which 2 were waited for; matrix products, arithmetic and copies ran while one was open for 6% of the time, Pallas kernels for 5%

profile of v1, /device:TPU:0, one launch (start us, length us, event | category | flops | bytes accessed | tf_op | source)
XLA Modules:
  0.0 39.8 jit_solution(6885521018911056248)
XLA Ops:
  0.0 0.0 copy-start
  0.0 0.9 %constant_dynamic-slice_fusion.2 = (f32[4,2,8,256]{3,2,1,0:T(8,128)S(1)}, f32[4,2,8,256]{3,2,1,0:T(8,128)S(1)}) fusion(f32[4,8,8,256]{3,2,1,0:T(8,128)} %state_ref.1, s32[]{:T(128)S(6)} %select_n.28, s32[]{:T(128)S(6)} %select_n.26), kind=kLoop, calls=%fused_computation.7 | loop fusion | bytes 262152 | tf_op jit(solution)/shard_map/dynamic_slice | solution.py:33
  0.9 0.8 %constant_dynamic-slice_fusion = (f32[1,8,256]{2,1,0:T(8,128)S(1)}, f32[1,8,256]{2,1,0:T(8,128)S(1)}, f32[1,8,256]{2,1,0:T(8,128)S(1)}, f32[1,8,256]{2,1,0:T(8,128)S(1)}) fusion(f32[8,8,256]{2,1,0:T(8,128)} %merid_ref.1, s32[]{:T(128)S(6)} %select_n.29, s32[]{:T(128)S(6)} %select_n.27, f32[8,8,256]{2,1,0:T(8,128)} %zonal_ref.1), kind=kLoop, calls=%fused_computation.5 | loop fusion | bytes 65544 | tf_op jit(solution)/shard_map/dynamic_slice | solution.py:34
  1.7 0.7 %collective-permute-start.1 = (f32[10,8,256]{2,1,0:T(8,128)S(1)}, f32[10,8,256]{2,1,0:T(8,128)S(1)}, u32[]{:S(2)}, u32[]{:S(2)}) collective-permute-start(f32[10,8,256]{2,1,0:T(8,128)S(1)} %pad_maximum_fusion.1), channel_id=1, source_target_pairs={{0,0},{1,2},{2,1},{3,3},{4,4},{5,6},{6,5},{7,7},{8,8},{9,10},{10,9... | collective-permute-start | bytes 245768 | tf_op jit(solution)/shard_map/ppermute | solution.py:214
  2.4 5.9 %collective-permute-start = (f32[10,8,256]{2,1,0:T(8,128)S(1)}, f32[10,8,256]{2,1,0:T(8,128)S(1)}, u32[]{:S(2)}, u32[]{:S(2)}) collective-permute-start(f32[10,8,256]{2,1,0:T(8,128)S(1)} %pad_maximum_fusion), channel_id=1, source_target_pairs={{0,1},{1,0},{2,3},{3,2},{4,5},{5,4},{6,7},{7,6},{8,9},{9,8},{10,11... | collective-permute-start | bytes 245768 | tf_op jit(solution)/shard_map/ppermute | solution.py:211
  8.3 0.6 %add_convert_fusion.where_ref = s32[3]{0:T(128)} fusion(pred[1]{0:T(512)(128)(4,1)} %bitcast.2, pred[1]{0:T(512)(128)(4,1)} %bitcast.1, pred[1]{0:T(512)(128)(4,1)} %bitcast), kind=kLoop, calls=%fused_computation.11 | loop fusion | flops 9 | bytes 15 | tf_op jit(solution)/shard_map/convert_element_type | solution.py:226
  8.9 0.0 collective-permute-done.1.o_ref
  8.9 0.0 copy-start.2
  8.9 1.8 %collective-permute-done.e_ref = f32[10,8,256]{2,1,0:T(8,128)S(1)} collective-permute-done((f32[10,8,256]{2,1,0:T(8,128)S(1)}, f32[10,8,256]{2,1,0:T(8,128)S(1)}, u32[]{:S(2)}, u32[]{:S(2)}) %collective-permute-start) | collective-permute-done | bytes 81952 | tf_op jit(solution)/shard_map/ppermute | solution.py:211
  10.7 0.0 copy-done.2
  10.7 0.0 copy-start.3
  10.7 0.6 %copy-done.3 = f32[10,8,256]{2,1,0:T(8,128)} copy-done((f32[10,8,256]{2,1,0:T(8,128)}, f32[10,8,256]{2,1,0:T(8,128)S(1)}, u32[]{:S(2)}) %copy-start.3) | copy-done | bytes 81944
  11.3 2.3 %forecast.1 = f32[8,4,8,256]{3,2,1,0:T(8,128)} custom-call(s32[3]{0:T(128)} %add_convert_fusion.where_ref, f32[4,8,8,256]{3,2,1,0:T(8,128)} %state_ref.1, f32[10,8,256]{2,1,0:T(8,128)} %copy-done.3, f32[10,8,256]{2,1,0:T(8,128)} %copy-done.2, f32[8,8,256]{2,1,0:T(8,128)} %zonal_ref.1, f32[8,8,256]{2,1,0:T(8,128)} %merid_ref.1), custom_call_target="tpu_custom_call" | custom-call | flops 1572864 | bytes 524288 | tf_op jit(solution)/shard_map/forecast/pallas_call | solution.py:80
  13.6 3.7 %all-to-all-start = ((f32[8,4,8,256]{3,2,1,0:T(8,128)}), f32[8,4,8,256]{3,2,1,0:T(8,128)S(1)}, u32[]{:S(2)}, u32[]{:S(2)}) async-start(f32[8,4,8,256]{3,2,1,0:T(8,128)} %forecast.1), calls=%async_computation | async-start | bytes 524288 | tf_op jit(solution)/shard_map/all_to_all | solution.py:229
  17.3 0.0 copy-done
  17.4 0.6 %dynamic-slice_bitcast_fusion.2.cell_ref = s32[8,128]{1,0:T(8,128)} fusion(s32[8,8,128]{2,1,0:T(8,128)S(1)} %copy-done, s32[]{:T(128)S(6)} %select_n.30), kind=kLoop, calls=%fused_computation.4 | loop fusion | bytes 8196 | tf_op jit(solution)/shard_map/jit(dynamic_index_in_dim)/squeeze | solution.py:222
  17.9 1.3 %dynamic-slice_bitcast_fusion = (f32[8,128]{1,0:T(8,128)}, f32[8,128]{1,0:T(8,128)}) fusion(f32[8,8,128]{2,1,0:T(8,128)} %param.11, s32[]{:T(128)S(6)} %select_n.30, f32[8,8,128]{2,1,0:T(8,128)} %param.10), kind=kLoop, calls=%fused_computation.2 | loop fusion | bytes 16388 | tf_op jit(solution)/shard_map/jit(dynamic_index_in_dim)/squeeze | solution.py:222
  19.2 1.9 %per_cell.1 = (f32[8,256]{1,0:T(8,128)}, f32[8,256]{1,0:T(8,128)}) custom-call(s32[8,128]{1,0:T(8,128)} %dynamic-slice_bitcast_fusion.2.cell_ref, f32[8,128]{1,0:T(8,128)} %get-tuple-element.18.value_ref, f32[8,128]{1,0:T(8,128)} %get-tuple-element.17.weight_ref), custom_call_target="tpu_custom_call" | custom-call | flops 1048576 | bytes 28672 | tf_op jit(solution)/shard_map/per_cell/pallas_call | solution.py:111
  21.1 3.1 %all-to-all-done = f32[8,4,8,256]{3,2,1,0:T(8,128)S(1)} async-done(((f32[8,4,8,256]{3,2,1,0:T(8,128)}), f32[8,4,8,256]{3,2,1,0:T(8,128)S(1)}, u32[]{:S(2)}, u32[]{:S(2)}) %all-to-all-start) | async-done | bytes 262176 | tf_op jit(solution)/shard_map/all_to_all | solution.py:229
  24.2 0.0 copy-start.1
  24.3 0.7 %copy-done.1 = f32[8,4,8,256]{3,2,1,0:T(8,128)} copy-done((f32[8,4,8,256]{3,2,1,0:T(8,128)}, f32[8,4,8,256]{3,2,1,0:T(8,128)S(1)}, u32[]{:S(2)}) %copy-start.1) | copy-done | bytes 262168
  25.0 3.9 %analysis.1 = f32[256,256]{1,0:T(8,128)} custom-call(f32[256,256]{1,0:T(8,128)} %bitcast.15, f32[8,256]{1,0:T(8,128)} %get-tuple-element.7.dsum_ref, f32[8,256]{1,0:T(8,128)} %get-tuple-element.8.vsum_ref), custom_call_target="tpu_custom_call" | custom-call | flops 805306368 | bytes 524288 | tf_op jit(solution)/shard_map/analysis/pallas_call | solution.py:189
  28.8 10.2 %all_to_all.10 = f32[8,4,8,256]{3,2,1,0:T(8,128)S(1)} all-to-all(f32[8,4,8,256]{3,2,1,0:T(8,128)} %bitcast.16), channel_id=1, replica_groups=mesh['member'=8,'lat'=4] {'member'}, dimensions={0} | all-to-all | bytes 524288 | tf_op jit(solution)/shard_map/all_to_all | solution.py:233
  39.0 0.7 %copy.8 = f32[4,8,8,256]{3,2,1,0:T(8,128)} copy(f32[4,8,8,256]{3,2,0,1:T(8,128)S(1)} %bitcast.14) | data formatting | bytes 524288 | tf_op jit(solution)/shard_map/transpose | solution.py:240
  (2 shorter events, 0.0 us)
Async XLA Ops:
  0.0 17.3 %copy-start = (s32[8,8,128]{2,1,0:T(8,128)S(1)}, s32[8,8,128]{2,1,0:T(8,128)}, u32[]{:S(2)}) copy-start(s32[8,8,128]{2,1,0:T(8,128)} %param.9) | copy-start | bytes 98308
  1.7 7.2 %collective-permute-start.1 = (f32[10,8,256]{2,1,0:T(8,128)S(1)}, f32[10,8,256]{2,1,0:T(8,128)S(1)}, u32[]{:S(2)}, u32[]{:S(2)}) collective-permute-start(f32[10,8,256]{2,1,0:T(8,128)S(1)} %pad_maximum_fusion.1), channel_id=1, source_target_pairs={{0,0},{1,2},{2,1},{3,3},{4,4},{5,6},{6,5},{7,7},{8,8},{9,10},{10,9... | collective-permute-start | bytes 245768 | tf_op jit(solution)/shard_map/ppermute | solution.py:214
  2.4 8.4 %collective-permute-start = (f32[10,8,256]{2,1,0:T(8,128)S(1)}, f32[10,8,256]{2,1,0:T(8,128)S(1)}, u32[]{:S(2)}, u32[]{:S(2)}) collective-permute-start(f32[10,8,256]{2,1,0:T(8,128)S(1)} %pad_maximum_fusion), channel_id=1, source_target_pairs={{0,1},{1,0},{2,3},{3,2},{4,5},{5,4},{6,7},{7,6},{8,9},{9,8},{10,11... | collective-permute-start | bytes 245768 | tf_op jit(solution)/shard_map/ppermute | solution.py:211
  8.9 1.8 %copy-start.2 = (f32[10,8,256]{2,1,0:T(8,128)}, f32[10,8,256]{2,1,0:T(8,128)S(1)}, u32[]{:S(2)}) copy-start(f32[10,8,256]{2,1,0:T(8,128)S(1)} %collective-permute-done.1.o_ref) | copy-start | bytes 245764
  10.7 0.6 %copy-start.3 = (f32[10,8,256]{2,1,0:T(8,128)}, f32[10,8,256]{2,1,0:T(8,128)S(1)}, u32[]{:S(2)}) copy-start(f32[10,8,256]{2,1,0:T(8,128)S(1)} %collective-permute-done.e_ref) | copy-start | bytes 245764
  13.6 10.6 %all-to-all-start = ((f32[8,4,8,256]{3,2,1,0:T(8,128)}), f32[8,4,8,256]{3,2,1,0:T(8,128)S(1)}, u32[]{:S(2)}, u32[]{:S(2)}) async-start(f32[8,4,8,256]{3,2,1,0:T(8,128)} %forecast.1), calls=%async_computation | async-start | bytes 524288 | tf_op jit(solution)/shard_map/all_to_all | solution.py:229
  24.2 0.7 %copy-start.1 = (f32[8,4,8,256]{3,2,1,0:T(8,128)}, f32[8,4,8,256]{3,2,1,0:T(8,128)S(1)}, u32[]{:S(2)}) copy-start(f32[8,4,8,256]{3,2,1,0:T(8,128)S(1)} %all-to-all-done) | copy-start | bytes 786436

commit v2 on v1

--- a/solution.py
+++ b/solution.py
@@ -10,6 +10,7 @@
 SWEEPS = 3
 step_size = 0.3
 VM = pltpu.VMEM
+SMALL = pltpu.CompilerParams(vmem_limit_bytes=12 * 2**20)
 
 
 def whole(n):
@@ -26,13 +27,30 @@
     return pairs(0), pairs(1)
 
 
-def edge_message(state, zonal, meridional, at_high):
+def edges_kernel(state_ref, zonal_ref, merid_ref, e_ref, o_ref):
+    members, rows, levels, lon = state_ref.shape
+    odd = lax.rem(lax.axis_index("lat"), 2)
+    for out_ref, low in ((e_ref, odd), (o_ref, 1 - odd)):
+        first = (1 - low) * (rows - 2)
+        edge = (1 - low) * (rows - 1)
+        for m in range(members):
+            out_ref[2 * m] = state_ref[m, first]
+            out_ref[2 * m + 1] = state_ref[m, first + 1]
+        out_ref[2 * members] = zonal_ref[edge]
+        out_ref[2 * members + 1] = merid_ref[edge]
+
+
+def edge_messages(state, zonal, meridional):
     members, rows, levels, lon = state.shape
-    start = jnp.where(at_high, rows - 2, 0)
-    row = jnp.where(at_high, rows - 1, 0)
-    fields = lax.dynamic_slice_in_dim(state, start, 2, 1)
-    winds = [lax.dynamic_slice_in_dim(w, row, 1, 0) for w in (zonal, meridional)]
-    return jnp.concatenate([fields.reshape(members * 2, levels, lon), *winds], axis=0)
+    shape = jax.ShapeDtypeStruct((2 * members + 2, levels, lon), jnp.float32)
+    return pl.pallas_call(
+        edges_kernel,
+        out_shape=(shape, shape),
+        in_specs=whole(3),
+        out_specs=tuple(whole(2)),
+        compiler_params=SMALL,
+        name="edges",
+    )(state, zonal, meridional)
 
 
 def advance(south, middle, north, zonal, meridional):
@@ -45,16 +63,19 @@
     )
 
 
-def forecast_kernel(where_ref, state_ref, e_ref, o_ref, zonal_ref, merid_ref, out_ref):
+def forecast_kernel(
+    bands, state_ref, e_ref, o_ref, zonal_ref, merid_ref, dsum_ref, vsum_ref, out_ref
+):
     members, rows, levels, lon = state_ref.shape
-    even = where_ref[0] == 1
-    has_low = where_ref[1].astype(jnp.float32)
-    has_high = where_ref[2].astype(jnp.float32)
+    band = lax.axis_index("lat")
+    even = lax.rem(band, 2) == 0
+    has_low = band > 0
+    has_high = band < bands - 1
 
     def halo(i):
         e, o = e_ref[i], o_ref[i]
-        low = jnp.where(even, o, e) * has_low
-        high = jnp.where(even, e, o) * has_high
+        low = jnp.where(has_low, jnp.where(even, o, e), 0.0)
+        high = jnp.where(has_high, jnp.where(even, e, o), 0.0)
         return low, high
 
     z_low, z_high = halo(members * 2)
@@ -74,28 +95,30 @@
             )
 
 
-def forecast(where, state, e_msg, o_msg, zonal, merid):
+def forecast(bands, state, e_msg, o_msg, zonal, merid, dsum, vsum):
     members, rows, levels, lon = state.shape
     size = state.size
     return pl.pallas_call(
-        forecast_kernel,
+        functools.partial(forecast_kernel, bands),
         out_shape=jax.ShapeDtypeStruct((rows, members, levels, lon), jnp.float32),
-        in_specs=[pl.BlockSpec(memory_space=pltpu.SMEM)] + whole(5),
+        in_specs=whole(5) + [pl.BlockSpec(memory_space=pl.ANY)] * 2,
         out_specs=pl.BlockSpec(memory_space=VM),
         cost_estimate=pl.CostEstimate(
             flops=24 * size, bytes_accessed=8 * size, transcendentals=0
         ),
+        compiler_params=SMALL,
         name="forecast",
-    )(where, state, e_msg, o_msg, zonal, merid)
+    )(state, e_msg, o_msg, zonal, merid, dsum, vsum)
 
 
 def cells_kernel(cell_ref, value_ref, weight_ref, dsum_ref, vsum_ref):
-    regions, obs = cell_ref.shape
+    groups, regions, obs = cell_ref.shape
     lon = dsum_ref.shape[1]
-    weight = weight_ref[...]
-    cell_t = cell_ref[...].T
+    mine = lax.axis_index("member")
+    weight = weight_ref[mine]
+    cell_t = cell_ref[mine].T
     weight_t = weight.T
-    value_t = (weight * value_ref[...]).T
+    value_t = (weight * value_ref[mine]).T
     index = lax.broadcasted_iota(jnp.int32, (obs, lon), 1)
     for r in range(regions):
         hit = jnp.broadcast_to(cell_t[:, r : r + 1], (obs, lon)) == index
@@ -106,7 +129,7 @@
 
 
 def per_cell(cells, values, weights, lon):
-    regions, obs = cells.shape
+    groups, regions, obs = cells.shape
     shape = jax.ShapeDtypeStruct((regions, lon), jnp.float32)
     return pl.pallas_call(
         cells_kernel,
@@ -118,6 +141,7 @@
             bytes_accessed=4 * (3 * regions * obs + 2 * regions * lon),
             transcendentals=0,
         ),
+        compiler_params=SMALL,
         name="per_cell",
     )(cells, values, weights)
 
@@ -194,6 +218,7 @@
         cost_estimate=pl.CostEstimate(
             flops=48 * size * size * lon, bytes_accessed=8 * size * lon, transcendentals=0
         ),
+        compiler_params=SMALL,
         name="analysis",
     )(ens, dsum, vsum)
 
@@ -204,27 +229,21 @@
     bands = lax.axis_size("lat")
     regions = lat_dev * levels // groups
     count = members_dev * groups
-    band = lax.axis_index("lat")
-    even = lax.rem(band, 2) == 0
 
     first_round, second_round = pair_rounds(bands)
-    e_msg = lax.ppermute(
-        edge_message(state, zonal_wind, meridional_wind, even), "lat", first_round
-    )
-    o_msg = lax.ppermute(
-        edge_message(state, zonal_wind, meridional_wind, jnp.logical_not(even)),
-        "lat",
-        second_round,
-    )
-
-    def mine(x):
-        x = x.reshape(groups, regions, x.shape[-1])
-        return lax.dynamic_index_in_dim(x, lax.axis_index("member"), 0, keepdims=False)
-
-    dsum, vsum = per_cell(mine(obs_cell), mine(obs_value), mine(obs_weight), longitudes)
-
-    where = jnp.stack([even, band > 0, band < bands - 1]).astype(jnp.int32)
-    field = forecast(where, state, e_msg, o_msg, zonal_wind, meridional_wind)
+    e_msg, o_msg = edge_messages(state, zonal_wind, meridional_wind)
+    e_msg = lax.ppermute(e_msg, "lat", first_round)
+    o_msg = lax.ppermute(o_msg, "lat", second_round)
+
+    def grouped(x):
+        return x.reshape(groups, regions, x.shape[-1])
+
+    dsum, vsum = per_cell(
+        grouped(obs_cell), grouped(obs_value), grouped(obs_weight), longitudes
+    )
+    field = forecast(
+        bands, state, e_msg, o_msg, zonal_wind, meridional_wind, dsum, vsum
+    )
     blocks = field.transpose(1, 0, 2, 3).reshape(members_dev, groups, regions, longitudes)
     ensemble = lax.all_to_all(
         blocks.transpose(1, 0, 2, 3), "member", split_axis=0, concat_axis=0, tiled=True

time: 40.3 us -> 34.1 us (0.85)
  the two profiles are of different devices: /device:TPU:0 before, /device:TPU:16 now
where the time goes in v2:
time: 34.1 us; the launch traced here: 33.8 us
  blocking collectives  19.7 us (58%)
  waiting for transfers between devices  3.72 us (11%)
  starting transfers between devices  3.55 us (10%)
  Pallas kernels  3.4 us (10%)
  local copies, waits for them, and re-layouts  3.36 us (10%)
    all_to_all x1, blocking collectives, body(): lax.all_to_all(blocks.transpose(1, 0, 2, 3), 'member', split_axis=0, conc...  10.4 us
    all_to_all x1, blocking collectives, body(): lax.all_to_all(analysed.reshape(groups, members_dev, regions, longitudes)...  9.32 us
    ppermute x1, waiting for transfers between devices, body(): o_msg = lax.ppermute(o_msg, 'lat', second_round)  3.46 us
    unnamed x14, local copies, waits for them, and re-layouts  2.64 us
    pallas_call x1, Pallas kernels, analysis(): pl.pallas_call(functools.partial(analysis_kernel, regions), out_shape=jax...  2.2 us
    ppermute x1, starting transfers between devices, body(): o_msg = lax.ppermute(o_msg, 'lat', second_round)  1.91 us
    ppermute x1, starting transfers between devices, body(): e_msg = lax.ppermute(e_msg, 'lat', first_round)  1.64 us
    transpose x1, local copies, waits for them, and re-layouts, body(): return returned.transpose(1, 0, 2, 3).reshape(state.shape)  0.72 us
  transfers between devices with their start and end apart: 2, of which 2 were waited for; matrix products, arithmetic and copies ran while one was open for 0% of the time, Pallas kernels for 2%

profile of v2, /device:TPU:16, one launch (start us, length us, event | category | flops | bytes accessed | tf_op | source)
XLA Modules:
  0.0 33.8 jit_solution(14887932918367764800)
XLA Ops:
  0.0 0.0 copy-start
  0.0 0.9 %copy-done = f32[4,8,8,256]{3,2,1,0:T(8,128)S(1)} copy-done((f32[4,8,8,256]{3,2,1,0:T(8,128)S(1)}, f32[4,8,8,256]{3,2,1,0:T(8,128)}, u32[]{:S(2)}) %copy-start) | copy-done | bytes 262168
  1.0 0.0 copy-start.2
  1.0 0.8 %copy-done.2 = f32[8,8,256]{2,1,0:T(8,128)S(1)} copy-done((f32[8,8,256]{2,1,0:T(8,128)S(1)}, f32[8,8,256]{2,1,0:T(8,128)}, u32[]{:S(2)}) %copy-start.2) | copy-done | bytes 65560
  1.8 0.0 copy-start.3
  1.8 0.8 %copy-done.3 = f32[8,8,256]{2,1,0:T(8,128)S(1)} copy-done((f32[8,8,256]{2,1,0:T(8,128)S(1)}, f32[8,8,256]{2,1,0:T(8,128)}, u32[]{:S(2)}) %copy-start.3) | copy-done | bytes 65560
  2.6 0.0 copy-start.4
  2.6 0.0 copy-start.5
  2.6 0.0 copy-start.6
  2.6 0.0 copy-start.1
  2.7 1.6 %collective-permute-start = (f32[10,8,256]{2,1,0:T(8,128)S(1)}, f32[10,8,256]{2,1,0:T(8,128)S(1)}, u32[]{:S(2)}, u32[]{:S(2)}) collective-permute-start(f32[10,8,256]{2,1,0:T(8,128)S(1)} %get-tuple-element.9), channel_id=1, source_target_pairs={{0,1},{1,0},{2,3},{3,2},{4,5},{5,4},{6,7},{7,6},{8,9},{9,8},{10,11... | collective-permute-start | bytes 245768 | tf_op jit(solution)/shard_map/ppermute | solution.py:235
  4.3 1.9 %collective-permute-start.1 = (f32[10,8,256]{2,1,0:T(8,128)S(1)}, f32[10,8,256]{2,1,0:T(8,128)S(1)}, u32[]{:S(2)}, u32[]{:S(2)}) collective-permute-start(f32[10,8,256]{2,1,0:T(8,128)S(1)} %get-tuple-element.10), channel_id=1, source_target_pairs={{0,0},{1,2},{2,1},{3,3},{4,4},{5,6},{6,5},{7,7},{8,8},{9,10},{10,9... | collective-permute-start | bytes 245768 | tf_op jit(solution)/shard_map/ppermute | solution.py:236
  6.2 0.0 copy-done.4
  6.2 0.0 copy-done.5
  6.3 0.0 copy-done.6
  6.3 0.7 %per_cell.1 = (f32[8,256]{1,0:T(8,128)S(1)}, f32[8,256]{1,0:T(8,128)S(1)}) custom-call(s32[8,8,128]{2,1,0:T(8,128)S(1)} %copy-done.4, f32[8,8,128]{2,1,0:T(8,128)S(1)} %copy-done.5, f32[8,8,128]{2,1,0:T(8,128)S(1)} %copy-done.6), custom_call_target="tpu_custom_call" | custom-call | flops 1048576 | bytes 28672 | tf_op jit(solution)/shard_map/per_cell/pallas_call | solution.py:134
  6.9 0.3 collective-permute-done.e_ref
  7.2 3.5 %collective-permute-done.1.o_ref = f32[10,8,256]{2,1,0:T(8,128)S(1)} collective-permute-done((f32[10,8,256]{2,1,0:T(8,128)S(1)}, f32[10,8,256]{2,1,0:T(8,128)S(1)}, u32[]{:S(2)}, u32[]{:S(2)}) %collective-permute-start.1) | collective-permute-done | bytes 81952 | tf_op jit(solution)/shard_map/ppermute | solution.py:236
  10.6 0.0 copy-done.1
  10.6 0.5 %forecast.1 = f32[8,4,8,256]{3,2,1,0:T(8,128)S(1)} custom-call(f32[4,8,8,256]{3,2,1,0:T(8,128)S(1)} %copy-done.1, f32[10,8,256]{2,1,0:T(8,128)S(1)} %collective-permute-done.e_ref, f32[10,8,256]{2,1,0:T(8,128)S(1)} %collective-permute-done.1.o_ref, f32[8,8,256]{2,1,0:T(8,128)S(1)} %copy-done.2, f32[8,8,256]{2,1,0:T(8,128)S(1)} %copy-done.3, ...), custom_call_target="tpu_custom_call" | custom-call | flops 1572864 | bytes 524288 | tf_op jit(solution)/shard_map/forecast/pallas_call | solution.py:101
  11.2 10.4 %all_to_all.10 = f32[8,4,8,256]{3,2,1,0:T(8,128)S(1)} all-to-all(f32[8,4,8,256]{3,2,1,0:T(8,128)S(1)} %forecast.1), channel_id=1, replica_groups=mesh['member'=8,'lat'=4] {'member'}, dimensions={0} | all-to-all | bytes 524288 | tf_op jit(solution)/shard_map/all_to_all | solution.py:248
  21.6 2.2 %analysis.1 = f32[256,256]{1,0:T(8,128)S(1)} custom-call(f32[256,256]{1,0:T(8,128)S(1)} %bitcast.3, f32[8,256]{1,0:T(8,128)S(1)} %get-tuple-element.11.dsum_ref, f32[8,256]{1,0:T(8,128)S(1)} %get-tuple-element.12.vsum_ref), custom_call_target="tpu_custom_call" | custom-call | flops 805306368 | bytes 524288 | tf_op jit(solution)/shard_map/analysis/pallas_call | solution.py:213
  23.8 9.3 %all_to_all.11 = f32[8,4,8,256]{3,2,1,0:T(8,128)S(1)} all-to-all(f32[8,4,8,256]{3,2,1,0:T(8,128)S(1)} %bitcast.4), channel_id=1, replica_groups=mesh['member'=8,'lat'=4] {'member'}, dimensions={0} | all-to-all | bytes 524288 | tf_op jit(solution)/shard_map/all_to_all | solution.py:252
  33.1 0.7 %copy.8 = f32[4,8,8,256]{3,2,1,0:T(8,128)} copy(f32[4,8,8,256]{3,2,0,1:T(8,128)S(1)} %bitcast.5) | data formatting | bytes 524288 | tf_op jit(solution)/shard_map/transpose | solution.py:259
  (1 shorter events, 0.0 us)
Async XLA Ops:
  0.0 0.9 %copy-start = (f32[4,8,8,256]{3,2,1,0:T(8,128)S(1)}, f32[4,8,8,256]{3,2,1,0:T(8,128)}, u32[]{:S(2)}) copy-start(f32[4,8,8,256]{3,2,1,0:T(8,128)} %state_ref.3) | copy-start | bytes 786436
  1.0 0.8 %copy-start.2 = (f32[8,8,256]{2,1,0:T(8,128)S(1)}, f32[8,8,256]{2,1,0:T(8,128)}, u32[]{:S(2)}) copy-start(f32[8,8,256]{2,1,0:T(8,128)} %zonal_ref.3) | copy-start | bytes 196612
  1.8 0.8 %copy-start.3 = (f32[8,8,256]{2,1,0:T(8,128)S(1)}, f32[8,8,256]{2,1,0:T(8,128)}, u32[]{:S(2)}) copy-start(f32[8,8,256]{2,1,0:T(8,128)} %merid_ref.3) | copy-start | bytes 196612
  2.6 3.6 %copy-start.4 = (s32[8,8,128]{2,1,0:T(8,128)S(1)}, s32[8,8,128]{2,1,0:T(8,128)}, u32[]{:S(2)}) copy-start(s32[8,8,128]{2,1,0:T(8,128)} %cell_ref.1) | copy-start | bytes 98308
  2.6 3.6 %copy-start.5 = (f32[8,8,128]{2,1,0:T(8,128)S(1)}, f32[8,8,128]{2,1,0:T(8,128)}, u32[]{:S(2)}) copy-start(f32[8,8,128]{2,1,0:T(8,128)} %value_ref.1) | copy-start | bytes 98308
  2.6 3.6 %copy-start.6 = (f32[8,8,128]{2,1,0:T(8,128)S(1)}, f32[8,8,128]{2,1,0:T(8,128)}, u32[]{:S(2)}) copy-start(f32[8,8,128]{2,1,0:T(8,128)} %weight_ref.1) | copy-start | bytes 98308
  2.6 8.0 %copy-start.1 = (f32[4,8,8,256]{3,2,1,0:T(8,128)S(1)}, f32[4,8,8,256]{3,2,1,0:T(8,128)}, u32[]{:S(2)}) copy-start(f32[4,8,8,256]{3,2,1,0:T(8,128)} %state_ref.3) | copy-start | bytes 786436
  2.7 4.5 %collective-permute-start = (f32[10,8,256]{2,1,0:T(8,128)S(1)}, f32[10,8,256]{2,1,0:T(8,128)S(1)}, u32[]{:S(2)}, u32[]{:S(2)}) collective-permute-start(f32[10,8,256]{2,1,0:T(8,128)S(1)} %get-tuple-element.9), channel_id=1, source_target_pairs={{0,1},{1,0},{2,3},{3,2},{4,5},{5,4},{6,7},{7,6},{8,9},{9,8},{10,11... | collective-permute-start | bytes 245768 | tf_op jit(solution)/shard_map/ppermute | solution.py:235
  4.3 6.3 %collective-permute-start.1 = (f32[10,8,256]{2,1,0:T(8,128)S(1)}, f32[10,8,256]{2,1,0:T(8,128)S(1)}, u32[]{:S(2)}, u32[]{:S(2)}) collective-permute-start(f32[10,8,256]{2,1,0:T(8,128)S(1)} %get-tuple-element.10), channel_id=1, source_target_pairs={{0,0},{1,2},{2,1},{3,3},{4,4},{5,6},{6,5},{7,7},{8,8},{9,10},{10,9... | collective-permute-start | bytes 245768 | tf_op jit(solution)/shard_map/ppermute | solution.py:236

commit v3 on v2

--- a/solution.py
+++ b/solution.py
@@ -27,30 +27,43 @@
     return pairs(0), pairs(1)
 
 
-def edges_kernel(state_ref, zonal_ref, merid_ref, e_ref, o_ref):
+def edges_kernel(state_ref, zonal_ref, merid_ref, e_ref, o_ref, sems):
     members, rows, levels, lon = state_ref.shape
     odd = lax.rem(lax.axis_index("lat"), 2)
+    copies = []
     for out_ref, low in ((e_ref, odd), (o_ref, 1 - odd)):
         first = (1 - low) * (rows - 2)
         edge = (1 - low) * (rows - 1)
-        for m in range(members):
-            out_ref[2 * m] = state_ref[m, first]
-            out_ref[2 * m + 1] = state_ref[m, first + 1]
-        out_ref[2 * members] = zonal_ref[edge]
-        out_ref[2 * members + 1] = merid_ref[edge]
+        parts = [
+            (state_ref.at[m, pl.ds(first, 2)], out_ref.at[pl.ds(2 * m, 2)])
+            for m in range(members)
+        ]
+        parts.append((zonal_ref.at[edge], out_ref.at[2 * members]))
+        parts.append((merid_ref.at[edge], out_ref.at[2 * members + 1]))
+        for source, target in parts:
+            copies.append(pltpu.make_async_copy(source, target, sems.at[len(copies)]))
+    for copy in copies:
+        copy.start()
+    for copy in copies:
+        copy.wait()
 
 
 def edge_messages(state, zonal, meridional):
     members, rows, levels, lon = state.shape
     shape = jax.ShapeDtypeStruct((2 * members + 2, levels, lon), jnp.float32)
+    held = [
+        pltpu.with_memory_space_constraint(x, pltpu.HBM)
+        for x in (state, zonal, meridional)
+    ]
     return pl.pallas_call(
         edges_kernel,
         out_shape=(shape, shape),
-        in_specs=whole(3),
+        in_specs=[pl.BlockSpec(memory_space=pltpu.HBM)] * 3,
         out_specs=tuple(whole(2)),
+        scratch_shapes=[pltpu.SemaphoreType.DMA((2 * members + 4,))],
         compiler_params=SMALL,
         name="edges",
-    )(state, zonal, meridional)
+    )(*held)
 
 
 def advance(south, middle, north, zonal, meridional):

time: 34.1 us -> 32.5 us (0.953)
  local copies, waits for them, and re-layouts: 3.36 us -> 1.5 us
  Pallas kernels: 3.4 us -> 4.33 us
  waiting for transfers between devices: 3.72 us -> 2.97 us
    unnamed x14 -> x12, local copies, waits for them, and re-layouts: 2.64 us -> 0.77 us
    pallas_call x1, Pallas kernels: 0.03 us -> 0.97 us  [edge_messages(): pl.pallas_call(edges_kernel, out_shape=(shape, shape), in_specs=[pl.Block...]
    ppermute x1, waiting for transfers between devices: 3.46 us -> 2.97 us  [body(): o_msg = lax.ppermute(o_msg, 'lat', second_round)]
  transfers between devices with their start and end apart: 2 -> 2, of which waited for: 2 -> 1; matrix products, arithmetic and copies ran while one was open for 0% -> 0% of each run, Pallas kernels for 2% -> 2%
where the time goes in v3:
time: 32.5 us; the launch traced here: 32.2 us
  blocking collectives  19.7 us (61%)
  Pallas kernels  4.33 us (13%)
  starting transfers between devices  3.55 us (11%)
  waiting for transfers between devices  2.97 us (9%)
  local copies, waits for them, and re-layouts  1.5 us (5%)
    all_to_all x1, blocking collectives, body(): lax.all_to_all(blocks.transpose(1, 0, 2, 3), 'member', split_axis=0, conc...  10.4 us
    all_to_all x1, blocking collectives, body(): lax.all_to_all(analysed.reshape(groups, members_dev, regions, longitudes)...  9.32 us
    ppermute x1, waiting for transfers between devices, body(): o_msg = lax.ppermute(o_msg, 'lat', second_round)  2.97 us
    pallas_call x1, Pallas kernels, analysis(): pl.pallas_call(functools.partial(analysis_kernel, regions), out_shape=jax...  2.2 us
    ppermute x1, starting transfers between devices, body(): o_msg = lax.ppermute(o_msg, 'lat', second_round)  1.91 us
    ppermute x1, starting transfers between devices, body(): e_msg = lax.ppermute(e_msg, 'lat', first_round)  1.64 us
    pallas_call x1, Pallas kernels, edge_messages(): pl.pallas_call(edges_kernel, out_shape=(shape, shape), in_specs=[pl.Block...  0.97 us
    unnamed x12, local copies, waits for them, and re-layouts  0.77 us
  transfers between devices with their start and end apart: 2, of which 1 were waited for; matrix products, arithmetic and copies ran while one was open for 0% of the time, Pallas kernels for 2%

profile of v3, /device:TPU:16, one launch (start us, length us, event | category | flops | bytes accessed | tf_op | source)
XLA Modules:
  0.0 32.2 jit_solution(12843673990265502376)
XLA Ops:
  0.0 0.0 copy-start
  0.0 0.0 copy-start.4
  0.0 0.0 copy-start.3
  0.0 0.0 copy-start.2
  0.0 1.0 %edges.1 = (f32[10,8,256]{2,1,0:T(8,128)S(1)}, f32[10,8,256]{2,1,0:T(8,128)S(1)}) custom-call(f32[4,8,8,256]{3,2,1,0:T(8,128)} %state_ref.3, f32[8,8,256]{2,1,0:T(8,128)} %zonal_ref.3, f32[8,8,256]{2,1,0:T(8,128)} %merid_ref.3), custom_call_target="tpu_custom_call" | custom-call | tf_op jit(solution)/shard_map/edges/pallas_call | solution.py:58
  1.0 0.0 copy-start.1
  1.0 1.6 %collective-permute-start = (f32[10,8,256]{2,1,0:T(8,128)S(1)}, f32[10,8,256]{2,1,0:T(8,128)S(1)}, u32[]{:S(2)}, u32[]{:S(2)}) collective-permute-start(f32[10,8,256]{2,1,0:T(8,128)S(1)} %get-tuple-element.9), channel_id=1, source_target_pairs={{0,1},{1,0},{2,3},{3,2},{4,5},{5,4},{6,7},{7,6},{8,9},{9,8},{10,11... | collective-permute-start | bytes 245768 | tf_op jit(solution)/shard_map/ppermute | solution.py:248
  2.7 1.9 %collective-permute-start.1 = (f32[10,8,256]{2,1,0:T(8,128)S(1)}, f32[10,8,256]{2,1,0:T(8,128)S(1)}, u32[]{:S(2)}, u32[]{:S(2)}) collective-permute-start(f32[10,8,256]{2,1,0:T(8,128)S(1)} %get-tuple-element.10), channel_id=1, source_target_pairs={{0,0},{1,2},{2,1},{3,3},{4,4},{5,6},{6,5},{7,7},{8,8},{9,10},{10,9... | collective-permute-start | bytes 245768 | tf_op jit(solution)/shard_map/ppermute | solution.py:249
  4.6 0.0 copy-done.4
  4.6 0.0 copy-done.3
  4.6 0.0 copy-start.5
  4.6 0.7 %copy-done.5 = f32[8,8,128]{2,1,0:T(8,128)S(1)} copy-done((f32[8,8,128]{2,1,0:T(8,128)S(1)}, f32[8,8,128]{2,1,0:T(8,128)}, u32[]{:S(2)}) %copy-start.5) | copy-done | bytes 32792
  5.4 0.6 %per_cell.1 = (f32[8,256]{1,0:T(8,128)S(1)}, f32[8,256]{1,0:T(8,128)S(1)}) custom-call(s32[8,8,128]{2,1,0:T(8,128)S(1)} %copy-done.3, f32[8,8,128]{2,1,0:T(8,128)S(1)} %copy-done.4, f32[8,8,128]{2,1,0:T(8,128)S(1)} %copy-done.5), custom_call_target="tpu_custom_call" | custom-call | flops 1048576 | bytes 28672 | tf_op jit(solution)/shard_map/per_cell/pallas_call | solution.py:147
  6.0 0.0 collective-permute-done.e_ref
  6.0 3.0 %collective-permute-done.1.o_ref = f32[10,8,256]{2,1,0:T(8,128)S(1)} collective-permute-done((f32[10,8,256]{2,1,0:T(8,128)S(1)}, f32[10,8,256]{2,1,0:T(8,128)S(1)}, u32[]{:S(2)}, u32[]{:S(2)}) %collective-permute-start.1) | collective-permute-done | bytes 81952 | tf_op jit(solution)/shard_map/ppermute | solution.py:249
  9.0 0.0 copy-done
  9.0 0.0 copy-done.2
  9.0 0.0 copy-done.1
  9.0 0.5 %forecast.1 = f32[8,4,8,256]{3,2,1,0:T(8,128)S(1)} custom-call(f32[4,8,8,256]{3,2,1,0:T(8,128)S(1)} %copy-done, f32[10,8,256]{2,1,0:T(8,128)S(1)} %collective-permute-done.e_ref, f32[10,8,256]{2,1,0:T(8,128)S(1)} %collective-permute-done.1.o_ref, f32[8,8,256]{2,1,0:T(8,128)S(1)} %copy-done.1, f32[8,8,256]{2,1,0:T(8,128)S(1)} %copy-done.2, ...), custom_call_target="tpu_custom_call" | custom-call | flops 1572864 | bytes 524288 | tf_op jit(solution)/shard_map/forecast/pallas_call | solution.py:114
  9.5 10.4 %all_to_all.10 = f32[8,4,8,256]{3,2,1,0:T(8,128)S(1)} all-to-all(f32[8,4,8,256]{3,2,1,0:T(8,128)S(1)} %forecast.1), channel_id=1, replica_groups=mesh['member'=8,'lat'=4] {'member'}, dimensions={0} | all-to-all | bytes 524288 | tf_op jit(solution)/shard_map/all_to_all | solution.py:261
  19.9 2.2 %analysis.1 = f32[256,256]{1,0:T(8,128)S(1)} custom-call(f32[256,256]{1,0:T(8,128)S(1)} %bitcast.3, f32[8,256]{1,0:T(8,128)S(1)} %get-tuple-element.11.dsum_ref, f32[8,256]{1,0:T(8,128)S(1)} %get-tuple-element.12.vsum_ref), custom_call_target="tpu_custom_call" | custom-call | flops 805306368 | bytes 524288 | tf_op jit(solution)/shard_map/analysis/pallas_call | solution.py:226
  22.1 9.3 %all_to_all.11 = f32[8,4,8,256]{3,2,1,0:T(8,128)S(1)} all-to-all(f32[8,4,8,256]{3,2,1,0:T(8,128)S(1)} %bitcast.4), channel_id=1, replica_groups=mesh['member'=8,'lat'=4] {'member'}, dimensions={0} | all-to-all | bytes 524288 | tf_op jit(solution)/shard_map/all_to_all | solution.py:265
  31.5 0.7 %copy.8 = f32[4,8,8,256]{3,2,1,0:T(8,128)} copy(f32[4,8,8,256]{3,2,0,1:T(8,128)S(1)} %bitcast.5) | data formatting | bytes 524288 | tf_op jit(solution)/shard_map/transpose | solution.py:272
Async XLA Ops:
  0.0 9.0 %copy-start = (f32[4,8,8,256]{3,2,1,0:T(8,128)S(1)}, f32[4,8,8,256]{3,2,1,0:T(8,128)}, u32[]{:S(2)}) copy-start(f32[4,8,8,256]{3,2,1,0:T(8,128)} %state_ref.3) | copy-start | bytes 786436
  0.0 4.6 %copy-start.4 = (f32[8,8,128]{2,1,0:T(8,128)S(1)}, f32[8,8,128]{2,1,0:T(8,128)}, u32[]{:S(2)}) copy-start(f32[8,8,128]{2,1,0:T(8,128)} %value_ref.1) | copy-start | bytes 98308
  0.0 4.6 %copy-start.3 = (s32[8,8,128]{2,1,0:T(8,128)S(1)}, s32[8,8,128]{2,1,0:T(8,128)}, u32[]{:S(2)}) copy-start(s32[8,8,128]{2,1,0:T(8,128)} %cell_ref.1) | copy-start | bytes 98308
  0.0 9.0 %copy-start.2 = (f32[8,8,256]{2,1,0:T(8,128)S(1)}, f32[8,8,256]{2,1,0:T(8,128)}, u32[]{:S(2)}) copy-start(f32[8,8,256]{2,1,0:T(8,128)} %merid_ref.3) | copy-start | bytes 196612
  1.0 8.0 %copy-start.1 = (f32[8,8,256]{2,1,0:T(8,128)S(1)}, f32[8,8,256]{2,1,0:T(8,128)}, u32[]{:S(2)}) copy-start(f32[8,8,256]{2,1,0:T(8,128)} %zonal_ref.3) | copy-start | bytes 196612
  1.0 5.0 %collective-permute-start = (f32[10,8,256]{2,1,0:T(8,128)S(1)}, f32[10,8,256]{2,1,0:T(8,128)S(1)}, u32[]{:S(2)}, u32[]{:S(2)}) collective-permute-start(f32[10,8,256]{2,1,0:T(8,128)S(1)} %get-tuple-element.9), channel_id=1, source_target_pairs={{0,1},{1,0},{2,3},{3,2},{4,5},{5,4},{6,7},{7,6},{8,9},{9,8},{10,11... | collective-permute-start | bytes 245768 | tf_op jit(solution)/shard_map/ppermute | solution.py:248
  2.7 6.3 %collective-permute-start.1 = (f32[10,8,256]{2,1,0:T(8,128)S(1)}, f32[10,8,256]{2,1,0:T(8,128)S(1)}, u32[]{:S(2)}, u32[]{:S(2)}) collective-permute-start(f32[10,8,256]{2,1,0:T(8,128)S(1)} %get-tuple-element.10), channel_id=1, source_target_pairs={{0,0},{1,2},{2,1},{3,3},{4,4},{5,6},{6,5},{7,7},{8,8},{9,10},{10,9... | collective-permute-start | bytes 245768 | tf_op jit(solution)/shard_map/ppermute | solution.py:249
  4.6 0.8 %copy-start.5 = (f32[8,8,128]{2,1,0:T(8,128)S(1)}, f32[8,8,128]{2,1,0:T(8,128)}, u32[]{:S(2)}) copy-start(f32[8,8,128]{2,1,0:T(8,128)} %weight_ref.1) | copy-start | bytes 98308

commit v4 on v1

v4 whole, which is shorter than its diff:
```python
import functools

import jax
import jax.numpy as jnp
from jax import lax
from jax.experimental import pallas as pl
from jax.experimental.pallas import tpu as pltpu
from jax.sharding import PartitionSpec as P

SWEEPS = 3
step_size = 0.3
VM = pltpu.VMEM
SMALL = pltpu.CompilerParams(vmem_limit_bytes=12 * 2**20)


def whole(n):
    return [pl.BlockSpec(memory_space=VM)] * n


def place(bands):
    member, band = lax.axis_index("member"), lax.axis_index("lat")
    core, chip = lax.rem(member, 2), lax.div(member, 2)
    high = lax.rem(core + band, 2) == 0
    at_edge = jnp.where(high, band == bands - 1, band == 0)
    return chip, high, at_edge


def halo_pairs(groups, bands):
    pairs = []
    for member in range(groups):
        for band in range(bands):
            step = 1 if (member + band) % 2 == 0 else -1
            other = band + step if 0 <= band + step < bands else band
            pairs.append((member * bands + band, member * bands + other))
    return pairs


def swap(x, groups, distance):
    return lax.ppermute(x, "member", [(i, i ^ distance) for i in range(groups)])


def stage_kernel(bands, *refs):
    sources, targets, sems = refs[:6], refs[6:12], refs[12]
    chip, high, at_edge = place(bands)
    mine = jnp.where(high, sources[3].shape[0] // 2, 0) + chip
    sources = list(sources[:3]) + [ref.at[mine] for ref in sources[3:]]
    copies = [
        pltpu.make_async_copy(source, target, sems.at[i])
        for i, (source, target) in enumerate(zip(sources, targets))
    ]
    for copy in copies:
        copy.start()
    for copy in copies:
        copy.wait()


def stage(bands, fields, tables):
    shapes = [x.shape for x in fields] + [x.shape[1:] for x in tables]
    args = [pltpu.with_memory_space_constraint(x, pltpu.HBM) for x in (*fields, *tables)]
    return pl.pallas_call(
        functools.partial(stage_kernel, bands),
        out_shape=tuple(jax.ShapeDtypeStruct(n, x.dtype) for n, x in zip(shapes, args)),
        in_specs=[pl.BlockSpec(memory_space=pltpu.HBM)] * 6,
        out_specs=tuple(whole(6)),
        scratch_shapes=[pltpu.SemaphoreType.DMA((6,))],
        cost_estimate=pl.CostEstimate(flops=0, bytes_accessed=2**21, transcendentals=0),
        compiler_params=SMALL,
        name="stage",
    )(*args)


def edges_kernel(bands, own_ref, partner_ref, zonal_ref, merid_ref, out_ref):
    members, rows, levels, lon = own_ref.shape
    chip, high, at_edge = place(bands)
    first = jnp.where(high, rows - 2, 0)
    edge = jnp.where(high, rows - 1, 0)
    for m in range(2 * members):
        ref = own_ref if m < members else partner_ref
        out_ref[2 * m] = ref[m % members, first]
        out_ref[2 * m + 1] = ref[m % members, first + 1]
    out_ref[4 * members] = zonal_ref[edge]
    out_ref[4 * members + 1] = merid_ref[edge]


def edge_message(bands, own, partner, zonal, merid):
    members, rows, levels, lon = own.shape
    return pl.pallas_call(
        functools.partial(edges_kernel, bands),
        out_shape=jax.ShapeDtypeStruct((4 * members + 2, levels, lon), jnp.float32),
        in_specs=whole(4),
        out_specs=pl.BlockSpec(memory_space=VM),
        compiler_params=SMALL,
        name="edges",
    )(own, partner, zonal, merid)


def advance(south, middle, north, zonal, meridional):
    lon = middle.shape[-1]
    axis = middle.ndim - 1
    east = pltpu.roll(middle, lon - 1, axis)
    west = pltpu.roll(middle, 1, axis)
    return middle - step_size * (
        (zonal + middle) * (east - west) * 0.5 + meridional * (north - south) * 0.5
    )


def forecast_kernel(
    bands,
    crossed,
    own_ref,
    partner_ref,
    halo_ref,
    zonal_ref,
    merid_ref,
    dsum_ref,
    vsum_ref,
    *refs,
):
    out_refs, first_ref = refs[:-1], refs[-1]
    members, rows, levels, lon = own_ref.shape
    half = rows // 2
    chip, high, at_edge = place(bands)
    base = jnp.where(high, half, 0)

    def halo(i):
        return jnp.where(at_edge, 0.0, halo_ref[i])

    def winds(ref, outside):
        inside = [ref[base + r] for r in range(half)]
        before = jnp.where(high, ref[half - 1], outside)
        after = jnp.where(high, outside, ref[half])
        return [before, *inside, after]

    zonal = winds(zonal_ref, halo(4 * members))
    merid = winds(merid_ref, halo(4 * members + 1))
    for m in range(2 * members):
        ref, k = (own_ref if m < members else partner_ref), m % members
        outside = [halo(2 * m), halo(2 * m + 1)]
        q = [jnp.where(high, ref[k, half - 2 + i], outside[i]) for i in range(2)]
        q += [ref[k, base + r] for r in range(half)]
        q += [jnp.where(high, outside[i], ref[k, half + i]) for i in range(2)]
        for r in range(half + 2):
            first_ref[r, m] = advance(q[r], q[r + 1], q[r + 2], zonal[r], merid[r])
    for t in range(half):
        r = row_of(chip, t, crossed)
        zonal_row, merid_row = zonal_ref[base + r], merid_ref[base + r]
        for m in range(2 * members):
            out_refs[t][m] = advance(
                first_ref[r, m], first_ref[r + 1, m], first_ref[r + 2, m], zonal_row, merid_row
            )


def row_of(chip, t, crossed):
    return lax.bitwise_xor(chip, t) if crossed else t


def forecast(bands, crossed, own, partner, halo, zonal, merid, dsum, vsum):
    members, rows, levels, lon = own.shape
    half = rows // 2
    size = own.size
    shape = jax.ShapeDtypeStruct((2 * members, levels, lon), jnp.float32)
    return pl.pallas_call(
        functools.partial(forecast_kernel, bands, crossed),
        out_shape=(shape,) * half,
        in_specs=whole(5) + [pl.BlockSpec(memory_space=pl.ANY)] * 2,
        out_specs=tuple(whole(half)),
        scratch_shapes=[VM((half + 2, 2 * members, levels, lon), jnp.float32)],
        cost_estimate=pl.CostEstimate(
            flops=24 * size, bytes_accessed=8 * size, transcendentals=0
        ),
        compiler_params=SMALL,
        name="forecast",
    )(own, partner, halo, zonal, merid, dsum, vsum)


def cells_kernel(cell_ref, value_ref, weight_ref, dsum_ref, vsum_ref):
    regions, obs = cell_ref.shape
    lon = dsum_ref.shape[1]
    weight = weight_ref[...]
    cell_t = cell_ref[...].T
    weight_t = weight.T
    value_t = (weight * value_ref[...]).T
    index = lax.broadcasted_iota(jnp.int32, (obs, lon), 1)
    for r in range(regions):
        hit = jnp.broadcast_to(cell_t[:, r : r + 1], (obs, lon)) == index
        w = jnp.broadcast_to(weight_t[:, r : r + 1], (obs, lon))
        v = jnp.broadcast_to(value_t[:, r : r + 1], (obs, lon))
        dsum_ref[r : r + 1, :] = jnp.sum(jnp.where(hit, w, 0.0), axis=0, keepdims=True)
        vsum_ref[r : r + 1, :] = jnp.sum(jnp.where(hit, v, 0.0), axis=0, keepdims=True)


def per_cell(cells, values, weights, lon):
    regions, obs = cells.shape
    shape = jax.ShapeDtypeStruct((regions, lon), jnp.float32)
    return pl.pallas_call(
        cells_kernel,
        out_shape=(shape, shape),
        in_specs=whole(3),
        out_specs=tuple(whole(2)),
        cost_estimate=pl.CostEstimate(
            flops=4 * regions * obs * lon,
            bytes_accessed=4 * (3 * regions * obs + 2 * regions * lon),
            transcendentals=0,
        ),
        compiler_params=SMALL,
        name="per_cell",
    )(cells, values, weights)


def split(x):
    high = x.astype(jnp.bfloat16)
    low = (x - high.astype(jnp.float32)).astype(jnp.bfloat16)
    return high, low


def product(a, b, dims=((1,), (0,))):
    def dot(x, y):
        return lax.dot_general(x, y, (dims, ((), ())), preferred_element_type=jnp.float32)

    return dot(a[0], b[0]) + (dot(a[0], b[1]) + dot(a[1], b[0]))


def analysis_kernel(regions, parts, *refs):
    ens_refs, (dsum_ref, vsum_ref) = refs[:parts], refs[parts : parts + 2]
    out_refs = refs[parts + 2 :]
    share, lon = ens_refs[0].shape
    size = share * parts
    count = size // regions

    def over_members(x):
        if regions == 1:
            return jnp.sum(x, axis=0, keepdims=True)
        return jnp.sum(x.reshape(count, regions, x.shape[-1]), axis=0)

    def spread(x):
        if regions == 1:
            return jnp.broadcast_to(x, (size, x.shape[-1]))
        x = jnp.broadcast_to(x[None], (count, regions, x.shape[-1]))
        return x.reshape(size, x.shape[-1])

    ens = jnp.concatenate([ref[...] for ref in ens_refs], axis=0)
    dsum = dsum_ref[...]
    mean = over_members(ens) * (1.0 / count)
    pert = ens - spread(mean)
    pull = vsum_ref[...] - dsum * mean

    row = lax.broadcasted_iota(jnp.int32, (size, size), 0)
    col = lax.broadcasted_iota(jnp.int32, (size, size), 1)
    same = lax.rem(row, regions) == lax.rem(col, regions)
    one = jnp.where(row == col, 1.0, 0.0)

    pert_s = split(pert)
    gram = product(split(pert * spread(dsum)), pert_s, ((1,), (1,)))
    system = jnp.where(same, gram, 0.0) + (count - 1.0) * one
    total = over_members(jnp.sum(system * system, axis=1, keepdims=True))
    frob = jnp.sqrt(total)
    iterate = system * spread(1.0 / frob)
    iterate_s = split(iterate)
    inverse_s = None
    for sweep in range(SWEEPS):
        step = iterate if inverse_s is None else product(inverse_s, iterate_s)
        factor_s = split(1.5 * one - 0.5 * step)
        if sweep == SWEEPS - 1:
            break
        iterate_s = split(product(iterate_s, factor_s))
        inverse_s = factor_s if inverse_s is None else split(product(factor_s, inverse_s))
    part_s = split(product(inverse_s, pert_s))
    update = product(factor_s, part_s) * spread(lax.rsqrt(frob))
    gain = jnp.sum(update * spread(pull), axis=1, keepdims=True)
    shift = mean + over_members(update * gain)
    result = spread(shift) + jnp.sqrt(count - 1.0) * update
    for i, ref in enumerate(out_refs):
        ref[...] = result[i * share : (i + 1) * share]


def analysis(ens, dsum, vsum):
    parts = len(ens)
    share, lon = ens[0].shape
    size = share * parts
    regions = dsum.shape[0]
    return pl.pallas_call(
        functools.partial(analysis_kernel, regions, parts),
        out_shape=(jax.ShapeDtypeStruct((share, lon), jnp.float32),) * parts,
        in_specs=whole(parts + 2),
        out_specs=tuple(whole(parts)),
        cost_estimate=pl.CostEstimate(
            flops=48 * size * size * lon, bytes_accessed=8 * size * lon, transcendentals=0
        ),
        compiler_params=SMALL,
        name="analysis",
    )(*ens, dsum, vsum)


def place_rows_kernel(bands, crossed, got_ref, *refs):
    half_refs, out_ref, sems = refs[:-2], refs[-2], refs[-1]
    half = len(half_refs)
    members = out_ref.shape[0]
    chip, high, at_edge = place(bands)
    base = jnp.where(high, half, 0)
    copies = []
    for t, ref in enumerate(half_refs):
        r = row_of(chip, t, crossed)
        for source, row in ((ref.at[pl.ds(0, members)], base + r), (got_ref.at[t], half - base + r)):
            copies.append(
                pltpu.make_async_copy(source, out_ref.at[:, row], sems.at[len(copies)])
            )
    for copy in copies:
        copy.start()
    for copy in copies:
        copy.wait()


def place_rows(bands, crossed, got, halves, shape):
    half = len(halves)
    return pl.pallas_call(
        functools.partial(place_rows_kernel, bands, crossed),
        out_shape=jax.ShapeDtypeStruct(shape, jnp.float32),
        in_specs=whole(1 + half),
        out_specs=pl.BlockSpec(memory_space=pltpu.HBM),
        scratch_shapes=[pltpu.SemaphoreType.DMA((2 * half,))],
        compiler_params=SMALL,
        name="place_rows",
    )(got, *halves)


def body(state, zonal_wind, meridional_wind, obs_cell, obs_value, obs_weight):
    members, rows, levels, lon = state.shape
    groups = lax.axis_size("member")
    bands = lax.axis_size("lat")
    half = rows // 2
    chips = groups // 2
    regions = half * levels // chips
    crossed = chips == half and chips <= 4 and chips & (chips - 1) == 0

    def grouped(x):
        return x.reshape(groups, regions, x.shape[-1])

    partner = swap(state, groups, 1)
    own, zonal, merid, *tables = stage(
        bands,
        (state, zonal_wind, meridional_wind),
        (grouped(obs_cell), grouped(obs_value), grouped(obs_weight)),
    )
    message = edge_message(bands, own, partner, zonal, merid)
    halo = lax.ppermute(message, ("member", "lat"), halo_pairs(groups, bands))

    dsum, vsum = per_cell(*tables, lon)
    sent = forecast(bands, crossed, own, partner, halo, zonal, merid, dsum, vsum)
    same_core = [list(range(core, groups, 2)) for core in range(2)]

    def exchange(blocks):
        if crossed:
            return [blocks[0]] + [swap(b, groups, 2 * t) for t, b in enumerate(blocks) if t]
        return [
            lax.all_to_all(
                blocks[0], "member", 0, 0, tiled=True, axis_index_groups=same_core
            )
        ]

    if not crossed:
        field = jnp.stack(sent, axis=1).reshape(2 * members, chips, regions, lon)
        sent = [field.transpose(1, 0, 2, 3)]
    ensemble = exchange(sent)
    flat = [x.reshape(-1, lon) for x in ensemble]
    analysed = analysis(flat, dsum, vsum)
    back = exchange([x.reshape(e.shape) for x, e in zip(analysed, ensemble)])
    if not crossed:
        field = back[0].transpose(1, 0, 2, 3).reshape(2 * members, half, levels, lon)
        back = [field[:, t] for t in range(half)]
    got = swap(jnp.stack([b[members:] for b in back]), groups, 1)
    return place_rows(bands, crossed, got, back, state.shape)


def solution(mesh):
    in_specs = (
        P("member", "lat", None, None),
        P("lat", None, None),
        P("lat", None, None),
        P("lat", None, None),
        P("lat", None, None),
        P("lat", None, None),
    )
    out_specs = P("member", "lat", None, None)
    return jax.shard_map(body, mesh=mesh, in_specs=in_specs, out_specs=out_specs, check_vma=False)
```

time: 40.3 us -> 30.8 us (0.76)
  blocking collectives: 10.2 us -> 0 us
  waiting for transfers between devices: 4.92 us -> 12.9 us
  local copies, waits for them, and re-layouts: 5.6 us -> 0.01 us
  Pallas kernels: 8.05 us -> 5.1 us
  starting transfers between devices: 10.3 us -> 12.5 us
  other arithmetic: 0.62 us -> 0.01 us
    ppermute x2 -> x9, waiting for transfers between devices: 1.82 us -> 12.9 us  [the longest x8 10.4 us: swap(): return lax.ppermute(x, 'member', [(i, i ^ distance) for i in range(groups)])]
    all_to_all x1 -> x0, blocking collectives: 10.2 us -> none  [body(): lax.all_to_all(analysed.reshape(groups, members_dev, regions, longitudes)...]
    ppermute x2 -> x9, starting transfers between devices: 6.6 us -> 12.5 us  [the longest x8 7.67 us: swap(): return lax.ppermute(x, 'member', [(i, i ^ distance) for i in range(groups)])]
    all_to_all x1 -> x0, starting transfers between devices: 3.72 us -> none  [body(): lax.all_to_all(blocks.transpose(1, 0, 2, 3), 'member', split_axis=0, conc...]
    all_to_all x1 -> x0, waiting for transfers between devices: 3.1 us -> none  [body(): lax.all_to_all(blocks.transpose(1, 0, 2, 3), 'member', split_axis=0, conc...]
    squeeze x2 -> x0, local copies, waits for them, and re-layouts: 1.89 us -> none  [mine(): lax.dynamic_index_in_dim(x, lax.axis_index('member'), 0, keepdims=False)]
    pallas_call x2 -> x5, Pallas kernels: 6.15 us -> 4.47 us  [the longest x1 2.2 us: analysis(): pl.pallas_call(functools.partial(analysis_kernel, regions, parts), out_sh...]
    dynamic_slice x2 -> x0, local copies, waits for them, and re-layouts: 1.65 us -> none  [the longest x1 0.89 us: edge_message(): fields = lax.dynamic_slice_in_dim(state, start, 2, 1)]
  transfers between devices with their start and end apart: 3 -> 9, of which waited for: 2 -> 9; matrix products, arithmetic and copies ran while one was open for 6% -> 0% of each run, Pallas kernels for 5% -> 5%
where the time goes in v4:
time: 30.8 us; the launch traced here: 30.6 us
  waiting for transfers between devices  12.9 us (42%)
  starting transfers between devices  12.5 us (41%)
  Pallas kernels  5.1 us (17%)
    ppermute x8, waiting for transfers between devices, swap(): return lax.ppermute(x, 'member', [(i, i ^ distance) for i in range(groups)])  10.4 us
    ppermute x8, starting transfers between devices, swap(): return lax.ppermute(x, 'member', [(i, i ^ distance) for i in range(groups)])  7.67 us
    ppermute x1, starting transfers between devices, body(): halo = lax.ppermute(message, ('member', 'lat'), halo_pairs(groups, bands))  4.84 us
    ppermute x1, waiting for transfers between devices, body(): halo = lax.ppermute(message, ('member', 'lat'), halo_pairs(groups, bands))  2.48 us
    pallas_call x1, Pallas kernels, analysis(): pl.pallas_call(functools.partial(analysis_kernel, regions, parts), out_sh...  2.2 us
    pallas_call x1, Pallas kernels, stage(): pl.pallas_call(functools.partial(stage_kernel, bands), out_shape=tuple((j...  1.01 us
    pallas_call x1, Pallas kernels, place_rows(): pl.pallas_call(functools.partial(place_rows_kernel, bands, crossed), out_...  0.76 us
    pallas_call x1, Pallas kernels, per_cell(): pl.pallas_call(cells_kernel, out_shape=(shape, shape), in_specs=whole(3),...  0.63 us
  transfers between devices with their start and end apart: 9, of which 9 were waited for; matrix products, arithmetic and copies ran while one was open for 0% of the time, Pallas kernels for 5%

profile of v4, /device:TPU:0, one launch (start us, length us, event | category | flops | bytes accessed | tf_op | source)
XLA Modules:
  0.0 30.6 jit_solution(3556262757200698684)
XLA Ops:
  0.0 0.5 %collective-permute-start = (f32[4,8,8,256]{3,2,1,0:T(8,128)}, f32[4,8,8,256]{3,2,1,0:T(8,128)S(1)}, u32[]{:S(2)}, u32[]{:S(2)}) collective-permute-start(f32[4,8,8,256]{3,2,1,0:T(8,128)} %refs_0_.1), channel_id=1, source_target_pairs={{0,4},{4,0},{8,12},{12,8},{16,20},{20,16},{24,28},{28,24},{1,5},{5... | collective-permute-start | bytes 786440 | tf_op jit(solution)/shard_map/ppermute | solution.py:39
  0.5 1.0 %stage.1 = (f32[4,8,8,256]{3,2,1,0:T(8,128)S(1)}, f32[8,8,256]{2,1,0:T(8,128)S(1)}, f32[8,8,256]{2,1,0:T(8,128)S(1)}, s32[8,128]{1,0:T(8,128)S(1)}, f32[8,128]{1,0:T(8,128)S(1)}, /*index=5*/f32[8,128]{1,0:T(8,128)S(1)}) custom-call(f32[4,8,8,256]{3,2,1,0:T(8,128)} %refs_0_.1, f32[8,8,256]{2,1,0:T(8,128)} %refs_1_.1, f32[8,8,256]{2,1,0:T(8,128)} %refs_2_.1, ...), custom_call_target="tpu_custom_call" | custom-call | bytes 2097152 | tf_op jit(solution)/shard_map/stage/pallas_call | solution.py:60
  1.5 0.4 %collective-permute-done.partner_ref = f32[4,8,8,256]{3,2,1,0:T(8,128)S(1)} collective-permute-done((f32[4,8,8,256]{3,2,1,0:T(8,128)}, f32[4,8,8,256]{3,2,1,0:T(8,128)S(1)}, u32[]{:S(2)}, u32[]{:S(2)}) %collective-permute-start) | collective-permute-done | bytes 262176 | tf_op jit(solution)/shard_map/ppermute | solution.py:39
  1.9 4.8 %collective-permute-start.1 = (f32[18,8,256]{2,1,0:T(8,128)S(1)}, f32[18,8,256]{2,1,0:T(8,128)S(1)}, u32[]{:S(2)}, u32[]{:S(2)}) collective-permute-start(f32[18,8,256]{2,1,0:T(8,128)S(1)} %edges.1), channel_id=1, source_target_pairs={{0,1},{1,0},{2,3},{3,2},{4,4},{5,6},{6,5},{7,7},{8,9},{9,8},{10,11... | collective-permute-start | bytes 442376 | tf_op jit(solution)/shard_map/ppermute | solution.py:345
  6.7 0.6 %per_cell.1 = (f32[8,256]{1,0:T(8,128)S(1)}, f32[8,256]{1,0:T(8,128)S(1)}) custom-call(s32[8,128]{1,0:T(8,128)S(1)} %get-tuple-element.24.cell_ref, f32[8,128]{1,0:T(8,128)S(1)} %get-tuple-element.25.value_ref, f32[8,128]{1,0:T(8,128)S(1)} %get-tuple-element.26.weight_ref), custom_call_target="tpu_custom_call" | custom-call | flops 1048576 | bytes 28672 | tf_op jit(solution)/shard_map/per_cell/pallas_call | solution.py:195
  7.4 2.5 %collective-permute-done.1.halo_ref = f32[18,8,256]{2,1,0:T(8,128)S(1)} collective-permute-done((f32[18,8,256]{2,1,0:T(8,128)S(1)}, f32[18,8,256]{2,1,0:T(8,128)S(1)}, u32[]{:S(2)}, u32[]{:S(2)}) %collective-permute-start.1) | collective-permute-done | bytes 147488 | tf_op jit(solution)/shard_map/ppermute | solution.py:345
  9.8 0.5 %forecast.1 = (f32[8,8,256]{2,1,0:T(8,128)S(1)}, f32[8,8,256]{2,1,0:T(8,128)S(1)}, f32[8,8,256]{2,1,0:T(8,128)S(1)}, f32[8,8,256]{2,1,0:T(8,128)S(1)}) custom-call(f32[4,8,8,256]{3,2,1,0:T(8,128)S(1)} %get-tuple-element.21.own_ref, f32[4,8,8,256]{3,2,1,0:T(8,128)S(1)} %collective-permute-done.partner_ref, f32[18,8,256]{2,1,0:T(8,128)S(1)} %collective-permute-done.1.halo_ref, ...), custom_call_target="tpu_custom_call" | custom-call | flops 1572864 | bytes 524288 | tf_op jit(solution)/shard_map/forecast/pallas_call | solution.py:162
  10.3 2.0 %collective-permute-start.2 = (f32[8,8,256]{2,1,0:T(8,128)S(1)}, f32[8,8,256]{2,1,0:T(8,128)S(1)}, u32[]{:S(2)}, u32[]{:S(2)}) collective-permute-start(f32[8,8,256]{2,1,0:T(8,128)S(1)} %get-tuple-element.30), channel_id=1, source_target_pairs={{0,8},{4,12},{8,0},{12,4},{16,24},{20,28},{24,16},{28,20},{1,9},{5... | collective-permute-start | bytes 196616 | tf_op jit(solution)/shard_map/ppermute | solution.py:39
  12.3 1.5 %collective-permute-start.3 = (f32[8,8,256]{2,1,0:T(8,128)S(1)}, f32[8,8,256]{2,1,0:T(8,128)S(1)}, u32[]{:S(2)}, u32[]{:S(2)}) collective-permute-start(f32[8,8,256]{2,1,0:T(8,128)S(1)} %get-tuple-element.31), channel_id=1, source_target_pairs={{0,16},{4,20},{8,24},{12,28},{16,0},{20,4},{24,8},{28,12},{1,17},{... | collective-permute-start | bytes 196616 | tf_op jit(solution)/shard_map/ppermute | solution.py:39
  13.8 0.0 collective-permute-start.4
  13.9 0.8 %collective-permute-done.2 = f32[8,8,256]{2,1,0:T(8,128)S(1)} collective-permute-done((f32[8,8,256]{2,1,0:T(8,128)S(1)}, f32[8,8,256]{2,1,0:T(8,128)S(1)}, u32[]{:S(2)}, u32[]{:S(2)}) %collective-permute-start.2) | collective-permute-done | bytes 65568 | tf_op jit(solution)/shard_map/ppermute | solution.py:39
  14.7 1.9 %collective-permute-done.3 = f32[8,8,256]{2,1,0:T(8,128)S(1)} collective-permute-done((f32[8,8,256]{2,1,0:T(8,128)S(1)}, f32[8,8,256]{2,1,0:T(8,128)S(1)}, u32[]{:S(2)}, u32[]{:S(2)}) %collective-permute-start.3) | collective-permute-done | bytes 65568 | tf_op jit(solution)/shard_map/ppermute | solution.py:39
  16.6 3.1 %collective-permute-done.4 = f32[8,8,256]{2,1,0:T(8,128)S(1)} collective-permute-done((f32[8,8,256]{2,1,0:T(8,128)S(1)}, f32[8,8,256]{2,1,0:T(8,128)S(1)}, u32[]{:S(2)}, u32[]{:S(2)}) %collective-permute-start.4) | collective-permute-done | bytes 65568 | tf_op jit(solution)/shard_map/ppermute | solution.py:39
  19.7 2.2 %analysis.1 = (f32[64,256]{1,0:T(8,128)S(1)}, f32[64,256]{1,0:T(8,128)S(1)}, f32[64,256]{1,0:T(8,128)S(1)}, f32[64,256]{1,0:T(8,128)S(1)}) custom-call(f32[64,256]{1,0:T(8,128)S(1)} %bitcast.17, f32[64,256]{1,0:T(8,128)S(1)} %bitcast.19, f32[64,256]{1,0:T(8,128)S(1)} %bitcast.21, f32[64,256]{1,0:T(8,128)S(1)} %bitcast.22, ...), custom_call_target="tpu_custom_call" | custom-call | flops 805306368 | bytes 524288 | tf_op jit(solution)/shard_map/analysis/pallas_call | solution.py:281
  21.9 0.2 collective-permute-start.6
  22.2 0.2 collective-permute-start.5
  22.4 3.1 %collective-permute-start.7 = (f32[8,8,256]{2,1,0:T(8,128)S(1)}, f32[8,8,256]{2,1,0:T(8,128)S(1)}, u32[]{:S(2)}, u32[]{:S(2)}) collective-permute-start(f32[8,8,256]{2,1,0:T(8,128)S(1)} %bitcast.18), channel_id=1, source_target_pairs={{0,24},{4,28},{8,16},{12,20},{16,8},{20,12},{24,0},{28,4},{1,25},{... | collective-permute-start | bytes 196616 | tf_op jit(solution)/shard_map/ppermute | solution.py:39
  25.5 0.8 %collective-permute-done.6.refs_2_ = f32[8,8,256]{2,1,0:T(8,128)S(1)} collective-permute-done((f32[8,8,256]{2,1,0:T(8,128)S(1)}, f32[8,8,256]{2,1,0:T(8,128)S(1)}, u32[]{:S(2)}, u32[]{:S(2)}) %collective-permute-start.6) | collective-permute-done | bytes 65568 | tf_op jit(solution)/shard_map/ppermute | solution.py:39
  26.3 0.2 collective-permute-done.5.refs_1_
  26.4 2.0 %collective-permute-done.7.refs_3_ = f32[8,8,256]{2,1,0:T(8,128)S(1)} collective-permute-done((f32[8,8,256]{2,1,0:T(8,128)S(1)}, f32[8,8,256]{2,1,0:T(8,128)S(1)}, u32[]{:S(2)}, u32[]{:S(2)}) %collective-permute-start.7) | collective-permute-done | bytes 65568 | tf_op jit(solution)/shard_map/ppermute | solution.py:39
  28.4 0.1 collective-permute-start.8
  28.5 1.3 %collective-permute-done.8.got_ref = f32[4,4,8,256]{3,2,1,0:T(8,128)S(1)} collective-permute-done((f32[4,4,8,256]{3,2,1,0:T(8,128)S(1)}, f32[4,4,8,256]{3,2,1,0:T(8,128)S(1)}, u32[]{:S(2)}, u32[]{:S(2)}) %collective-permute-start.8) | collective-permute-done | bytes 131104 | tf_op jit(solution)/shard_map/ppermute | solution.py:39
  29.8 0.8 %place_rows.1 = f32[4,8,8,256]{3,2,1,0:T(8,128)} custom-call(f32[4,4,8,256]{3,2,1,0:T(8,128)S(1)} %collective-permute-done.8.got_ref, f32[8,8,256]{2,1,0:T(8,128)S(1)} %bitcast.16, f32[8,8,256]{2,1,0:T(8,128)S(1)} %collective-permute-done.5.refs_1_, f32[8,8,256]{2,1,0:T(8,128)S(1)} %collective-permute-done.6.refs_2_, ...), custom_call_target="tpu_custom_call" | custom-call | tf_op jit(solution)/shard_map/place_rows/pallas_call | solution.py:315
  (6 shorter events, 0.0 us)
Async XLA Ops:
  0.0 1.9 %collective-permute-start = (f32[4,8,8,256]{3,2,1,0:T(8,128)}, f32[4,8,8,256]{3,2,1,0:T(8,128)S(1)}, u32[]{:S(2)}, u32[]{:S(2)}) collective-permute-start(f32[4,8,8,256]{3,2,1,0:T(8,128)} %refs_0_.1), channel_id=1, source_target_pairs={{0,4},{4,0},{8,12},{12,8},{16,20},{20,16},{24,28},{28,24},{1,5},{5... | collective-permute-start | bytes 786440 | tf_op jit(solution)/shard_map/ppermute | solution.py:39
  1.9 8.0 %collective-permute-start.1 = (f32[18,8,256]{2,1,0:T(8,128)S(1)}, f32[18,8,256]{2,1,0:T(8,128)S(1)}, u32[]{:S(2)}, u32[]{:S(2)}) collective-permute-start(f32[18,8,256]{2,1,0:T(8,128)S(1)} %edges.1), channel_id=1, source_target_pairs={{0,1},{1,0},{2,3},{3,2},{4,4},{5,6},{6,5},{7,7},{8,9},{9,8},{10,11... | collective-permute-start | bytes 442376 | tf_op jit(solution)/shard_map/ppermute | solution.py:345
  10.3 4.3 %collective-permute-start.2 = (f32[8,8,256]{2,1,0:T(8,128)S(1)}, f32[8,8,256]{2,1,0:T(8,128)S(1)}, u32[]{:S(2)}, u32[]{:S(2)}) collective-permute-start(f32[8,8,256]{2,1,0:T(8,128)S(1)} %get-tuple-element.30), channel_id=1, source_target_pairs={{0,8},{4,12},{8,0},{12,4},{16,24},{20,28},{24,16},{28,20},{1,9},{5... | collective-permute-start | bytes 196616 | tf_op jit(solution)/shard_map/ppermute | solution.py:39
  12.3 4.3 %collective-permute-start.3 = (f32[8,8,256]{2,1,0:T(8,128)S(1)}, f32[8,8,256]{2,1,0:T(8,128)S(1)}, u32[]{:S(2)}, u32[]{:S(2)}) collective-permute-start(f32[8,8,256]{2,1,0:T(8,128)S(1)} %get-tuple-element.31), channel_id=1, source_target_pairs={{0,16},{4,20},{8,24},{12,28},{16,0},{20,4},{24,8},{28,12},{1,17},{... | collective-permute-start | bytes 196616 | tf_op jit(solution)/shard_map/ppermute | solution.py:39
  13.8 5.9 %collective-permute-start.4 = (f32[8,8,256]{2,1,0:T(8,128)S(1)}, f32[8,8,256]{2,1,0:T(8,128)S(1)}, u32[]{:S(2)}, u32[]{:S(2)}) collective-permute-start(f32[8,8,256]{2,1,0:T(8,128)S(1)} %get-tuple-element.32), channel_id=1, source_target_pairs={{0,24},{4,28},{8,16},{12,20},{16,8},{20,12},{24,0},{28,4},{1,25},{... | collective-permute-start | bytes 196616 | tf_op jit(solution)/shard_map/ppermute | solution.py:39
  21.9 4.3 %collective-permute-start.6 = (f32[8,8,256]{2,1,0:T(8,128)S(1)}, f32[8,8,256]{2,1,0:T(8,128)S(1)}, u32[]{:S(2)}, u32[]{:S(2)}) collective-permute-start(f32[8,8,256]{2,1,0:T(8,128)S(1)} %bitcast.23), channel_id=1, source_target_pairs={{0,16},{4,20},{8,24},{12,28},{16,0},{20,4},{24,8},{28,12},{1,17},{... | collective-permute-start | bytes 196616 | tf_op jit(solution)/shard_map/ppermute | solution.py:39
  22.2 4.3 %collective-permute-start.5 = (f32[8,8,256]{2,1,0:T(8,128)S(1)}, f32[8,8,256]{2,1,0:T(8,128)S(1)}, u32[]{:S(2)}, u32[]{:S(2)}) collective-permute-start(f32[8,8,256]{2,1,0:T(8,128)S(1)} %bitcast.20), channel_id=1, source_target_pairs={{0,8},{4,12},{8,0},{12,4},{16,24},{20,28},{24,16},{28,20},{1,9},{5... | collective-permute-start | bytes 196616 | tf_op jit(solution)/shard_map/ppermute | solution.py:39
  22.4 6.0 %collective-permute-start.7 = (f32[8,8,256]{2,1,0:T(8,128)S(1)}, f32[8,8,256]{2,1,0:T(8,128)S(1)}, u32[]{:S(2)}, u32[]{:S(2)}) collective-permute-start(f32[8,8,256]{2,1,0:T(8,128)S(1)} %bitcast.18), channel_id=1, source_target_pairs={{0,24},{4,28},{8,16},{12,20},{16,8},{20,12},{24,0},{28,4},{1,25},{... | collective-permute-start | bytes 196616 | tf_op jit(solution)/shard_map/ppermute | solution.py:39
  28.4 1.4 %collective-permute-start.8 = (f32[4,4,8,256]{3,2,1,0:T(8,128)S(1)}, f32[4,4,8,256]{3,2,1,0:T(8,128)S(1)}, u32[]{:S(2)}, u32[]{:S(2)}) collective-permute-start(f32[4,4,8,256]{3,2,1,0:T(8,128)S(1)} %pad_maximum_fusion), channel_id=1, source_target_pairs={{0,4},{4,0},{8,12},{12,8},{16,20},{20,16},{24,28},{28,24},{1,5},{5... | collective-permute-start | bytes 393224 | tf_op jit(solution)/shard_map/ppermute | solution.py:39

commit v5 on v4

--- a/solution.py
+++ b/solution.py
@@ -29,9 +29,10 @@
     pairs = []
     for member in range(groups):
         for band in range(bands):
-            step = 1 if (member + band) % 2 == 0 else -1
-            other = band + step if 0 <= band + step < bands else band
-            pairs.append((member * bands + band, member * bands + other))
+            other, peer = band + (1 if (member + band) % 2 == 0 else -1), member
+            if not 0 <= other < bands:
+                other, peer = band, member ^ 2 if groups % 4 == 0 else member
+            pairs.append((member * bands + band, peer * bands + other))
     return pairs
 
 

time: 30.8 us -> 28.2 us (0.916)
  starting transfers between devices: 12.5 us -> 10.7 us
  waiting for transfers between devices: 12.9 us -> 12.2 us
    ppermute x1, starting transfers between devices: 4.84 us -> 3 us  [body(): halo = lax.ppermute(message, ('member', 'lat'), halo_pairs(groups, bands))]
    ppermute x8, waiting for transfers between devices: 10.4 us -> 9.75 us  [swap(): return lax.ppermute(x, 'member', [(i, i ^ distance) for i in range(groups)])]
  transfers between devices with their start and end apart: 9 -> 9, of which waited for: 9 -> 9; matrix products, arithmetic and copies ran while one was open for 0% -> 0% of each run, Pallas kernels for 5% -> 6%
where the time goes in v5:
time: 28.2 us; the launch traced here: 28.1 us
  waiting for transfers between devices  12.2 us (43%)
  starting transfers between devices  10.7 us (38%)
  Pallas kernels  5.09 us (18%)
    ppermute x8, waiting for transfers between devices, swap(): return lax.ppermute(x, 'member', [(i, i ^ distance) for i in range(groups)])  9.75 us
    ppermute x8, starting transfers between devices, swap(): return lax.ppermute(x, 'member', [(i, i ^ distance) for i in range(groups)])  7.67 us
    ppermute x1, starting transfers between devices, body(): halo = lax.ppermute(message, ('member', 'lat'), halo_pairs(groups, bands))  3 us
    ppermute x1, waiting for transfers between devices, body(): halo = lax.ppermute(message, ('member', 'lat'), halo_pairs(groups, bands))  2.5 us
    pallas_call x1, Pallas kernels, analysis(): pl.pallas_call(functools.partial(analysis_kernel, regions, parts), out_sh...  2.2 us
    pallas_call x1, Pallas kernels, stage(): pl.pallas_call(functools.partial(stage_kernel, bands), out_shape=tuple((j...  1.01 us
    pallas_call x1, Pallas kernels, place_rows(): pl.pallas_call(functools.partial(place_rows_kernel, bands, crossed), out_...  0.76 us
    pallas_call x1, Pallas kernels, per_cell(): pl.pallas_call(cells_kernel, out_shape=(shape, shape), in_specs=whole(3),...  0.63 us
  transfers between devices with their start and end apart: 9, of which 9 were waited for; matrix products, arithmetic and copies ran while one was open for 0% of the time, Pallas kernels for 6%

profile of v5, /device:TPU:0, one launch (start us, length us, event | category | flops | bytes accessed | tf_op | source)
XLA Modules:
  0.0 28.1 jit_solution(16616709144743075443)
XLA Ops:
  0.0 0.5 %collective-permute-start = (f32[4,8,8,256]{3,2,1,0:T(8,128)}, f32[4,8,8,256]{3,2,1,0:T(8,128)S(1)}, u32[]{:S(2)}, u32[]{:S(2)}) collective-permute-start(f32[4,8,8,256]{3,2,1,0:T(8,128)} %refs_0_.1), channel_id=1, source_target_pairs={{0,4},{4,0},{8,12},{12,8},{16,20},{20,16},{24,28},{28,24},{1,5},{5... | collective-permute-start | bytes 786440 | tf_op jit(solution)/shard_map/ppermute | solution.py:40
  0.5 1.0 %stage.1 = (f32[4,8,8,256]{3,2,1,0:T(8,128)S(1)}, f32[8,8,256]{2,1,0:T(8,128)S(1)}, f32[8,8,256]{2,1,0:T(8,128)S(1)}, s32[8,128]{1,0:T(8,128)S(1)}, f32[8,128]{1,0:T(8,128)S(1)}, /*index=5*/f32[8,128]{1,0:T(8,128)S(1)}) custom-call(f32[4,8,8,256]{3,2,1,0:T(8,128)} %refs_0_.1, f32[8,8,256]{2,1,0:T(8,128)} %refs_1_.1, f32[8,8,256]{2,1,0:T(8,128)} %refs_2_.1, ...), custom_call_target="tpu_custom_call" | custom-call | bytes 2097152 | tf_op jit(solution)/shard_map/stage/pallas_call | solution.py:61
  1.5 0.4 %collective-permute-done.partner_ref = f32[4,8,8,256]{3,2,1,0:T(8,128)S(1)} collective-permute-done((f32[4,8,8,256]{3,2,1,0:T(8,128)}, f32[4,8,8,256]{3,2,1,0:T(8,128)S(1)}, u32[]{:S(2)}, u32[]{:S(2)}) %collective-permute-start) | collective-permute-done | bytes 262176 | tf_op jit(solution)/shard_map/ppermute | solution.py:40
  1.9 3.0 %collective-permute-start.1 = (f32[18,8,256]{2,1,0:T(8,128)S(1)}, f32[18,8,256]{2,1,0:T(8,128)S(1)}, u32[]{:S(2)}, u32[]{:S(2)}) collective-permute-start(f32[18,8,256]{2,1,0:T(8,128)S(1)} %edges.1), channel_id=1, source_target_pairs={{0,1},{1,0},{2,3},{3,2},{4,12},{5,6},{6,5},{7,15},{8,9},{9,8},{10,... | collective-permute-start | bytes 442376 | tf_op jit(solution)/shard_map/ppermute | solution.py:346
  4.9 0.6 %per_cell.1 = (f32[8,256]{1,0:T(8,128)S(1)}, f32[8,256]{1,0:T(8,128)S(1)}) custom-call(s32[8,128]{1,0:T(8,128)S(1)} %get-tuple-element.24.cell_ref, f32[8,128]{1,0:T(8,128)S(1)} %get-tuple-element.25.value_ref, f32[8,128]{1,0:T(8,128)S(1)} %get-tuple-element.26.weight_ref), custom_call_target="tpu_custom_call" | custom-call | flops 1048576 | bytes 28672 | tf_op jit(solution)/shard_map/per_cell/pallas_call | solution.py:196
  5.5 2.5 %collective-permute-done.1.halo_ref = f32[18,8,256]{2,1,0:T(8,128)S(1)} collective-permute-done((f32[18,8,256]{2,1,0:T(8,128)S(1)}, f32[18,8,256]{2,1,0:T(8,128)S(1)}, u32[]{:S(2)}, u32[]{:S(2)}) %collective-permute-start.1) | collective-permute-done | bytes 147488 | tf_op jit(solution)/shard_map/ppermute | solution.py:346
  8.0 0.5 %forecast.1 = (f32[8,8,256]{2,1,0:T(8,128)S(1)}, f32[8,8,256]{2,1,0:T(8,128)S(1)}, f32[8,8,256]{2,1,0:T(8,128)S(1)}, f32[8,8,256]{2,1,0:T(8,128)S(1)}) custom-call(f32[4,8,8,256]{3,2,1,0:T(8,128)S(1)} %get-tuple-element.21.own_ref, f32[4,8,8,256]{3,2,1,0:T(8,128)S(1)} %collective-permute-done.partner_ref, f32[18,8,256]{2,1,0:T(8,128)S(1)} %collective-permute-done.1.halo_ref, ...), custom_call_target="tpu_custom_call" | custom-call | flops 1572864 | bytes 524288 | tf_op jit(solution)/shard_map/forecast/pallas_call | solution.py:163
  8.5 2.0 %collective-permute-start.2 = (f32[8,8,256]{2,1,0:T(8,128)S(1)}, f32[8,8,256]{2,1,0:T(8,128)S(1)}, u32[]{:S(2)}, u32[]{:S(2)}) collective-permute-start(f32[8,8,256]{2,1,0:T(8,128)S(1)} %get-tuple-element.30), channel_id=1, source_target_pairs={{0,8},{4,12},{8,0},{12,4},{16,24},{20,28},{24,16},{28,20},{1,9},{5... | collective-permute-start | bytes 196616 | tf_op jit(solution)/shard_map/ppermute | solution.py:40
  10.5 1.5 %collective-permute-start.3 = (f32[8,8,256]{2,1,0:T(8,128)S(1)}, f32[8,8,256]{2,1,0:T(8,128)S(1)}, u32[]{:S(2)}, u32[]{:S(2)}) collective-permute-start(f32[8,8,256]{2,1,0:T(8,128)S(1)} %get-tuple-element.31), channel_id=1, source_target_pairs={{0,16},{4,20},{8,24},{12,28},{16,0},{20,4},{24,8},{28,12},{1,17},{... | collective-permute-start | bytes 196616 | tf_op jit(solution)/shard_map/ppermute | solution.py:40
  12.0 0.0 collective-permute-start.4
  12.1 0.8 %collective-permute-done.2 = f32[8,8,256]{2,1,0:T(8,128)S(1)} collective-permute-done((f32[8,8,256]{2,1,0:T(8,128)S(1)}, f32[8,8,256]{2,1,0:T(8,128)S(1)}, u32[]{:S(2)}, u32[]{:S(2)}) %collective-permute-start.2) | collective-permute-done | bytes 65568 | tf_op jit(solution)/shard_map/ppermute | solution.py:40
  12.8 2.6 %collective-permute-done.3 = f32[8,8,256]{2,1,0:T(8,128)S(1)} collective-permute-done((f32[8,8,256]{2,1,0:T(8,128)S(1)}, f32[8,8,256]{2,1,0:T(8,128)S(1)}, u32[]{:S(2)}, u32[]{:S(2)}) %collective-permute-start.3) | collective-permute-done | bytes 65568 | tf_op jit(solution)/shard_map/ppermute | solution.py:40
  15.5 1.7 %collective-permute-done.4 = f32[8,8,256]{2,1,0:T(8,128)S(1)} collective-permute-done((f32[8,8,256]{2,1,0:T(8,128)S(1)}, f32[8,8,256]{2,1,0:T(8,128)S(1)}, u32[]{:S(2)}, u32[]{:S(2)}) %collective-permute-start.4) | collective-permute-done | bytes 65568 | tf_op jit(solution)/shard_map/ppermute | solution.py:40
  17.2 2.2 %analysis.1 = (f32[64,256]{1,0:T(8,128)S(1)}, f32[64,256]{1,0:T(8,128)S(1)}, f32[64,256]{1,0:T(8,128)S(1)}, f32[64,256]{1,0:T(8,128)S(1)}) custom-call(f32[64,256]{1,0:T(8,128)S(1)} %bitcast.17, f32[64,256]{1,0:T(8,128)S(1)} %bitcast.19, f32[64,256]{1,0:T(8,128)S(1)} %bitcast.21, f32[64,256]{1,0:T(8,128)S(1)} %bitcast.22, ...), custom_call_target="tpu_custom_call" | custom-call | flops 805306368 | bytes 524288 | tf_op jit(solution)/shard_map/analysis/pallas_call | solution.py:282
  19.4 0.6 %collective-permute-start.6 = (f32[8,8,256]{2,1,0:T(8,128)S(1)}, f32[8,8,256]{2,1,0:T(8,128)S(1)}, u32[]{:S(2)}, u32[]{:S(2)}) collective-permute-start(f32[8,8,256]{2,1,0:T(8,128)S(1)} %bitcast.23), channel_id=1, source_target_pairs={{0,16},{4,20},{8,24},{12,28},{16,0},{20,4},{24,8},{28,12},{1,17},{... | collective-permute-start | bytes 196616 | tf_op jit(solution)/shard_map/ppermute | solution.py:40
  20.0 0.1 collective-permute-start.5
  20.1 2.9 %collective-permute-start.7 = (f32[8,8,256]{2,1,0:T(8,128)S(1)}, f32[8,8,256]{2,1,0:T(8,128)S(1)}, u32[]{:S(2)}, u32[]{:S(2)}) collective-permute-start(f32[8,8,256]{2,1,0:T(8,128)S(1)} %bitcast.18), channel_id=1, source_target_pairs={{0,24},{4,28},{8,16},{12,20},{16,8},{20,12},{24,0},{28,4},{1,25},{... | collective-permute-start | bytes 196616 | tf_op jit(solution)/shard_map/ppermute | solution.py:40
  22.9 0.8 %collective-permute-done.6.refs_2_ = f32[8,8,256]{2,1,0:T(8,128)S(1)} collective-permute-done((f32[8,8,256]{2,1,0:T(8,128)S(1)}, f32[8,8,256]{2,1,0:T(8,128)S(1)}, u32[]{:S(2)}, u32[]{:S(2)}) %collective-permute-start.6) | collective-permute-done | bytes 65568 | tf_op jit(solution)/shard_map/ppermute | solution.py:40
  23.7 0.5 %collective-permute-done.5.refs_1_ = f32[8,8,256]{2,1,0:T(8,128)S(1)} collective-permute-done((f32[8,8,256]{2,1,0:T(8,128)S(1)}, f32[8,8,256]{2,1,0:T(8,128)S(1)}, u32[]{:S(2)}, u32[]{:S(2)}) %collective-permute-start.5) | collective-permute-done | bytes 65568 | tf_op jit(solution)/shard_map/ppermute | solution.py:40
  24.2 1.7 %collective-permute-done.7.refs_3_ = f32[8,8,256]{2,1,0:T(8,128)S(1)} collective-permute-done((f32[8,8,256]{2,1,0:T(8,128)S(1)}, f32[8,8,256]{2,1,0:T(8,128)S(1)}, u32[]{:S(2)}, u32[]{:S(2)}) %collective-permute-start.7) | collective-permute-done | bytes 65568 | tf_op jit(solution)/shard_map/ppermute | solution.py:40
  25.9 0.1 collective-permute-start.8
  26.0 1.3 %collective-permute-done.8.got_ref = f32[4,4,8,256]{3,2,1,0:T(8,128)S(1)} collective-permute-done((f32[4,4,8,256]{3,2,1,0:T(8,128)S(1)}, f32[4,4,8,256]{3,2,1,0:T(8,128)S(1)}, u32[]{:S(2)}, u32[]{:S(2)}) %collective-permute-start.8) | collective-permute-done | bytes 131104 | tf_op jit(solution)/shard_map/ppermute | solution.py:40
  27.3 0.8 %place_rows.1 = f32[4,8,8,256]{3,2,1,0:T(8,128)} custom-call(f32[4,4,8,256]{3,2,1,0:T(8,128)S(1)} %collective-permute-done.8.got_ref, f32[8,8,256]{2,1,0:T(8,128)S(1)} %bitcast.16, f32[8,8,256]{2,1,0:T(8,128)S(1)} %collective-permute-done.5.refs_1_, f32[8,8,256]{2,1,0:T(8,128)S(1)} %collective-permute-done.6.refs_2_, ...), custom_call_target="tpu_custom_call" | custom-call | tf_op jit(solution)/shard_map/place_rows/pallas_call | solution.py:316
  (6 shorter events, 0.0 us)
Async XLA Ops:
  0.0 1.9 %collective-permute-start = (f32[4,8,8,256]{3,2,1,0:T(8,128)}, f32[4,8,8,256]{3,2,1,0:T(8,128)S(1)}, u32[]{:S(2)}, u32[]{:S(2)}) collective-permute-start(f32[4,8,8,256]{3,2,1,0:T(8,128)} %refs_0_.1), channel_id=1, source_target_pairs={{0,4},{4,0},{8,12},{12,8},{16,20},{20,16},{24,28},{28,24},{1,5},{5... | collective-permute-start | bytes 786440 | tf_op jit(solution)/shard_map/ppermute | solution.py:40
  1.9 6.1 %collective-permute-start.1 = (f32[18,8,256]{2,1,0:T(8,128)S(1)}, f32[18,8,256]{2,1,0:T(8,128)S(1)}, u32[]{:S(2)}, u32[]{:S(2)}) collective-permute-start(f32[18,8,256]{2,1,0:T(8,128)S(1)} %edges.1), channel_id=1, source_target_pairs={{0,1},{1,0},{2,3},{3,2},{4,12},{5,6},{6,5},{7,15},{8,9},{9,8},{10,... | collective-permute-start | bytes 442376 | tf_op jit(solution)/shard_map/ppermute | solution.py:346
  8.5 4.3 %collective-permute-start.2 = (f32[8,8,256]{2,1,0:T(8,128)S(1)}, f32[8,8,256]{2,1,0:T(8,128)S(1)}, u32[]{:S(2)}, u32[]{:S(2)}) collective-permute-start(f32[8,8,256]{2,1,0:T(8,128)S(1)} %get-tuple-element.30), channel_id=1, source_target_pairs={{0,8},{4,12},{8,0},{12,4},{16,24},{20,28},{24,16},{28,20},{1,9},{5... | collective-permute-start | bytes 196616 | tf_op jit(solution)/shard_map/ppermute | solution.py:40
  10.5 5.0 %collective-permute-start.3 = (f32[8,8,256]{2,1,0:T(8,128)S(1)}, f32[8,8,256]{2,1,0:T(8,128)S(1)}, u32[]{:S(2)}, u32[]{:S(2)}) collective-permute-start(f32[8,8,256]{2,1,0:T(8,128)S(1)} %get-tuple-element.31), channel_id=1, source_target_pairs={{0,16},{4,20},{8,24},{12,28},{16,0},{20,4},{24,8},{28,12},{1,17},{... | collective-permute-start | bytes 196616 | tf_op jit(solution)/shard_map/ppermute | solution.py:40
  12.0 5.2 %collective-permute-start.4 = (f32[8,8,256]{2,1,0:T(8,128)S(1)}, f32[8,8,256]{2,1,0:T(8,128)S(1)}, u32[]{:S(2)}, u32[]{:S(2)}) collective-permute-start(f32[8,8,256]{2,1,0:T(8,128)S(1)} %get-tuple-element.32), channel_id=1, source_target_pairs={{0,24},{4,28},{8,16},{12,20},{16,8},{20,12},{24,0},{28,4},{1,25},{... | collective-permute-start | bytes 196616 | tf_op jit(solution)/shard_map/ppermute | solution.py:40
  19.4 4.3 %collective-permute-start.6 = (f32[8,8,256]{2,1,0:T(8,128)S(1)}, f32[8,8,256]{2,1,0:T(8,128)S(1)}, u32[]{:S(2)}, u32[]{:S(2)}) collective-permute-start(f32[8,8,256]{2,1,0:T(8,128)S(1)} %bitcast.23), channel_id=1, source_target_pairs={{0,16},{4,20},{8,24},{12,28},{16,0},{20,4},{24,8},{28,12},{1,17},{... | collective-permute-start | bytes 196616 | tf_op jit(solution)/shard_map/ppermute | solution.py:40
  20.0 4.3 %collective-permute-start.5 = (f32[8,8,256]{2,1,0:T(8,128)S(1)}, f32[8,8,256]{2,1,0:T(8,128)S(1)}, u32[]{:S(2)}, u32[]{:S(2)}) collective-permute-start(f32[8,8,256]{2,1,0:T(8,128)S(1)} %bitcast.20), channel_id=1, source_target_pairs={{0,8},{4,12},{8,0},{12,4},{16,24},{20,28},{24,16},{28,20},{1,9},{5... | collective-permute-start | bytes 196616 | tf_op jit(solution)/shard_map/ppermute | solution.py:40
  20.1 5.8 %collective-permute-start.7 = (f32[8,8,256]{2,1,0:T(8,128)S(1)}, f32[8,8,256]{2,1,0:T(8,128)S(1)}, u32[]{:S(2)}, u32[]{:S(2)}) collective-permute-start(f32[8,8,256]{2,1,0:T(8,128)S(1)} %bitcast.18), channel_id=1, source_target_pairs={{0,24},{4,28},{8,16},{12,20},{16,8},{20,12},{24,0},{28,4},{1,25},{... | collective-permute-start | bytes 196616 | tf_op jit(solution)/shard_map/ppermute | solution.py:40
  25.9 1.4 %collective-permute-start.8 = (f32[4,4,8,256]{3,2,1,0:T(8,128)S(1)}, f32[4,4,8,256]{3,2,1,0:T(8,128)S(1)}, u32[]{:S(2)}, u32[]{:S(2)}) collective-permute-start(f32[4,4,8,256]{3,2,1,0:T(8,128)S(1)} %pad_maximum_fusion), channel_id=1, source_target_pairs={{0,4},{4,0},{8,12},{12,8},{16,20},{20,16},{24,28},{28,24},{1,5},{5... | collective-permute-start | bytes 393224 | tf_op jit(solution)/shard_map/ppermute | solution.py:40

commit v6 on v5

--- a/solution.py
+++ b/solution.py
@@ -274,13 +274,124 @@
         ref[...] = result[i * share : (i + 1) * share]
 
 
+def halves(x):
+    return jnp.concatenate(split(x), axis=1)
+
+
+def folded_product(a, b):
+    n = b.shape[1] // 2
+    both = jnp.concatenate([b, b], axis=0)
+    out = jnp.dot(a, both, preferred_element_type=jnp.float32)
+    return out[:, :n] + out[:, n:]
+
+
+def folded_analysis_kernel(parts, *refs):
+    ens_refs, (dsum_ref, vsum_ref) = refs[:parts], refs[parts : parts + 2]
+    out_refs = refs[parts + 2 :]
+    share, lon = ens_refs[0].shape
+    count = share * parts // 8
+    size = count * 4
+
+    def low(n):
+        return lax.broadcasted_iota(jnp.int32, (8, n), 0) < 4
+
+    def turn(x):
+        return pltpu.roll(x, 4, x.ndim - 2)
+
+    def pattern(x):
+        r, first = turn(x), low(x.shape[1])
+        return jnp.where(first, x, r), jnp.where(first, r, x)
+
+    def spread(x):
+        n = x.shape[1]
+        return jnp.broadcast_to(x[None], (count // 2, 8, n)).reshape(size, n)
+
+    def over_members(x):
+        total = jnp.sum(x.reshape(count // 2, 8, x.shape[1]), axis=0)
+        return total + turn(total)
+
+    ens = jnp.concatenate([ref[...] for ref in ens_refs], axis=0).reshape(count, 8, lon)
+    dsum = dsum_ref[...]
+    mean = jnp.sum(ens, axis=0) * (1.0 / count)
+    pert = ens - mean[None]
+    turned = turn(pert).reshape(count // 2, 2, 8, lon)
+    pert = pert.reshape(count // 2, 2, 8, lon)
+    first = low(lon)[None]
+    groups = (
+        jnp.where(first, pert[:, 0], turned[:, 1]).reshape(size, lon),
+        jnp.where(first, turned[:, 0], pert[:, 1]).reshape(size, lon),
+    )
+    means = pattern(mean)
+    dsums = pattern(dsum)
+    pulls = pattern(vsum_ref[...] - dsum * mean)
+
+    row = lax.broadcasted_iota(jnp.int32, (size, size), 0)
+    col = lax.broadcasted_iota(jnp.int32, (size, size), 1)
+    same = lax.rem(row, 4) == lax.rem(col, 4)
+    one = jnp.where(row == col, 1.0, 0.0)
+
+    def start(x, dsum):
+        high, rest = split(x)
+        w_high, w_low = split(x * spread(dsum))
+        nt = (((1,), (1,)), ((), ()))
+        main = lax.dot_general(
+            w_high,
+            jnp.concatenate([high, rest], axis=0),
+            nt,
+            preferred_element_type=jnp.float32,
+        )
+        more = lax.dot_general(w_low, high, nt, preferred_element_type=jnp.float32)
+        gram = main[:, :size] + main[:, size:] + more
+        system = jnp.where(same, gram, 0.0) + (count - 1.0) * one
+        squares = jnp.sum(system * system, axis=1, keepdims=True)
+        frob = jnp.sqrt(over_members(jnp.broadcast_to(squares, (size, size))))
+        return system * spread(1.0 / frob), frob, jnp.concatenate([high, rest], axis=1)
+
+    begun = [start(x, d) for x, d in zip(groups, dsums)]
+    frobs = [b[1] for b in begun]
+    perts = [b[2] for b in begun]
+    steps = [b[0] for b in begun]
+    iterates = [halves(x) for x in steps]
+    inverses = None
+    for sweep in range(SWEEPS):
+        if inverses is not None:
+            steps = [folded_product(z, y) for z, y in zip(inverses, iterates)]
+        factors = [halves(1.5 * one - 0.5 * x) for x in steps]
+        if sweep == SWEEPS - 1:
+            break
+        iterates = [halves(folded_product(y, f)) for y, f in zip(iterates, factors)]
+        if inverses is None:
+            inverses = factors
+        else:
+            inverses = [halves(folded_product(f, z)) for f, z in zip(factors, inverses)]
+    partials = [halves(folded_product(z, x)) for z, x in zip(inverses, perts)]
+    results = []
+    for factor, part, frob, pull, mean_g in zip(factors, partials, frobs, pulls, means):
+        scale = jnp.concatenate([spread(lax.rsqrt(frob))] * (lon // size), axis=1)
+        update = folded_product(factor, part) * scale
+        gain = jnp.sum(update * spread(pull), axis=1, keepdims=True)
+        shift = mean_g + over_members(update * gain)
+        results.append(
+            (spread(shift) + jnp.sqrt(count - 1.0) * update).reshape(count // 2, 8, lon)
+        )
+    x, y = results
+    even, odd = jnp.where(first, x, turn(y)), jnp.where(first, turn(x), y)
+    for i in range(count // 2):
+        ref, k = out_refs[2 * i // (share // 8)], (2 * i) % (share // 8)
+        ref[8 * k : 8 * k + 8] = even[i]
+        ref[8 * k + 8 : 8 * k + 16] = odd[i]
+
+
 def analysis(ens, dsum, vsum):
     parts = len(ens)
     share, lon = ens[0].shape
     size = share * parts
     regions = dsum.shape[0]
-    return pl.pallas_call(
-        functools.partial(analysis_kernel, regions, parts),
+    kernel = functools.partial(analysis_kernel, regions, parts)
+    if regions == 8 and size == 256 and lon % 128 == 0 and share % 16 == 0:
+        kernel = functools.partial(folded_analysis_kernel, parts)
+    return pl.pallas_call(
+        kernel,
         out_shape=(jax.ShapeDtypeStruct((share, lon), jnp.float32),) * parts,
         in_specs=whole(parts + 2),
         out_specs=tuple(whole(parts)),

time: 28.2 us -> 27.5 us (0.975)
  Pallas kernels: 5.09 us -> 4.42 us
    pallas_call x1, Pallas kernels: 2.2 us -> 1.52 us  [analysis(): pl.pallas_call(kernel, out_shape=(jax.ShapeDtypeStruct((share, lon), jnp....]
where the time goes in v6:
time: 27.5 us; the launch traced here: 27.4 us
  waiting for transfers between devices  12.2 us (44%)
  starting transfers between devices  10.7 us (39%)
  Pallas kernels  4.42 us (16%)
    ppermute x8, waiting for transfers between devices, swap(): return lax.ppermute(x, 'member', [(i, i ^ distance) for i in range(groups)])  9.75 us
    ppermute x8, starting transfers between devices, swap(): return lax.ppermute(x, 'member', [(i, i ^ distance) for i in range(groups)])  7.67 us
    ppermute x1, starting transfers between devices, body(): halo = lax.ppermute(message, ('member', 'lat'), halo_pairs(groups, bands))  3 us
    ppermute x1, waiting for transfers between devices, body(): halo = lax.ppermute(message, ('member', 'lat'), halo_pairs(groups, bands))  2.5 us
    pallas_call x1, Pallas kernels, analysis(): pl.pallas_call(kernel, out_shape=(jax.ShapeDtypeStruct((share, lon), jnp....  1.52 us
    pallas_call x1, Pallas kernels, stage(): pl.pallas_call(functools.partial(stage_kernel, bands), out_shape=tuple((j...  1.01 us
    pallas_call x1, Pallas kernels, place_rows(): pl.pallas_call(functools.partial(place_rows_kernel, bands, crossed), out_...  0.76 us
    pallas_call x1, Pallas kernels, per_cell(): pl.pallas_call(cells_kernel, out_shape=(shape, shape), in_specs=whole(3),...  0.63 us
  transfers between devices with their start and end apart: 9, of which 9 were waited for; matrix products, arithmetic and copies ran while one was open for 0% of the time, Pallas kernels for 6%

profile of v6, /device:TPU:0, one launch (start us, length us, event | category | flops | bytes accessed | tf_op | source)
XLA Modules:
  0.0 27.4 jit_solution(7183538113759399894)
XLA Ops:
  0.0 0.5 %collective-permute-start = (f32[4,8,8,256]{3,2,1,0:T(8,128)}, f32[4,8,8,256]{3,2,1,0:T(8,128)S(1)}, u32[]{:S(2)}, u32[]{:S(2)}) collective-permute-start(f32[4,8,8,256]{3,2,1,0:T(8,128)} %refs_0_.1), channel_id=1, source_target_pairs={{0,4},{4,0},{8,12},{12,8},{16,20},{20,16},{24,28},{28,24},{1,5},{5... | collective-permute-start | bytes 786440 | tf_op jit(solution)/shard_map/ppermute | solution.py:40
  0.5 1.0 %stage.1 = (f32[4,8,8,256]{3,2,1,0:T(8,128)S(1)}, f32[8,8,256]{2,1,0:T(8,128)S(1)}, f32[8,8,256]{2,1,0:T(8,128)S(1)}, s32[8,128]{1,0:T(8,128)S(1)}, f32[8,128]{1,0:T(8,128)S(1)}, /*index=5*/f32[8,128]{1,0:T(8,128)S(1)}) custom-call(f32[4,8,8,256]{3,2,1,0:T(8,128)} %refs_0_.1, f32[8,8,256]{2,1,0:T(8,128)} %refs_1_.1, f32[8,8,256]{2,1,0:T(8,128)} %refs_2_.1, ...), custom_call_target="tpu_custom_call" | custom-call | bytes 2097152 | tf_op jit(solution)/shard_map/stage/pallas_call | solution.py:61
  1.5 0.4 %collective-permute-done.partner_ref = f32[4,8,8,256]{3,2,1,0:T(8,128)S(1)} collective-permute-done((f32[4,8,8,256]{3,2,1,0:T(8,128)}, f32[4,8,8,256]{3,2,1,0:T(8,128)S(1)}, u32[]{:S(2)}, u32[]{:S(2)}) %collective-permute-start) | collective-permute-done | bytes 262176 | tf_op jit(solution)/shard_map/ppermute | solution.py:40
  1.9 3.0 %collective-permute-start.1 = (f32[18,8,256]{2,1,0:T(8,128)S(1)}, f32[18,8,256]{2,1,0:T(8,128)S(1)}, u32[]{:S(2)}, u32[]{:S(2)}) collective-permute-start(f32[18,8,256]{2,1,0:T(8,128)S(1)} %edges.1), channel_id=1, source_target_pairs={{0,1},{1,0},{2,3},{3,2},{4,12},{5,6},{6,5},{7,15},{8,9},{9,8},{10,... | collective-permute-start | bytes 442376 | tf_op jit(solution)/shard_map/ppermute | solution.py:457
  4.9 0.6 %per_cell.1 = (f32[8,256]{1,0:T(8,128)S(1)}, f32[8,256]{1,0:T(8,128)S(1)}) custom-call(s32[8,128]{1,0:T(8,128)S(1)} %get-tuple-element.24.cell_ref, f32[8,128]{1,0:T(8,128)S(1)} %get-tuple-element.25.value_ref, f32[8,128]{1,0:T(8,128)S(1)} %get-tuple-element.26.weight_ref), custom_call_target="tpu_custom_call" | custom-call | flops 1048576 | bytes 28672 | tf_op jit(solution)/shard_map/per_cell/pallas_call | solution.py:196
  5.5 2.5 %collective-permute-done.1.halo_ref = f32[18,8,256]{2,1,0:T(8,128)S(1)} collective-permute-done((f32[18,8,256]{2,1,0:T(8,128)S(1)}, f32[18,8,256]{2,1,0:T(8,128)S(1)}, u32[]{:S(2)}, u32[]{:S(2)}) %collective-permute-start.1) | collective-permute-done | bytes 147488 | tf_op jit(solution)/shard_map/ppermute | solution.py:457
  8.0 0.5 %forecast.1 = (f32[8,8,256]{2,1,0:T(8,128)S(1)}, f32[8,8,256]{2,1,0:T(8,128)S(1)}, f32[8,8,256]{2,1,0:T(8,128)S(1)}, f32[8,8,256]{2,1,0:T(8,128)S(1)}) custom-call(f32[4,8,8,256]{3,2,1,0:T(8,128)S(1)} %get-tuple-element.21.own_ref, f32[4,8,8,256]{3,2,1,0:T(8,128)S(1)} %collective-permute-done.partner_ref, f32[18,8,256]{2,1,0:T(8,128)S(1)} %collective-permute-done.1.halo_ref, ...), custom_call_target="tpu_custom_call" | custom-call | flops 1572864 | bytes 524288 | tf_op jit(solution)/shard_map/forecast/pallas_call | solution.py:163
  8.5 2.0 %collective-permute-start.2 = (f32[8,8,256]{2,1,0:T(8,128)S(1)}, f32[8,8,256]{2,1,0:T(8,128)S(1)}, u32[]{:S(2)}, u32[]{:S(2)}) collective-permute-start(f32[8,8,256]{2,1,0:T(8,128)S(1)} %get-tuple-element.30), channel_id=1, source_target_pairs={{0,8},{4,12},{8,0},{12,4},{16,24},{20,28},{24,16},{28,20},{1,9},{5... | collective-permute-start | bytes 196616 | tf_op jit(solution)/shard_map/ppermute | solution.py:40
  10.5 1.5 %collective-permute-start.3 = (f32[8,8,256]{2,1,0:T(8,128)S(1)}, f32[8,8,256]{2,1,0:T(8,128)S(1)}, u32[]{:S(2)}, u32[]{:S(2)}) collective-permute-start(f32[8,8,256]{2,1,0:T(8,128)S(1)} %get-tuple-element.31), channel_id=1, source_target_pairs={{0,16},{4,20},{8,24},{12,28},{16,0},{20,4},{24,8},{28,12},{1,17},{... | collective-permute-start | bytes 196616 | tf_op jit(solution)/shard_map/ppermute | solution.py:40
  12.0 0.0 collective-permute-start.4
  12.1 0.8 %collective-permute-done.2 = f32[8,8,256]{2,1,0:T(8,128)S(1)} collective-permute-done((f32[8,8,256]{2,1,0:T(8,128)S(1)}, f32[8,8,256]{2,1,0:T(8,128)S(1)}, u32[]{:S(2)}, u32[]{:S(2)}) %collective-permute-start.2) | collective-permute-done | bytes 65568 | tf_op jit(solution)/shard_map/ppermute | solution.py:40
  12.8 2.6 %collective-permute-done.3 = f32[8,8,256]{2,1,0:T(8,128)S(1)} collective-permute-done((f32[8,8,256]{2,1,0:T(8,128)S(1)}, f32[8,8,256]{2,1,0:T(8,128)S(1)}, u32[]{:S(2)}, u32[]{:S(2)}) %collective-permute-start.3) | collective-permute-done | bytes 65568 | tf_op jit(solution)/shard_map/ppermute | solution.py:40
  15.5 1.7 %collective-permute-done.4 = f32[8,8,256]{2,1,0:T(8,128)S(1)} collective-permute-done((f32[8,8,256]{2,1,0:T(8,128)S(1)}, f32[8,8,256]{2,1,0:T(8,128)S(1)}, u32[]{:S(2)}, u32[]{:S(2)}) %collective-permute-start.4) | collective-permute-done | bytes 65568 | tf_op jit(solution)/shard_map/ppermute | solution.py:40
  17.2 1.5 %analysis.1 = (f32[64,256]{1,0:T(8,128)S(1)}, f32[64,256]{1,0:T(8,128)S(1)}, f32[64,256]{1,0:T(8,128)S(1)}, f32[64,256]{1,0:T(8,128)S(1)}) custom-call(f32[64,256]{1,0:T(8,128)S(1)} %bitcast.17, f32[64,256]{1,0:T(8,128)S(1)} %bitcast.19, f32[64,256]{1,0:T(8,128)S(1)} %bitcast.21, f32[64,256]{1,0:T(8,128)S(1)} %bitcast.22, ...), custom_call_target="tpu_custom_call" | custom-call | flops 805306368 | bytes 524288 | tf_op jit(solution)/shard_map/analysis/pallas_call | solution.py:393
  18.7 0.6 %collective-permute-start.6 = (f32[8,8,256]{2,1,0:T(8,128)S(1)}, f32[8,8,256]{2,1,0:T(8,128)S(1)}, u32[]{:S(2)}, u32[]{:S(2)}) collective-permute-start(f32[8,8,256]{2,1,0:T(8,128)S(1)} %bitcast.23), channel_id=1, source_target_pairs={{0,16},{4,20},{8,24},{12,28},{16,0},{20,4},{24,8},{28,12},{1,17},{... | collective-permute-start | bytes 196616 | tf_op jit(solution)/shard_map/ppermute | solution.py:40
  19.3 0.1 collective-permute-start.5
  19.4 2.9 %collective-permute-start.7 = (f32[8,8,256]{2,1,0:T(8,128)S(1)}, f32[8,8,256]{2,1,0:T(8,128)S(1)}, u32[]{:S(2)}, u32[]{:S(2)}) collective-permute-start(f32[8,8,256]{2,1,0:T(8,128)S(1)} %bitcast.18), channel_id=1, source_target_pairs={{0,24},{4,28},{8,16},{12,20},{16,8},{20,12},{24,0},{28,4},{1,25},{... | collective-permute-start | bytes 196616 | tf_op jit(solution)/shard_map/ppermute | solution.py:40
  22.3 0.8 %collective-permute-done.6.refs_2_ = f32[8,8,256]{2,1,0:T(8,128)S(1)} collective-permute-done((f32[8,8,256]{2,1,0:T(8,128)S(1)}, f32[8,8,256]{2,1,0:T(8,128)S(1)}, u32[]{:S(2)}, u32[]{:S(2)}) %collective-permute-start.6) | collective-permute-done | bytes 65568 | tf_op jit(solution)/shard_map/ppermute | solution.py:40
  23.1 0.5 %collective-permute-done.5.refs_1_ = f32[8,8,256]{2,1,0:T(8,128)S(1)} collective-permute-done((f32[8,8,256]{2,1,0:T(8,128)S(1)}, f32[8,8,256]{2,1,0:T(8,128)S(1)}, u32[]{:S(2)}, u32[]{:S(2)}) %collective-permute-start.5) | collective-permute-done | bytes 65568 | tf_op jit(solution)/shard_map/ppermute | solution.py:40
  23.6 1.7 %collective-permute-done.7.refs_3_ = f32[8,8,256]{2,1,0:T(8,128)S(1)} collective-permute-done((f32[8,8,256]{2,1,0:T(8,128)S(1)}, f32[8,8,256]{2,1,0:T(8,128)S(1)}, u32[]{:S(2)}, u32[]{:S(2)}) %collective-permute-start.7) | collective-permute-done | bytes 65568 | tf_op jit(solution)/shard_map/ppermute | solution.py:40
  25.2 0.1 collective-permute-start.8
  25.3 1.3 %collective-permute-done.8.got_ref = f32[4,4,8,256]{3,2,1,0:T(8,128)S(1)} collective-permute-done((f32[4,4,8,256]{3,2,1,0:T(8,128)S(1)}, f32[4,4,8,256]{3,2,1,0:T(8,128)S(1)}, u32[]{:S(2)}, u32[]{:S(2)}) %collective-permute-start.8) | collective-permute-done | bytes 131104 | tf_op jit(solution)/shard_map/ppermute | solution.py:40
  26.6 0.8 %place_rows.1 = f32[4,8,8,256]{3,2,1,0:T(8,128)} custom-call(f32[4,4,8,256]{3,2,1,0:T(8,128)S(1)} %collective-permute-done.8.got_ref, f32[8,8,256]{2,1,0:T(8,128)S(1)} %bitcast.16, f32[8,8,256]{2,1,0:T(8,128)S(1)} %collective-permute-done.5.refs_1_, f32[8,8,256]{2,1,0:T(8,128)S(1)} %collective-permute-done.6.refs_2_, ...), custom_call_target="tpu_custom_call" | custom-call | tf_op jit(solution)/shard_map/place_rows/pallas_call | solution.py:427
  (6 shorter events, 0.0 us)
Async XLA Ops:
  0.0 1.9 %collective-permute-start = (f32[4,8,8,256]{3,2,1,0:T(8,128)}, f32[4,8,8,256]{3,2,1,0:T(8,128)S(1)}, u32[]{:S(2)}, u32[]{:S(2)}) collective-permute-start(f32[4,8,8,256]{3,2,1,0:T(8,128)} %refs_0_.1), channel_id=1, source_target_pairs={{0,4},{4,0},{8,12},{12,8},{16,20},{20,16},{24,28},{28,24},{1,5},{5... | collective-permute-start | bytes 786440 | tf_op jit(solution)/shard_map/ppermute | solution.py:40
  1.9 6.1 %collective-permute-start.1 = (f32[18,8,256]{2,1,0:T(8,128)S(1)}, f32[18,8,256]{2,1,0:T(8,128)S(1)}, u32[]{:S(2)}, u32[]{:S(2)}) collective-permute-start(f32[18,8,256]{2,1,0:T(8,128)S(1)} %edges.1), channel_id=1, source_target_pairs={{0,1},{1,0},{2,3},{3,2},{4,12},{5,6},{6,5},{7,15},{8,9},{9,8},{10,... | collective-permute-start | bytes 442376 | tf_op jit(solution)/shard_map/ppermute | solution.py:457
  8.5 4.3 %collective-permute-start.2 = (f32[8,8,256]{2,1,0:T(8,128)S(1)}, f32[8,8,256]{2,1,0:T(8,128)S(1)}, u32[]{:S(2)}, u32[]{:S(2)}) collective-permute-start(f32[8,8,256]{2,1,0:T(8,128)S(1)} %get-tuple-element.30), channel_id=1, source_target_pairs={{0,8},{4,12},{8,0},{12,4},{16,24},{20,28},{24,16},{28,20},{1,9},{5... | collective-permute-start | bytes 196616 | tf_op jit(solution)/shard_map/ppermute | solution.py:40
  10.5 5.0 %collective-permute-start.3 = (f32[8,8,256]{2,1,0:T(8,128)S(1)}, f32[8,8,256]{2,1,0:T(8,128)S(1)}, u32[]{:S(2)}, u32[]{:S(2)}) collective-permute-start(f32[8,8,256]{2,1,0:T(8,128)S(1)} %get-tuple-element.31), channel_id=1, source_target_pairs={{0,16},{4,20},{8,24},{12,28},{16,0},{20,4},{24,8},{28,12},{1,17},{... | collective-permute-start | bytes 196616 | tf_op jit(solution)/shard_map/ppermute | solution.py:40
  12.0 5.2 %collective-permute-start.4 = (f32[8,8,256]{2,1,0:T(8,128)S(1)}, f32[8,8,256]{2,1,0:T(8,128)S(1)}, u32[]{:S(2)}, u32[]{:S(2)}) collective-permute-start(f32[8,8,256]{2,1,0:T(8,128)S(1)} %get-tuple-element.32), channel_id=1, source_target_pairs={{0,24},{4,28},{8,16},{12,20},{16,8},{20,12},{24,0},{28,4},{1,25},{... | collective-permute-start | bytes 196616 | tf_op jit(solution)/shard_map/ppermute | solution.py:40
  18.7 4.3 %collective-permute-start.6 = (f32[8,8,256]{2,1,0:T(8,128)S(1)}, f32[8,8,256]{2,1,0:T(8,128)S(1)}, u32[]{:S(2)}, u32[]{:S(2)}) collective-permute-start(f32[8,8,256]{2,1,0:T(8,128)S(1)} %bitcast.23), channel_id=1, source_target_pairs={{0,16},{4,20},{8,24},{12,28},{16,0},{20,4},{24,8},{28,12},{1,17},{... | collective-permute-start | bytes 196616 | tf_op jit(solution)/shard_map/ppermute | solution.py:40
  19.3 4.3 %collective-permute-start.5 = (f32[8,8,256]{2,1,0:T(8,128)S(1)}, f32[8,8,256]{2,1,0:T(8,128)S(1)}, u32[]{:S(2)}, u32[]{:S(2)}) collective-permute-start(f32[8,8,256]{2,1,0:T(8,128)S(1)} %bitcast.20), channel_id=1, source_target_pairs={{0,8},{4,12},{8,0},{12,4},{16,24},{20,28},{24,16},{28,20},{1,9},{5... | collective-permute-start | bytes 196616 | tf_op jit(solution)/shard_map/ppermute | solution.py:40
  19.4 5.8 %collective-permute-start.7 = (f32[8,8,256]{2,1,0:T(8,128)S(1)}, f32[8,8,256]{2,1,0:T(8,128)S(1)}, u32[]{:S(2)}, u32[]{:S(2)}) collective-permute-start(f32[8,8,256]{2,1,0:T(8,128)S(1)} %bitcast.18), channel_id=1, source_target_pairs={{0,24},{4,28},{8,16},{12,20},{16,8},{20,12},{24,0},{28,4},{1,25},{... | collective-permute-start | bytes 196616 | tf_op jit(solution)/shard_map/ppermute | solution.py:40
  25.2 1.4 %collective-permute-start.8 = (f32[4,4,8,256]{3,2,1,0:T(8,128)S(1)}, f32[4,4,8,256]{3,2,1,0:T(8,128)S(1)}, u32[]{:S(2)}, u32[]{:S(2)}) collective-permute-start(f32[4,4,8,256]{3,2,1,0:T(8,128)S(1)} %pad_maximum_fusion), channel_id=1, source_target_pairs={{0,4},{4,0},{8,12},{12,8},{16,20},{20,16},{24,28},{28,24},{1,5},{5... | collective-permute-start | bytes 393224 | tf_op jit(solution)/shard_map/ppermute | solution.py:40

commit v7 on v6

--- a/solution.py
+++ b/solution.py
@@ -403,16 +403,17 @@
     )(*ens, dsum, vsum)
 
 
-def place_rows_kernel(bands, crossed, got_ref, *refs):
-    half_refs, out_ref, sems = refs[:-2], refs[-2], refs[-1]
-    half = len(half_refs)
+def place_rows_kernel(bands, crossed, *refs):
+    out_ref, sems = refs[-2:]
+    half = out_ref.shape[1] // 2
+    got_refs, half_refs = refs[:half], refs[half : 2 * half]
     members = out_ref.shape[0]
     chip, high, at_edge = place(bands)
     base = jnp.where(high, half, 0)
     copies = []
     for t, ref in enumerate(half_refs):
         r = row_of(chip, t, crossed)
-        for source, row in ((ref.at[pl.ds(0, members)], base + r), (got_ref.at[t], half - base + r)):
+        for source, row in ((ref.at[pl.ds(0, members)], base + r), (got_refs[t], half - base + r)):
             copies.append(
                 pltpu.make_async_copy(source, out_ref.at[:, row], sems.at[len(copies)])
             )
@@ -427,12 +428,12 @@
     return pl.pallas_call(
         functools.partial(place_rows_kernel, bands, crossed),
         out_shape=jax.ShapeDtypeStruct(shape, jnp.float32),
-        in_specs=whole(1 + half),
+        in_specs=whole(2 * half),
         out_specs=pl.BlockSpec(memory_space=pltpu.HBM),
         scratch_shapes=[pltpu.SemaphoreType.DMA((2 * half,))],
         compiler_params=SMALL,
         name="place_rows",
-    )(got, *halves)
+    )(*got, *halves)
 
 
 def body(state, zonal_wind, meridional_wind, obs_cell, obs_value, obs_weight):
@@ -479,7 +480,7 @@
     if not crossed:
         field = back[0].transpose(1, 0, 2, 3).reshape(2 * members, half, levels, lon)
         back = [field[:, t] for t in range(half)]
-    got = swap(jnp.stack([b[members:] for b in back]), groups, 1)
+    got = [swap(b[members:], groups, 1) for b in back]
     return place_rows(bands, crossed, got, back, state.shape)
 
 

time: 27.5 us -> 27.3 us (level)
    ppermute x8 -> x11, waiting for transfers between devices: 9.75 us -> 9.58 us  [swap(): return lax.ppermute(x, 'member', [(i, i ^ distance) for i in range(groups)])]
    ppermute x8 -> x11, starting transfers between devices: 7.67 us -> 7.62 us  [swap(): return lax.ppermute(x, 'member', [(i, i ^ distance) for i in range(groups)])]
  transfers between devices with their start and end apart: 9 -> 12, of which waited for: 9 -> 9; matrix products, arithmetic and copies ran while one was open for 0% -> 0% of each run, Pallas kernels for 6% -> 6%
where the time goes in v7:
time: 27.3 us; the launch traced here: 27.2 us
  waiting for transfers between devices  12.1 us (44%)
  starting transfers between devices  10.6 us (39%)
  Pallas kernels  4.42 us (16%)
    ppermute x11, waiting for transfers between devices, swap(): return lax.ppermute(x, 'member', [(i, i ^ distance) for i in range(groups)])  9.58 us
    ppermute x11, starting transfers between devices, swap(): return lax.ppermute(x, 'member', [(i, i ^ distance) for i in range(groups)])  7.62 us
    ppermute x1, starting transfers between devices, body(): halo = lax.ppermute(message, ('member', 'lat'), halo_pairs(groups, bands))  3 us
    ppermute x1, waiting for transfers between devices, body(): halo = lax.ppermute(message, ('member', 'lat'), halo_pairs(groups, bands))  2.5 us
    pallas_call x1, Pallas kernels, analysis(): pl.pallas_call(kernel, out_shape=(jax.ShapeDtypeStruct((share, lon), jnp....  1.52 us
    pallas_call x1, Pallas kernels, stage(): pl.pallas_call(functools.partial(stage_kernel, bands), out_shape=tuple((j...  1.01 us
    pallas_call x1, Pallas kernels, place_rows(): pl.pallas_call(functools.partial(place_rows_kernel, bands, crossed), out_...  0.76 us
    pallas_call x1, Pallas kernels, per_cell(): pl.pallas_call(cells_kernel, out_shape=(shape, shape), in_specs=whole(3),...  0.63 us
  transfers between devices with their start and end apart: 12, of which 9 were waited for; matrix products, arithmetic and copies ran while one was open for 0% of the time, Pallas kernels for 6%

profile of v7, /device:TPU:0, one launch (start us, length us, event | category | flops | bytes accessed | tf_op | source)
XLA Modules:
  0.0 27.2 jit_solution(14210496373029247760)
XLA Ops:
  0.0 0.5 %collective-permute-start = (f32[4,8,8,256]{3,2,1,0:T(8,128)}, f32[4,8,8,256]{3,2,1,0:T(8,128)S(1)}, u32[]{:S(2)}, u32[]{:S(2)}) collective-permute-start(f32[4,8,8,256]{3,2,1,0:T(8,128)} %refs_0_.1), channel_id=1, source_target_pairs={{0,4},{4,0},{8,12},{12,8},{16,20},{20,16},{24,28},{28,24},{1,5},{5... | collective-permute-start | bytes 786440 | tf_op jit(solution)/shard_map/ppermute | solution.py:40
  0.5 1.0 %stage.1 = (f32[4,8,8,256]{3,2,1,0:T(8,128)S(1)}, f32[8,8,256]{2,1,0:T(8,128)S(1)}, f32[8,8,256]{2,1,0:T(8,128)S(1)}, s32[8,128]{1,0:T(8,128)S(1)}, f32[8,128]{1,0:T(8,128)S(1)}, /*index=5*/f32[8,128]{1,0:T(8,128)S(1)}) custom-call(f32[4,8,8,256]{3,2,1,0:T(8,128)} %refs_0_.1, f32[8,8,256]{2,1,0:T(8,128)} %refs_1_.1, f32[8,8,256]{2,1,0:T(8,128)} %refs_2_.1, ...), custom_call_target="tpu_custom_call" | custom-call | bytes 2097152 | tf_op jit(solution)/shard_map/stage/pallas_call | solution.py:61
  1.5 0.4 %collective-permute-done.partner_ref = f32[4,8,8,256]{3,2,1,0:T(8,128)S(1)} collective-permute-done((f32[4,8,8,256]{3,2,1,0:T(8,128)}, f32[4,8,8,256]{3,2,1,0:T(8,128)S(1)}, u32[]{:S(2)}, u32[]{:S(2)}) %collective-permute-start) | collective-permute-done | bytes 262176 | tf_op jit(solution)/shard_map/ppermute | solution.py:40
  1.9 3.0 %collective-permute-start.1 = (f32[18,8,256]{2,1,0:T(8,128)S(1)}, f32[18,8,256]{2,1,0:T(8,128)S(1)}, u32[]{:S(2)}, u32[]{:S(2)}) collective-permute-start(f32[18,8,256]{2,1,0:T(8,128)S(1)} %edges.1), channel_id=1, source_target_pairs={{0,1},{1,0},{2,3},{3,2},{4,12},{5,6},{6,5},{7,15},{8,9},{9,8},{10,... | collective-permute-start | bytes 442376 | tf_op jit(solution)/shard_map/ppermute | solution.py:458
  4.9 0.6 %per_cell.1 = (f32[8,256]{1,0:T(8,128)S(1)}, f32[8,256]{1,0:T(8,128)S(1)}) custom-call(s32[8,128]{1,0:T(8,128)S(1)} %get-tuple-element.24.cell_ref, f32[8,128]{1,0:T(8,128)S(1)} %get-tuple-element.25.value_ref, f32[8,128]{1,0:T(8,128)S(1)} %get-tuple-element.26.weight_ref), custom_call_target="tpu_custom_call" | custom-call | flops 1048576 | bytes 28672 | tf_op jit(solution)/shard_map/per_cell/pallas_call | solution.py:196
  5.5 2.5 %collective-permute-done.1.halo_ref = f32[18,8,256]{2,1,0:T(8,128)S(1)} collective-permute-done((f32[18,8,256]{2,1,0:T(8,128)S(1)}, f32[18,8,256]{2,1,0:T(8,128)S(1)}, u32[]{:S(2)}, u32[]{:S(2)}) %collective-permute-start.1) | collective-permute-done | bytes 147488 | tf_op jit(solution)/shard_map/ppermute | solution.py:458
  8.0 0.5 %forecast.1 = (f32[8,8,256]{2,1,0:T(8,128)S(1)}, f32[8,8,256]{2,1,0:T(8,128)S(1)}, f32[8,8,256]{2,1,0:T(8,128)S(1)}, f32[8,8,256]{2,1,0:T(8,128)S(1)}) custom-call(f32[4,8,8,256]{3,2,1,0:T(8,128)S(1)} %get-tuple-element.21.own_ref, f32[4,8,8,256]{3,2,1,0:T(8,128)S(1)} %collective-permute-done.partner_ref, f32[18,8,256]{2,1,0:T(8,128)S(1)} %collective-permute-done.1.halo_ref, ...), custom_call_target="tpu_custom_call" | custom-call | flops 1572864 | bytes 524288 | tf_op jit(solution)/shard_map/forecast/pallas_call | solution.py:163
  8.5 2.0 %collective-permute-start.2 = (f32[8,8,256]{2,1,0:T(8,128)S(1)}, f32[8,8,256]{2,1,0:T(8,128)S(1)}, u32[]{:S(2)}, u32[]{:S(2)}) collective-permute-start(f32[8,8,256]{2,1,0:T(8,128)S(1)} %get-tuple-element.30), channel_id=1, source_target_pairs={{0,8},{4,12},{8,0},{12,4},{16,24},{20,28},{24,16},{28,20},{1,9},{5... | collective-permute-start | bytes 196616 | tf_op jit(solution)/shard_map/ppermute | solution.py:40
  10.5 1.5 %collective-permute-start.3 = (f32[8,8,256]{2,1,0:T(8,128)S(1)}, f32[8,8,256]{2,1,0:T(8,128)S(1)}, u32[]{:S(2)}, u32[]{:S(2)}) collective-permute-start(f32[8,8,256]{2,1,0:T(8,128)S(1)} %get-tuple-element.31), channel_id=1, source_target_pairs={{0,16},{4,20},{8,24},{12,28},{16,0},{20,4},{24,8},{28,12},{1,17},{... | collective-permute-start | bytes 196616 | tf_op jit(solution)/shard_map/ppermute | solution.py:40
  12.0 0.0 collective-permute-start.4
  12.1 0.8 %collective-permute-done.2 = f32[8,8,256]{2,1,0:T(8,128)S(1)} collective-permute-done((f32[8,8,256]{2,1,0:T(8,128)S(1)}, f32[8,8,256]{2,1,0:T(8,128)S(1)}, u32[]{:S(2)}, u32[]{:S(2)}) %collective-permute-start.2) | collective-permute-done | bytes 65568 | tf_op jit(solution)/shard_map/ppermute | solution.py:40
  12.8 2.6 %collective-permute-done.3 = f32[8,8,256]{2,1,0:T(8,128)S(1)} collective-permute-done((f32[8,8,256]{2,1,0:T(8,128)S(1)}, f32[8,8,256]{2,1,0:T(8,128)S(1)}, u32[]{:S(2)}, u32[]{:S(2)}) %collective-permute-start.3) | collective-permute-done | bytes 65568 | tf_op jit(solution)/shard_map/ppermute | solution.py:40
  15.5 1.7 %collective-permute-done.4 = f32[8,8,256]{2,1,0:T(8,128)S(1)} collective-permute-done((f32[8,8,256]{2,1,0:T(8,128)S(1)}, f32[8,8,256]{2,1,0:T(8,128)S(1)}, u32[]{:S(2)}, u32[]{:S(2)}) %collective-permute-start.4) | collective-permute-done | bytes 65568 | tf_op jit(solution)/shard_map/ppermute | solution.py:40
  17.2 1.5 %analysis.1 = (f32[64,256]{1,0:T(8,128)S(1)}, f32[64,256]{1,0:T(8,128)S(1)}, f32[64,256]{1,0:T(8,128)S(1)}, f32[64,256]{1,0:T(8,128)S(1)}) custom-call(f32[64,256]{1,0:T(8,128)S(1)} %bitcast.12, f32[64,256]{1,0:T(8,128)S(1)} %bitcast.14, f32[64,256]{1,0:T(8,128)S(1)} %bitcast.16, f32[64,256]{1,0:T(8,128)S(1)} %bitcast.17, ...), custom_call_target="tpu_custom_call" | custom-call | flops 805306368 | bytes 524288 | tf_op jit(solution)/shard_map/analysis/pallas_call | solution.py:393
  18.7 0.6 %collective-permute-start.8 = (f32[8,8,256]{2,1,0:T(8,128)S(1)}, f32[8,8,256]{2,1,0:T(8,128)S(1)}, u32[]{:S(2)}, u32[]{:S(2)}) collective-permute-start(f32[8,8,256]{2,1,0:T(8,128)S(1)} %bitcast.15), channel_id=1, source_target_pairs={{0,16},{4,20},{8,24},{12,28},{16,0},{20,4},{24,8},{28,12},{1,17},{... | collective-permute-start | bytes 196616 | tf_op jit(solution)/shard_map/ppermute | solution.py:40
  19.3 0.1 collective-permute-start.6
  19.4 2.9 %collective-permute-start.10 = (f32[8,8,256]{2,1,0:T(8,128)S(1)}, f32[8,8,256]{2,1,0:T(8,128)S(1)}, u32[]{:S(2)}, u32[]{:S(2)}) collective-permute-start(f32[8,8,256]{2,1,0:T(8,128)S(1)} %bitcast.11), channel_id=1, source_target_pairs={{0,24},{4,28},{8,16},{12,20},{16,8},{20,12},{24,0},{28,4},{1,25},{... | collective-permute-start | bytes 196616 | tf_op jit(solution)/shard_map/ppermute | solution.py:40
  22.3 0.0 collective-permute-start.5
  22.3 0.8 %collective-permute-done.8.refs_6_ = f32[8,8,256]{2,1,0:T(8,128)S(1)} collective-permute-done((f32[8,8,256]{2,1,0:T(8,128)S(1)}, f32[8,8,256]{2,1,0:T(8,128)S(1)}, u32[]{:S(2)}, u32[]{:S(2)}) %collective-permute-start.8) | collective-permute-done | bytes 65568 | tf_op jit(solution)/shard_map/ppermute | solution.py:40
  23.1 0.0 collective-permute-start.9
  23.1 0.5 %collective-permute-done.6.refs_5_ = f32[8,8,256]{2,1,0:T(8,128)S(1)} collective-permute-done((f32[8,8,256]{2,1,0:T(8,128)S(1)}, f32[8,8,256]{2,1,0:T(8,128)S(1)}, u32[]{:S(2)}, u32[]{:S(2)}) %collective-permute-start.6) | collective-permute-done | bytes 65568 | tf_op jit(solution)/shard_map/ppermute | solution.py:40
  23.6 0.0 collective-permute-start.7
  23.6 1.6 %collective-permute-done.10.refs_7_ = f32[8,8,256]{2,1,0:T(8,128)S(1)} collective-permute-done((f32[8,8,256]{2,1,0:T(8,128)S(1)}, f32[8,8,256]{2,1,0:T(8,128)S(1)}, u32[]{:S(2)}, u32[]{:S(2)}) %collective-permute-start.10) | collective-permute-done | bytes 65568 | tf_op jit(solution)/shard_map/ppermute | solution.py:40
  25.2 0.0 collective-permute-start.11
  25.2 0.0 collective-permute-done.5.refs_0_
  25.2 0.0 collective-permute-done.9.refs_2_
  25.2 0.0 collective-permute-done.7.refs_1_
  25.2 1.2 %collective-permute-done.11.refs_3_ = f32[4,8,256]{2,1,0:T(8,128)S(1)} collective-permute-done((f32[4,8,256]{2,1,0:T(8,128)S(1)}, f32[4,8,256]{2,1,0:T(8,128)S(1)}, u32[]{:S(2)}, u32[]{:S(2)}) %collective-permute-start.11) | collective-permute-done | bytes 32800 | tf_op jit(solution)/shard_map/ppermute | solution.py:40
  26.4 0.8 %place_rows.1 = f32[4,8,8,256]{3,2,1,0:T(8,128)} custom-call(f32[4,8,256]{2,1,0:T(8,128)S(1)} %collective-permute-done.5.refs_0_, f32[4,8,256]{2,1,0:T(8,128)S(1)} %collective-permute-done.7.refs_1_, f32[4,8,256]{2,1,0:T(8,128)S(1)} %collective-permute-done.9.refs_2_, f32[4,8,256]{2,1,0:T(8,128)S(1)} %collective-permute-done.11.refs_3_, ...), custom_call_target="tpu_custom_call" | custom-call | tf_op jit(solution)/shard_map/place_rows/pallas_call | solution.py:428
  (5 shorter events, 0.0 us)
Async XLA Ops:
  0.0 1.9 %collective-permute-start = (f32[4,8,8,256]{3,2,1,0:T(8,128)}, f32[4,8,8,256]{3,2,1,0:T(8,128)S(1)}, u32[]{:S(2)}, u32[]{:S(2)}) collective-permute-start(f32[4,8,8,256]{3,2,1,0:T(8,128)} %refs_0_.1), channel_id=1, source_target_pairs={{0,4},{4,0},{8,12},{12,8},{16,20},{20,16},{24,28},{28,24},{1,5},{5... | collective-permute-start | bytes 786440 | tf_op jit(solution)/shard_map/ppermute | solution.py:40
  1.9 6.1 %collective-permute-start.1 = (f32[18,8,256]{2,1,0:T(8,128)S(1)}, f32[18,8,256]{2,1,0:T(8,128)S(1)}, u32[]{:S(2)}, u32[]{:S(2)}) collective-permute-start(f32[18,8,256]{2,1,0:T(8,128)S(1)} %edges.1), channel_id=1, source_target_pairs={{0,1},{1,0},{2,3},{3,2},{4,12},{5,6},{6,5},{7,15},{8,9},{9,8},{10,... | collective-permute-start | bytes 442376 | tf_op jit(solution)/shard_map/ppermute | solution.py:458
  8.5 4.3 %collective-permute-start.2 = (f32[8,8,256]{2,1,0:T(8,128)S(1)}, f32[8,8,256]{2,1,0:T(8,128)S(1)}, u32[]{:S(2)}, u32[]{:S(2)}) collective-permute-start(f32[8,8,256]{2,1,0:T(8,128)S(1)} %get-tuple-element.30), channel_id=1, source_target_pairs={{0,8},{4,12},{8,0},{12,4},{16,24},{20,28},{24,16},{28,20},{1,9},{5... | collective-permute-start | bytes 196616 | tf_op jit(solution)/shard_map/ppermute | solution.py:40
  10.5 5.0 %collective-permute-start.3 = (f32[8,8,256]{2,1,0:T(8,128)S(1)}, f32[8,8,256]{2,1,0:T(8,128)S(1)}, u32[]{:S(2)}, u32[]{:S(2)}) collective-permute-start(f32[8,8,256]{2,1,0:T(8,128)S(1)} %get-tuple-element.31), channel_id=1, source_target_pairs={{0,16},{4,20},{8,24},{12,28},{16,0},{20,4},{24,8},{28,12},{1,17},{... | collective-permute-start | bytes 196616 | tf_op jit(solution)/shard_map/ppermute | solution.py:40
  12.0 5.2 %collective-permute-start.4 = (f32[8,8,256]{2,1,0:T(8,128)S(1)}, f32[8,8,256]{2,1,0:T(8,128)S(1)}, u32[]{:S(2)}, u32[]{:S(2)}) collective-permute-start(f32[8,8,256]{2,1,0:T(8,128)S(1)} %get-tuple-element.32), channel_id=1, source_target_pairs={{0,24},{4,28},{8,16},{12,20},{16,8},{20,12},{24,0},{28,4},{1,25},{... | collective-permute-start | bytes 196616 | tf_op jit(solution)/shard_map/ppermute | solution.py:40
  18.7 4.3 %collective-permute-start.8 = (f32[8,8,256]{2,1,0:T(8,128)S(1)}, f32[8,8,256]{2,1,0:T(8,128)S(1)}, u32[]{:S(2)}, u32[]{:S(2)}) collective-permute-start(f32[8,8,256]{2,1,0:T(8,128)S(1)} %bitcast.15), channel_id=1, source_target_pairs={{0,16},{4,20},{8,24},{12,28},{16,0},{20,4},{24,8},{28,12},{1,17},{... | collective-permute-start | bytes 196616 | tf_op jit(solution)/shard_map/ppermute | solution.py:40
  19.3 4.3 %collective-permute-start.6 = (f32[8,8,256]{2,1,0:T(8,128)S(1)}, f32[8,8,256]{2,1,0:T(8,128)S(1)}, u32[]{:S(2)}, u32[]{:S(2)}) collective-permute-start(f32[8,8,256]{2,1,0:T(8,128)S(1)} %bitcast.13), channel_id=1, source_target_pairs={{0,8},{4,12},{8,0},{12,4},{16,24},{20,28},{24,16},{28,20},{1,9},{5... | collective-permute-start | bytes 196616 | tf_op jit(solution)/shard_map/ppermute | solution.py:40
  19.4 5.8 %collective-permute-start.10 = (f32[8,8,256]{2,1,0:T(8,128)S(1)}, f32[8,8,256]{2,1,0:T(8,128)S(1)}, u32[]{:S(2)}, u32[]{:S(2)}) collective-permute-start(f32[8,8,256]{2,1,0:T(8,128)S(1)} %bitcast.11), channel_id=1, source_target_pairs={{0,24},{4,28},{8,16},{12,20},{16,8},{20,12},{24,0},{28,4},{1,25},{... | collective-permute-start | bytes 196616 | tf_op jit(solution)/shard_map/ppermute | solution.py:40
  22.3 2.9 %collective-permute-start.5 = (f32[4,8,256]{2,1,0:T(8,128)S(1)}, f32[4,8,256]{2,1,0:T(8,128)S(1)}, u32[]{:S(2)}, u32[]{:S(2)}) collective-permute-start(f32[4,8,256]{2,1,0:T(8,128)S(1)} %slice_bitcast_fusion), channel_id=1, source_target_pairs={{0,4},{4,0},{8,12},{12,8},{16,20},{20,16},{24,28},{28,24},{1,5},{5... | collective-permute-start | bytes 98312 | tf_op jit(solution)/shard_map/ppermute | solution.py:40
  23.1 2.2 %collective-permute-start.9 = (f32[4,8,256]{2,1,0:T(8,128)S(1)}, f32[4,8,256]{2,1,0:T(8,128)S(1)}, u32[]{:S(2)}, u32[]{:S(2)}) collective-permute-start(f32[4,8,256]{2,1,0:T(8,128)S(1)} %slice.21), channel_id=1, source_target_pairs={{0,4},{4,0},{8,12},{12,8},{16,20},{20,16},{24,28},{28,24},{1,5},{5... | collective-permute-start | bytes 98312 | tf_op jit(solution)/shard_map/ppermute | solution.py:40
  23.6 1.7 %collective-permute-start.7 = (f32[4,8,256]{2,1,0:T(8,128)S(1)}, f32[4,8,256]{2,1,0:T(8,128)S(1)}, u32[]{:S(2)}, u32[]{:S(2)}) collective-permute-start(f32[4,8,256]{2,1,0:T(8,128)S(1)} %slice.20), channel_id=1, source_target_pairs={{0,4},{4,0},{8,12},{12,8},{16,20},{20,16},{24,28},{28,24},{1,5},{5... | collective-permute-start | bytes 98312 | tf_op jit(solution)/shard_map/ppermute | solution.py:40
  25.2 1.2 %collective-permute-start.11 = (f32[4,8,256]{2,1,0:T(8,128)S(1)}, f32[4,8,256]{2,1,0:T(8,128)S(1)}, u32[]{:S(2)}, u32[]{:S(2)}) collective-permute-start(f32[4,8,256]{2,1,0:T(8,128)S(1)} %slice.22), channel_id=1, source_target_pairs={{0,4},{4,0},{8,12},{12,8},{16,20},{20,16},{24,28},{28,24},{1,5},{5... | collective-permute-start | bytes 98312 | tf_op jit(solution)/shard_map/ppermute | solution.py:40

commit v8 on v7

--- a/solution.py
+++ b/solution.py
@@ -23,6 +23,10 @@
     high = lax.rem(core + band, 2) == 0
     at_edge = jnp.where(high, band == bands - 1, band == 0)
     return chip, high, at_edge
+
+
+def row_at(high, rows, e):
+    return jnp.where(high, rows - 1 - e, e)
 
 
 def halo_pairs(groups, bands):
@@ -43,7 +47,9 @@
 def stage_kernel(bands, *refs):
     sources, targets, sems = refs[:6], refs[6:12], refs[12]
     chip, high, at_edge = place(bands)
-    mine = jnp.where(high, sources[3].shape[0] // 2, 0) + chip
+    rows, levels = sources[0].shape[1:3]
+    per_row = levels // sources[3].shape[1]
+    mine = row_at(high, rows, lax.div(chip, per_row)) * per_row + lax.rem(chip, per_row)
     sources = list(sources[:3]) + [ref.at[mine] for ref in sources[3:]]
     copies = [
         pltpu.make_async_copy(source, target, sems.at[i])
@@ -73,12 +79,11 @@
 def edges_kernel(bands, own_ref, partner_ref, zonal_ref, merid_ref, out_ref):
     members, rows, levels, lon = own_ref.shape
     chip, high, at_edge = place(bands)
-    first = jnp.where(high, rows - 2, 0)
-    edge = jnp.where(high, rows - 1, 0)
+    edge = row_at(high, rows, 0)
     for m in range(2 * members):
         ref = own_ref if m < members else partner_ref
-        out_ref[2 * m] = ref[m % members, first]
-        out_ref[2 * m + 1] = ref[m % members, first + 1]
+        out_ref[2 * m] = ref[m % members, edge]
+        out_ref[2 * m + 1] = ref[m % members, row_at(high, rows, 1)]
     out_ref[4 * members] = zonal_ref[edge]
     out_ref[4 * members + 1] = merid_ref[edge]
 
@@ -95,83 +100,126 @@
     )(own, partner, zonal, merid)
 
 
-def advance(south, middle, north, zonal, meridional):
+def advance(before, middle, after, zonal, inward):
     lon = middle.shape[-1]
     axis = middle.ndim - 1
     east = pltpu.roll(middle, lon - 1, axis)
     west = pltpu.roll(middle, 1, axis)
-    return middle - step_size * (
-        (zonal + middle) * (east - west) * 0.5 + meridional * (north - south) * 0.5
-    )
-
-
-def forecast_kernel(
-    bands,
-    crossed,
-    own_ref,
-    partner_ref,
-    halo_ref,
-    zonal_ref,
-    merid_ref,
-    dsum_ref,
-    vsum_ref,
-    *refs,
-):
-    out_refs, first_ref = refs[:-1], refs[-1]
+    change = (zonal + middle) * (east - west) + inward * (after - before)
+    return middle - (0.5 * step_size) * change
+
+
+def wind_row(high, rows, e, zonal_ref, merid_ref):
+    row = row_at(high, rows, e)
+    return zonal_ref[row], jnp.where(high, -merid_ref[row], merid_ref[row])
+
+
+def row_of(chip, t, crossed):
+    return lax.bitwise_xor(chip, t) if crossed else t
+
+
+def on(condition):
+    if isinstance(condition, bool):
+        return (lambda f: f()) if condition else (lambda f: None)
+    return pl.when(condition)
+
+
+def inner_kernel(bands, crossed, own_ref, partner_ref, zonal_ref, merid_ref, *refs):
+    first_ref, out_refs = refs[0], refs[1:]
     members, rows, levels, lon = own_ref.shape
     half = rows // 2
     chip, high, at_edge = place(bands)
-    base = jnp.where(high, half, 0)
+    wind = [wind_row(high, rows, e, zonal_ref, merid_ref) for e in range(1, half + 1)]
+    for m in range(2 * members):
+        ref, k = (own_ref if m < members else partner_ref), m % members
+        q = [ref[k, row_at(high, rows, e)] for e in range(half + 2)]
+        for e in range(1, half + 1):
+            first_ref[e - 1, m] = advance(q[e - 1], q[e], q[e + 1], *wind[e - 1])
+    for t, out_ref in enumerate(out_refs):
+        e = row_of(chip, t, crossed)
+
+        @on(e >= 2)
+        def _(e=e, out_ref=out_ref):
+            wind = wind_row(high, rows, e, zonal_ref, merid_ref)
+            for m in range(2 * members):
+                out_ref[m] = advance(
+                    first_ref[e - 2, m], first_ref[e - 1, m], first_ref[e, m], *wind
+                )
+
+
+def edge_kernel(bands, crossed, own_ref, partner_ref, halo_ref, zonal_ref, merid_ref, *refs):
+    members, rows, levels, lon = own_ref.shape
+    half = rows // 2
+    inner_ref, done_refs = refs[0], refs[1 : 1 + half]
+    out_refs, first_ref = refs[-1 - half : -1], refs[-1]
+    chip, high, at_edge = place(bands)
 
     def halo(i):
         return jnp.where(at_edge, 0.0, halo_ref[i])
 
-    def winds(ref, outside):
-        inside = [ref[base + r] for r in range(half)]
-        before = jnp.where(high, ref[half - 1], outside)
-        after = jnp.where(high, outside, ref[half])
-        return [before, *inside, after]
-
-    zonal = winds(zonal_ref, halo(4 * members))
-    merid = winds(merid_ref, halo(4 * members + 1))
+    merid = halo(4 * members + 1)
+    outside = halo(4 * members), jnp.where(high, -merid, merid)
+    edge = wind_row(high, rows, 0, zonal_ref, merid_ref)
     for m in range(2 * members):
         ref, k = (own_ref if m < members else partner_ref), m % members
-        outside = [halo(2 * m), halo(2 * m + 1)]
-        q = [jnp.where(high, ref[k, half - 2 + i], outside[i]) for i in range(2)]
-        q += [ref[k, base + r] for r in range(half)]
-        q += [jnp.where(high, outside[i], ref[k, half + i]) for i in range(2)]
-        for r in range(half + 2):
-            first_ref[r, m] = advance(q[r], q[r + 1], q[r + 2], zonal[r], merid[r])
-    for t in range(half):
-        r = row_of(chip, t, crossed)
-        zonal_row, merid_row = zonal_ref[base + r], merid_ref[base + r]
-        for m in range(2 * members):
-            out_refs[t][m] = advance(
-                first_ref[r, m], first_ref[r + 1, m], first_ref[r + 2, m], zonal_row, merid_row
-            )
-
-
-def row_of(chip, t, crossed):
-    return lax.bitwise_xor(chip, t) if crossed else t
-
-
-def forecast(bands, crossed, own, partner, halo, zonal, merid, dsum, vsum):
+        q = [halo(2 * m + 1), halo(2 * m)]
+        q += [ref[k, row_at(high, rows, e)] for e in range(2)]
+        first_ref[0, m] = advance(q[0], q[1], q[2], *outside)
+        first_ref[1, m] = advance(q[1], q[2], q[3], *edge)
+        first_ref[2, m] = inner_ref[0, m]
+        first_ref[3, m] = inner_ref[1, m]
+    for t, (done_ref, out_ref) in enumerate(zip(done_refs, out_refs)):
+        e = row_of(chip, t, crossed)
+
+        @on(e >= 2)
+        def _(done_ref=done_ref, out_ref=out_ref):
+            out_ref[...] = done_ref[...]
+
+        @on(e < 2)
+        def _(e=e, out_ref=out_ref):
+            wind = wind_row(high, rows, e, zonal_ref, merid_ref)
+            for m in range(2 * members):
+                out_ref[m] = advance(
+                    first_ref[e, m], first_ref[e + 1, m], first_ref[e + 2, m], *wind
+                )
+
+
+def forecast_inner(bands, crossed, own, partner, zonal, merid):
     members, rows, levels, lon = own.shape
     half = rows // 2
     size = own.size
-    shape = jax.ShapeDtypeStruct((2 * members, levels, lon), jnp.float32)
-    return pl.pallas_call(
-        functools.partial(forecast_kernel, bands, crossed),
-        out_shape=(shape,) * half,
-        in_specs=whole(5) + [pl.BlockSpec(memory_space=pl.ANY)] * 2,
+    block = (2 * members, levels, lon)
+    return pl.pallas_call(
+        functools.partial(inner_kernel, bands, crossed),
+        out_shape=(jax.ShapeDtypeStruct((half, *block), jnp.float32),)
+        + (jax.ShapeDtypeStruct(block, jnp.float32),) * half,
+        in_specs=whole(4),
+        out_specs=tuple(whole(half + 1)),
+        cost_estimate=pl.CostEstimate(
+            flops=16 * size, bytes_accessed=8 * size, transcendentals=0
+        ),
+        compiler_params=SMALL,
+        name="forecast_inner",
+    )(own, partner, zonal, merid)
+
+
+def forecast_edge(bands, crossed, own, partner, halo, zonal, merid, inner, sent, dsum, vsum):
+    members, rows, levels, lon = own.shape
+    half = rows // 2
+    size = own.size
+    block = (2 * members, levels, lon)
+    return pl.pallas_call(
+        functools.partial(edge_kernel, bands, crossed),
+        out_shape=(jax.ShapeDtypeStruct(block, jnp.float32),) * half,
+        in_specs=whole(6 + half) + [pl.BlockSpec(memory_space=pl.ANY)] * 2,
         out_specs=tuple(whole(half)),
-        scratch_shapes=[VM((half + 2, 2 * members, levels, lon), jnp.float32)],
+        scratch_shapes=[VM((4, *block), jnp.float32)],
         cost_estimate=pl.CostEstimate(
-            flops=24 * size, bytes_accessed=8 * size, transcendentals=0
+            flops=8 * size, bytes_accessed=4 * size, transcendentals=0
         ),
         compiler_params=SMALL,
-        name="forecast",
-    )(own, partner, halo, zonal, merid, dsum, vsum)
+        name="forecast_edge",
+    )(own, partner, halo, zonal, merid, inner, *sent, dsum, vsum)
 
 
 def cells_kernel(cell_ref, value_ref, weight_ref, dsum_ref, vsum_ref):
@@ -409,11 +457,11 @@
     got_refs, half_refs = refs[:half], refs[half : 2 * half]
     members = out_ref.shape[0]
     chip, high, at_edge = place(bands)
-    base = jnp.where(high, half, 0)
     copies = []
     for t, ref in enumerate(half_refs):
-        r = row_of(chip, t, crossed)
-        for source, row in ((ref.at[pl.ds(0, members)], base + r), (got_refs[t], half - base + r)):
+        mine = row_at(high, 2 * half, row_of(chip, t, crossed))
+        other = 2 * half - 1 - mine
+        for source, row in ((ref.at[pl.ds(0, members)], mine), (got_refs[t], other)):
             copies.append(
                 pltpu.make_async_copy(source, out_ref.at[:, row], sems.at[len(copies)])
             )
@@ -458,7 +506,10 @@
     halo = lax.ppermute(message, ("member", "lat"), halo_pairs(groups, bands))
 
     dsum, vsum = per_cell(*tables, lon)
-    sent = forecast(bands, crossed, own, partner, halo, zonal, merid, dsum, vsum)
+    inner, *sent = forecast_inner(bands, crossed, own, partner, zonal, merid)
+    sent = forecast_edge(
+        bands, crossed, own, partner, halo, zonal, merid, inner, sent, dsum, vsum
+    )
     same_core = [list(range(core, groups, 2)) for core in range(2)]
 
     def exchange(blocks):

time: 27.3 us -> 27.2 us (level)
  waiting for transfers between devices: 12.1 us -> 11.6 us
  Pallas kernels: 4.42 us -> 4.74 us
    ppermute x1, waiting for transfers between devices: 2.5 us -> 2.05 us  [body(): halo = lax.ppermute(message, ('member', 'lat'), halo_pairs(groups, bands))]
    pallas_call x1 -> x2, Pallas kernels: 0.49 us -> 0.81 us  [the longest x1 0.44 us: forecast_inner(): pl.pallas_call(functools.partial(inner_kernel, bands, crossed), out_shape...]
  transfers between devices with their start and end apart: 12 -> 12, of which waited for: 9 -> 9; matrix products, arithmetic and copies ran while one was open for 0% -> 0% of each run, Pallas kernels for 6% -> 8%
where the time goes in v8:
time: 27.2 us; the launch traced here: 27.1 us
  waiting for transfers between devices  11.6 us (43%)
  starting transfers between devices  10.6 us (39%)
  Pallas kernels  4.74 us (17%)
    ppermute x11, waiting for transfers between devices, swap(): return lax.ppermute(x, 'member', [(i, i ^ distance) for i in range(groups)])  9.58 us
    ppermute x11, starting transfers between devices, swap(): return lax.ppermute(x, 'member', [(i, i ^ distance) for i in range(groups)])  7.62 us
    ppermute x1, starting transfers between devices, body(): halo = lax.ppermute(message, ('member', 'lat'), halo_pairs(groups, bands))  3 us
    ppermute x1, waiting for transfers between devices, body(): halo = lax.ppermute(message, ('member', 'lat'), halo_pairs(groups, bands))  2.05 us
    pallas_call x1, Pallas kernels, analysis(): pl.pallas_call(kernel, out_shape=(jax.ShapeDtypeStruct((share, lon), jnp....  1.53 us
    pallas_call x1, Pallas kernels, stage(): pl.pallas_call(functools.partial(stage_kernel, bands), out_shape=tuple((j...  1.01 us
    pallas_call x1, Pallas kernels, place_rows(): pl.pallas_call(functools.partial(place_rows_kernel, bands, crossed), out_...  0.76 us
    pallas_call x1, Pallas kernels, per_cell(): pl.pallas_call(cells_kernel, out_shape=(shape, shape), in_specs=whole(3),...  0.63 us
  transfers between devices with their start and end apart: 12, of which 9 were waited for; matrix products, arithmetic and copies ran while one was open for 0% of the time, Pallas kernels for 8%

profile of v8, /device:TPU:0, one launch (start us, length us, event | category | flops | bytes accessed | tf_op | source)
XLA Modules:
  0.0 27.1 jit_solution(2225043365507500638)
XLA Ops:
  0.0 0.5 %collective-permute-start = (f32[4,8,8,256]{3,2,1,0:T(8,128)}, f32[4,8,8,256]{3,2,1,0:T(8,128)S(1)}, u32[]{:S(2)}, u32[]{:S(2)}) collective-permute-start(f32[4,8,8,256]{3,2,1,0:T(8,128)} %refs_0_.1), channel_id=1, source_target_pairs={{0,4},{4,0},{8,12},{12,8},{16,20},{20,16},{24,28},{28,24},{1,5},{5... | collective-permute-start | bytes 786440 | tf_op jit(solution)/shard_map/ppermute | solution.py:44
  0.5 1.0 %stage.1 = (f32[4,8,8,256]{3,2,1,0:T(8,128)S(1)}, f32[8,8,256]{2,1,0:T(8,128)S(1)}, f32[8,8,256]{2,1,0:T(8,128)S(1)}, s32[8,128]{1,0:T(8,128)S(1)}, f32[8,128]{1,0:T(8,128)S(1)}, /*index=5*/f32[8,128]{1,0:T(8,128)S(1)}) custom-call(f32[4,8,8,256]{3,2,1,0:T(8,128)} %refs_0_.1, f32[8,8,256]{2,1,0:T(8,128)} %refs_1_.1, f32[8,8,256]{2,1,0:T(8,128)} %refs_2_.1, ...), custom_call_target="tpu_custom_call" | custom-call | bytes 2097152 | tf_op jit(solution)/shard_map/stage/pallas_call | solution.py:67
  1.5 0.4 %collective-permute-done.partner_ref = f32[4,8,8,256]{3,2,1,0:T(8,128)S(1)} collective-permute-done((f32[4,8,8,256]{3,2,1,0:T(8,128)}, f32[4,8,8,256]{3,2,1,0:T(8,128)S(1)}, u32[]{:S(2)}, u32[]{:S(2)}) %collective-permute-start) | collective-permute-done | bytes 262176 | tf_op jit(solution)/shard_map/ppermute | solution.py:44
  1.9 3.0 %collective-permute-start.1 = (f32[18,8,256]{2,1,0:T(8,128)S(1)}, f32[18,8,256]{2,1,0:T(8,128)S(1)}, u32[]{:S(2)}, u32[]{:S(2)}) collective-permute-start(f32[18,8,256]{2,1,0:T(8,128)S(1)} %edges.1), channel_id=1, source_target_pairs={{0,1},{1,0},{2,3},{3,2},{4,12},{5,6},{6,5},{7,15},{8,9},{9,8},{10,... | collective-permute-start | bytes 442376 | tf_op jit(solution)/shard_map/ppermute | solution.py:506
  4.9 0.6 %per_cell.1 = (f32[8,256]{1,0:T(8,128)S(1)}, f32[8,256]{1,0:T(8,128)S(1)}) custom-call(s32[8,128]{1,0:T(8,128)S(1)} %get-tuple-element.34.cell_ref, f32[8,128]{1,0:T(8,128)S(1)} %get-tuple-element.35.value_ref, f32[8,128]{1,0:T(8,128)S(1)} %get-tuple-element.36.weight_ref), custom_call_target="tpu_custom_call" | custom-call | flops 1048576 | bytes 28672 | tf_op jit(solution)/shard_map/per_cell/pallas_call | solution.py:244
  5.5 0.4 %forecast_inner.1 = (f32[4,8,8,256]{3,2,1,0:T(8,128)S(1)}, f32[8,8,256]{2,1,0:T(8,128)S(1)}, f32[8,8,256]{2,1,0:T(8,128)S(1)}, f32[8,8,256]{2,1,0:T(8,128)S(1)}, f32[8,8,256]{2,1,0:T(8,128)S(1)}) custom-call(f32[4,8,8,256]{3,2,1,0:T(8,128)S(1)} %get-tuple-element.26.own_ref, f32[4,8,8,256]{3,2,1,0:T(8,128)S(1)} %collective-permute-done.partner_ref, ...), custom_call_target="tpu_custom_call" | custom-call | flops 1048576 | bytes 524288 | tf_op jit(solution)/shard_map/forecast_inner/pallas_call | solution.py:192
  6.0 2.0 %collective-permute-done.1.halo_ref = f32[18,8,256]{2,1,0:T(8,128)S(1)} collective-permute-done((f32[18,8,256]{2,1,0:T(8,128)S(1)}, f32[18,8,256]{2,1,0:T(8,128)S(1)}, u32[]{:S(2)}, u32[]{:S(2)}) %collective-permute-start.1) | collective-permute-done | bytes 147488 | tf_op jit(solution)/shard_map/ppermute | solution.py:506
  8.0 0.4 %forecast_edge.1 = (f32[8,8,256]{2,1,0:T(8,128)S(1)}, f32[8,8,256]{2,1,0:T(8,128)S(1)}, f32[8,8,256]{2,1,0:T(8,128)S(1)}, f32[8,8,256]{2,1,0:T(8,128)S(1)}) custom-call(f32[4,8,8,256]{3,2,1,0:T(8,128)S(1)} %get-tuple-element.26.own_ref, f32[4,8,8,256]{3,2,1,0:T(8,128)S(1)} %collective-permute-done.partner_ref, ...), custom_call_target="tpu_custom_call" | custom-call | flops 524288 | bytes 262144 | tf_op jit(solution)/shard_map/forecast_edge/pallas_call | solution.py:211
  8.4 2.0 %collective-permute-start.2 = (f32[8,8,256]{2,1,0:T(8,128)S(1)}, f32[8,8,256]{2,1,0:T(8,128)S(1)}, u32[]{:S(2)}, u32[]{:S(2)}) collective-permute-start(f32[8,8,256]{2,1,0:T(8,128)S(1)} %get-tuple-element.40), channel_id=1, source_target_pairs={{0,8},{4,12},{8,0},{12,4},{16,24},{20,28},{24,16},{28,20},{1,9},{5... | collective-permute-start | bytes 196616 | tf_op jit(solution)/shard_map/ppermute | solution.py:44
  10.4 1.5 %collective-permute-start.3 = (f32[8,8,256]{2,1,0:T(8,128)S(1)}, f32[8,8,256]{2,1,0:T(8,128)S(1)}, u32[]{:S(2)}, u32[]{:S(2)}) collective-permute-start(f32[8,8,256]{2,1,0:T(8,128)S(1)} %get-tuple-element.41), channel_id=1, source_target_pairs={{0,16},{4,20},{8,24},{12,28},{16,0},{20,4},{24,8},{28,12},{1,17},{... | collective-permute-start | bytes 196616 | tf_op jit(solution)/shard_map/ppermute | solution.py:44
  11.9 0.0 collective-permute-start.4
  11.9 0.8 %collective-permute-done.2 = f32[8,8,256]{2,1,0:T(8,128)S(1)} collective-permute-done((f32[8,8,256]{2,1,0:T(8,128)S(1)}, f32[8,8,256]{2,1,0:T(8,128)S(1)}, u32[]{:S(2)}, u32[]{:S(2)}) %collective-permute-start.2) | collective-permute-done | bytes 65568 | tf_op jit(solution)/shard_map/ppermute | solution.py:44
  12.7 2.6 %collective-permute-done.3 = f32[8,8,256]{2,1,0:T(8,128)S(1)} collective-permute-done((f32[8,8,256]{2,1,0:T(8,128)S(1)}, f32[8,8,256]{2,1,0:T(8,128)S(1)}, u32[]{:S(2)}, u32[]{:S(2)}) %collective-permute-start.3) | collective-permute-done | bytes 65568 | tf_op jit(solution)/shard_map/ppermute | solution.py:44
  15.4 1.7 %collective-permute-done.4 = f32[8,8,256]{2,1,0:T(8,128)S(1)} collective-permute-done((f32[8,8,256]{2,1,0:T(8,128)S(1)}, f32[8,8,256]{2,1,0:T(8,128)S(1)}, u32[]{:S(2)}, u32[]{:S(2)}) %collective-permute-start.4) | collective-permute-done | bytes 65568 | tf_op jit(solution)/shard_map/ppermute | solution.py:44
  17.1 1.5 %analysis.1 = (f32[64,256]{1,0:T(8,128)S(1)}, f32[64,256]{1,0:T(8,128)S(1)}, f32[64,256]{1,0:T(8,128)S(1)}, f32[64,256]{1,0:T(8,128)S(1)}) custom-call(f32[64,256]{1,0:T(8,128)S(1)} %bitcast.12, f32[64,256]{1,0:T(8,128)S(1)} %bitcast.14, f32[64,256]{1,0:T(8,128)S(1)} %bitcast.16, f32[64,256]{1,0:T(8,128)S(1)} %bitcast.17, ...), custom_call_target="tpu_custom_call" | custom-call | flops 805306368 | bytes 524288 | tf_op jit(solution)/shard_map/analysis/pallas_call | solution.py:441
  18.6 0.6 %collective-permute-start.8 = (f32[8,8,256]{2,1,0:T(8,128)S(1)}, f32[8,8,256]{2,1,0:T(8,128)S(1)}, u32[]{:S(2)}, u32[]{:S(2)}) collective-permute-start(f32[8,8,256]{2,1,0:T(8,128)S(1)} %bitcast.15), channel_id=1, source_target_pairs={{0,16},{4,20},{8,24},{12,28},{16,0},{20,4},{24,8},{28,12},{1,17},{... | collective-permute-start | bytes 196616 | tf_op jit(solution)/shard_map/ppermute | solution.py:44
  19.2 0.1 collective-permute-start.6
  19.3 2.9 %collective-permute-start.10 = (f32[8,8,256]{2,1,0:T(8,128)S(1)}, f32[8,8,256]{2,1,0:T(8,128)S(1)}, u32[]{:S(2)}, u32[]{:S(2)}) collective-permute-start(f32[8,8,256]{2,1,0:T(8,128)S(1)} %bitcast.11), channel_id=1, source_target_pairs={{0,24},{4,28},{8,16},{12,20},{16,8},{20,12},{24,0},{28,4},{1,25},{... | collective-permute-start | bytes 196616 | tf_op jit(solution)/shard_map/ppermute | solution.py:44
  22.2 0.0 collective-permute-start.5
  22.2 0.8 %collective-permute-done.8.refs_6_ = f32[8,8,256]{2,1,0:T(8,128)S(1)} collective-permute-done((f32[8,8,256]{2,1,0:T(8,128)S(1)}, f32[8,8,256]{2,1,0:T(8,128)S(1)}, u32[]{:S(2)}, u32[]{:S(2)}) %collective-permute-start.8) | collective-permute-done | bytes 65568 | tf_op jit(solution)/shard_map/ppermute | solution.py:44
  22.9 0.0 collective-permute-start.9
  22.9 0.5 %collective-permute-done.6.refs_5_ = f32[8,8,256]{2,1,0:T(8,128)S(1)} collective-permute-done((f32[8,8,256]{2,1,0:T(8,128)S(1)}, f32[8,8,256]{2,1,0:T(8,128)S(1)}, u32[]{:S(2)}, u32[]{:S(2)}) %collective-permute-start.6) | collective-permute-done | bytes 65568 | tf_op jit(solution)/shard_map/ppermute | solution.py:44
  23.4 0.0 collective-permute-start.7
  23.5 1.6 %collective-permute-done.10.refs_7_ = f32[8,8,256]{2,1,0:T(8,128)S(1)} collective-permute-done((f32[8,8,256]{2,1,0:T(8,128)S(1)}, f32[8,8,256]{2,1,0:T(8,128)S(1)}, u32[]{:S(2)}, u32[]{:S(2)}) %collective-permute-start.10) | collective-permute-done | bytes 65568 | tf_op jit(solution)/shard_map/ppermute | solution.py:44
  25.1 0.0 collective-permute-start.11
  25.1 0.0 collective-permute-done.5.refs_0_
  25.1 0.0 collective-permute-done.9.refs_2_
  25.1 0.0 collective-permute-done.7.refs_1_
  25.1 1.2 %collective-permute-done.11.refs_3_ = f32[4,8,256]{2,1,0:T(8,128)S(1)} collective-permute-done((f32[4,8,256]{2,1,0:T(8,128)S(1)}, f32[4,8,256]{2,1,0:T(8,128)S(1)}, u32[]{:S(2)}, u32[]{:S(2)}) %collective-permute-start.11) | collective-permute-done | bytes 32800 | tf_op jit(solution)/shard_map/ppermute | solution.py:44
  26.3 0.8 %place_rows.1 = f32[4,8,8,256]{3,2,1,0:T(8,128)} custom-call(f32[4,8,256]{2,1,0:T(8,128)S(1)} %collective-permute-done.5.refs_0_, f32[4,8,256]{2,1,0:T(8,128)S(1)} %collective-permute-done.7.refs_1_, f32[4,8,256]{2,1,0:T(8,128)S(1)} %collective-permute-done.9.refs_2_, f32[4,8,256]{2,1,0:T(8,128)S(1)} %collective-permute-done.11.refs_3_, ...), custom_call_target="tpu_custom_call" | custom-call | tf_op jit(solution)/shard_map/place_rows/pallas_call | solution.py:476
  (5 shorter events, 0.0 us)
Async XLA Ops:
  0.0 1.9 %collective-permute-start = (f32[4,8,8,256]{3,2,1,0:T(8,128)}, f32[4,8,8,256]{3,2,1,0:T(8,128)S(1)}, u32[]{:S(2)}, u32[]{:S(2)}) collective-permute-start(f32[4,8,8,256]{3,2,1,0:T(8,128)} %refs_0_.1), channel_id=1, source_target_pairs={{0,4},{4,0},{8,12},{12,8},{16,20},{20,16},{24,28},{28,24},{1,5},{5... | collective-permute-start | bytes 786440 | tf_op jit(solution)/shard_map/ppermute | solution.py:44
  1.9 6.1 %collective-permute-start.1 = (f32[18,8,256]{2,1,0:T(8,128)S(1)}, f32[18,8,256]{2,1,0:T(8,128)S(1)}, u32[]{:S(2)}, u32[]{:S(2)}) collective-permute-start(f32[18,8,256]{2,1,0:T(8,128)S(1)} %edges.1), channel_id=1, source_target_pairs={{0,1},{1,0},{2,3},{3,2},{4,12},{5,6},{6,5},{7,15},{8,9},{9,8},{10,... | collective-permute-start | bytes 442376 | tf_op jit(solution)/shard_map/ppermute | solution.py:506
  8.4 4.3 %collective-permute-start.2 = (f32[8,8,256]{2,1,0:T(8,128)S(1)}, f32[8,8,256]{2,1,0:T(8,128)S(1)}, u32[]{:S(2)}, u32[]{:S(2)}) collective-permute-start(f32[8,8,256]{2,1,0:T(8,128)S(1)} %get-tuple-element.40), channel_id=1, source_target_pairs={{0,8},{4,12},{8,0},{12,4},{16,24},{20,28},{24,16},{28,20},{1,9},{5... | collective-permute-start | bytes 196616 | tf_op jit(solution)/shard_map/ppermute | solution.py:44
  10.4 5.0 %collective-permute-start.3 = (f32[8,8,256]{2,1,0:T(8,128)S(1)}, f32[8,8,256]{2,1,0:T(8,128)S(1)}, u32[]{:S(2)}, u32[]{:S(2)}) collective-permute-start(f32[8,8,256]{2,1,0:T(8,128)S(1)} %get-tuple-element.41), channel_id=1, source_target_pairs={{0,16},{4,20},{8,24},{12,28},{16,0},{20,4},{24,8},{28,12},{1,17},{... | collective-permute-start | bytes 196616 | tf_op jit(solution)/shard_map/ppermute | solution.py:44
  11.9 5.2 %collective-permute-start.4 = (f32[8,8,256]{2,1,0:T(8,128)S(1)}, f32[8,8,256]{2,1,0:T(8,128)S(1)}, u32[]{:S(2)}, u32[]{:S(2)}) collective-permute-start(f32[8,8,256]{2,1,0:T(8,128)S(1)} %get-tuple-element.42), channel_id=1, source_target_pairs={{0,24},{4,28},{8,16},{12,20},{16,8},{20,12},{24,0},{28,4},{1,25},{... | collective-permute-start | bytes 196616 | tf_op jit(solution)/shard_map/ppermute | solution.py:44
  18.6 4.3 %collective-permute-start.8 = (f32[8,8,256]{2,1,0:T(8,128)S(1)}, f32[8,8,256]{2,1,0:T(8,128)S(1)}, u32[]{:S(2)}, u32[]{:S(2)}) collective-permute-start(f32[8,8,256]{2,1,0:T(8,128)S(1)} %bitcast.15), channel_id=1, source_target_pairs={{0,16},{4,20},{8,24},{12,28},{16,0},{20,4},{24,8},{28,12},{1,17},{... | collective-permute-start | bytes 196616 | tf_op jit(solution)/shard_map/ppermute | solution.py:44
  19.2 4.3 %collective-permute-start.6 = (f32[8,8,256]{2,1,0:T(8,128)S(1)}, f32[8,8,256]{2,1,0:T(8,128)S(1)}, u32[]{:S(2)}, u32[]{:S(2)}) collective-permute-start(f32[8,8,256]{2,1,0:T(8,128)S(1)} %bitcast.13), channel_id=1, source_target_pairs={{0,8},{4,12},{8,0},{12,4},{16,24},{20,28},{24,16},{28,20},{1,9},{5... | collective-permute-start | bytes 196616 | tf_op jit(solution)/shard_map/ppermute | solution.py:44
  19.3 5.8 %collective-permute-start.10 = (f32[8,8,256]{2,1,0:T(8,128)S(1)}, f32[8,8,256]{2,1,0:T(8,128)S(1)}, u32[]{:S(2)}, u32[]{:S(2)}) collective-permute-start(f32[8,8,256]{2,1,0:T(8,128)S(1)} %bitcast.11), channel_id=1, source_target_pairs={{0,24},{4,28},{8,16},{12,20},{16,8},{20,12},{24,0},{28,4},{1,25},{... | collective-permute-start | bytes 196616 | tf_op jit(solution)/shard_map/ppermute | solution.py:44
  22.2 2.9 %collective-permute-start.5 = (f32[4,8,256]{2,1,0:T(8,128)S(1)}, f32[4,8,256]{2,1,0:T(8,128)S(1)}, u32[]{:S(2)}, u32[]{:S(2)}) collective-permute-start(f32[4,8,256]{2,1,0:T(8,128)S(1)} %slice_bitcast_fusion), channel_id=1, source_target_pairs={{0,4},{4,0},{8,12},{12,8},{16,20},{20,16},{24,28},{28,24},{1,5},{5... | collective-permute-start | bytes 98312 | tf_op jit(solution)/shard_map/ppermute | solution.py:44
  22.9 2.2 %collective-permute-start.9 = (f32[4,8,256]{2,1,0:T(8,128)S(1)}, f32[4,8,256]{2,1,0:T(8,128)S(1)}, u32[]{:S(2)}, u32[]{:S(2)}) collective-permute-start(f32[4,8,256]{2,1,0:T(8,128)S(1)} %slice.21), channel_id=1, source_target_pairs={{0,4},{4,0},{8,12},{12,8},{16,20},{20,16},{24,28},{28,24},{1,5},{5... | collective-permute-start | bytes 98312 | tf_op jit(solution)/shard_map/ppermute | solution.py:44
  23.4 1.7 %collective-permute-start.7 = (f32[4,8,256]{2,1,0:T(8,128)S(1)}, f32[4,8,256]{2,1,0:T(8,128)S(1)}, u32[]{:S(2)}, u32[]{:S(2)}) collective-permute-start(f32[4,8,256]{2,1,0:T(8,128)S(1)} %slice.20), channel_id=1, source_target_pairs={{0,4},{4,0},{8,12},{12,8},{16,20},{20,16},{24,28},{28,24},{1,5},{5... | collective-permute-start | bytes 98312 | tf_op jit(solution)/shard_map/ppermute | solution.py:44
  25.1 1.2 %collective-permute-start.11 = (f32[4,8,256]{2,1,0:T(8,128)S(1)}, f32[4,8,256]{2,1,0:T(8,128)S(1)}, u32[]{:S(2)}, u32[]{:S(2)}) collective-permute-start(f32[4,8,256]{2,1,0:T(8,128)S(1)} %slice.22), channel_id=1, source_target_pairs={{0,4},{4,0},{8,12},{12,8},{16,20},{20,16},{24,28},{28,24},{1,5},{5... | collective-permute-start | bytes 98312 | tf_op jit(solution)/shard_map/ppermute | solution.py:44

commit v9 on v8

--- a/solution.py
+++ b/solution.py
@@ -118,14 +118,7 @@
     return lax.bitwise_xor(chip, t) if crossed else t
 
 
-def on(condition):
-    if isinstance(condition, bool):
-        return (lambda f: f()) if condition else (lambda f: None)
-    return pl.when(condition)
-
-
-def inner_kernel(bands, crossed, own_ref, partner_ref, zonal_ref, merid_ref, *refs):
-    first_ref, out_refs = refs[0], refs[1:]
+def inner_kernel(bands, own_ref, partner_ref, zonal_ref, merid_ref, first_ref, done_ref):
     members, rows, levels, lon = own_ref.shape
     half = rows // 2
     chip, high, at_edge = place(bands)
@@ -135,23 +128,31 @@
         q = [ref[k, row_at(high, rows, e)] for e in range(half + 2)]
         for e in range(1, half + 1):
             first_ref[e - 1, m] = advance(q[e - 1], q[e], q[e + 1], *wind[e - 1])
-    for t, out_ref in enumerate(out_refs):
-        e = row_of(chip, t, crossed)
-
-        @on(e >= 2)
-        def _(e=e, out_ref=out_ref):
-            wind = wind_row(high, rows, e, zonal_ref, merid_ref)
-            for m in range(2 * members):
-                out_ref[m] = advance(
-                    first_ref[e - 2, m], first_ref[e - 1, m], first_ref[e, m], *wind
-                )
-
-
-def edge_kernel(bands, crossed, own_ref, partner_ref, halo_ref, zonal_ref, merid_ref, *refs):
+    for e in range(2, half):
+        wind = wind_row(high, rows, e, zonal_ref, merid_ref)
+        for m in range(2 * members):
+            done_ref[e - 2, m] = advance(
+                first_ref[e - 2, m], first_ref[e - 1, m], first_ref[e, m], *wind
+            )
+
+
+def edge_kernel(
+    bands,
+    crossed,
+    own_ref,
+    partner_ref,
+    halo_ref,
+    zonal_ref,
+    merid_ref,
+    inner_ref,
+    done_ref,
+    dsum_ref,
+    vsum_ref,
+    *refs,
+):
     members, rows, levels, lon = own_ref.shape
     half = rows // 2
-    inner_ref, done_refs = refs[0], refs[1 : 1 + half]
-    out_refs, first_ref = refs[-1 - half : -1], refs[-1]
+    out_refs, edge_ref = refs[:half], refs[half]
     chip, high, at_edge = place(bands)
 
     def halo(i):
@@ -159,42 +160,41 @@
 
     merid = halo(4 * members + 1)
     outside = halo(4 * members), jnp.where(high, -merid, merid)
-    edge = wind_row(high, rows, 0, zonal_ref, merid_ref)
+    wind = [wind_row(high, rows, e, zonal_ref, merid_ref) for e in range(2)]
     for m in range(2 * members):
         ref, k = (own_ref if m < members else partner_ref), m % members
         q = [halo(2 * m + 1), halo(2 * m)]
         q += [ref[k, row_at(high, rows, e)] for e in range(2)]
-        first_ref[0, m] = advance(q[0], q[1], q[2], *outside)
-        first_ref[1, m] = advance(q[1], q[2], q[3], *edge)
-        first_ref[2, m] = inner_ref[0, m]
-        first_ref[3, m] = inner_ref[1, m]
-    for t, (done_ref, out_ref) in enumerate(zip(done_refs, out_refs)):
+        first = [
+            advance(q[0], q[1], q[2], *outside),
+            advance(q[1], q[2], q[3], *wind[0]),
+            inner_ref[0, m],
+            inner_ref[1, m],
+        ]
+        for e in range(2):
+            edge_ref[e, m] = advance(first[e], first[e + 1], first[e + 2], *wind[e])
+    for t, out_ref in enumerate(out_refs):
         e = row_of(chip, t, crossed)
-
-        @on(e >= 2)
-        def _(done_ref=done_ref, out_ref=out_ref):
-            out_ref[...] = done_ref[...]
-
-        @on(e < 2)
-        def _(e=e, out_ref=out_ref):
-            wind = wind_row(high, rows, e, zonal_ref, merid_ref)
-            for m in range(2 * members):
-                out_ref[m] = advance(
-                    first_ref[e, m], first_ref[e + 1, m], first_ref[e + 2, m], *wind
-                )
-
-
-def forecast_inner(bands, crossed, own, partner, zonal, merid):
+        if not crossed:
+            out_ref[...] = edge_ref[e] if e < 2 else done_ref[e - 2]
+            continue
+        near, far = jnp.minimum(e, 1), jnp.maximum(e - 2, 0)
+        for m in range(2 * members):
+            out_ref[m] = jnp.where(e < 2, edge_ref[near, m], done_ref[far, m])
+
+
+def forecast_inner(bands, own, partner, zonal, merid):
     members, rows, levels, lon = own.shape
     half = rows // 2
     size = own.size
     block = (2 * members, levels, lon)
     return pl.pallas_call(
-        functools.partial(inner_kernel, bands, crossed),
-        out_shape=(jax.ShapeDtypeStruct((half, *block), jnp.float32),)
-        + (jax.ShapeDtypeStruct(block, jnp.float32),) * half,
+        functools.partial(inner_kernel, bands),
+        out_shape=tuple(
+            jax.ShapeDtypeStruct((n, *block), jnp.float32) for n in (half, half - 2)
+        ),
         in_specs=whole(4),
-        out_specs=tuple(whole(half + 1)),
+        out_specs=tuple(whole(2)),
         cost_estimate=pl.CostEstimate(
             flops=16 * size, bytes_accessed=8 * size, transcendentals=0
         ),
@@ -203,7 +203,7 @@
     )(own, partner, zonal, merid)
 
 
-def forecast_edge(bands, crossed, own, partner, halo, zonal, merid, inner, sent, dsum, vsum):
+def forecast_edge(bands, crossed, own, partner, halo, zonal, merid, inner, done, dsum, vsum):
     members, rows, levels, lon = own.shape
     half = rows // 2
     size = own.size
@@ -211,15 +211,15 @@
     return pl.pallas_call(
         functools.partial(edge_kernel, bands, crossed),
         out_shape=(jax.ShapeDtypeStruct(block, jnp.float32),) * half,
-        in_specs=whole(6 + half) + [pl.BlockSpec(memory_space=pl.ANY)] * 2,
+        in_specs=whole(7) + [pl.BlockSpec(memory_space=pl.ANY)] * 2,
         out_specs=tuple(whole(half)),
-        scratch_shapes=[VM((4, *block), jnp.float32)],
+        scratch_shapes=[VM((2, *block), jnp.float32)],
         cost_estimate=pl.CostEstimate(
             flops=8 * size, bytes_accessed=4 * size, transcendentals=0
         ),
         compiler_params=SMALL,
         name="forecast_edge",
-    )(own, partner, halo, zonal, merid, inner, *sent, dsum, vsum)
+    )(own, partner, halo, zonal, merid, inner, done, dsum, vsum)
 
 
 def cells_kernel(cell_ref, value_ref, weight_ref, dsum_ref, vsum_ref):
@@ -391,27 +391,27 @@
         more = lax.dot_general(w_low, high, nt, preferred_element_type=jnp.float32)
         gram = main[:, :size] + main[:, size:] + more
         system = jnp.where(same, gram, 0.0) + (count - 1.0) * one
-        squares = jnp.sum(system * system, axis=1, keepdims=True)
-        frob = jnp.sqrt(over_members(jnp.broadcast_to(squares, (size, size))))
-        return system * spread(1.0 / frob), frob, jnp.concatenate([high, rest], axis=1)
+        system_s = halves(system)
+        square = folded_product(system_s, system_s)
+        total = jnp.sum(system * system, axis=1, keepdims=True)
+        frob = jnp.sqrt(over_members(jnp.broadcast_to(total, (size, size))))
+        scale = spread(1.0 / frob)
+        iterate = system * scale
+        first = 1.5 * iterate - (0.5 * scale) * (square * scale)
+        return iterate, first, frob, jnp.concatenate([high, rest], axis=1)
 
     begun = [start(x, d) for x, d in zip(groups, dsums)]
-    frobs = [b[1] for b in begun]
-    perts = [b[2] for b in begun]
-    steps = [b[0] for b in begun]
-    iterates = [halves(x) for x in steps]
-    inverses = None
-    for sweep in range(SWEEPS):
-        if inverses is not None:
-            steps = [folded_product(z, y) for z, y in zip(inverses, iterates)]
+    frobs = [b[2] for b in begun]
+    perts = [b[3] for b in begun]
+    inverses = [halves(1.5 * one - 0.5 * b[0]) for b in begun]
+    iterates = [halves(b[1]) for b in begun]
+    for sweep in range(1, SWEEPS):
+        steps = [folded_product(y, z) for z, y in zip(inverses, iterates)]
         factors = [halves(1.5 * one - 0.5 * x) for x in steps]
         if sweep == SWEEPS - 1:
             break
-        iterates = [halves(folded_product(y, f)) for y, f in zip(iterates, factors)]
-        if inverses is None:
-            inverses = factors
-        else:
-            inverses = [halves(folded_product(f, z)) for f, z in zip(factors, inverses)]
+        iterates = [halves(folded_product(f, y)) for y, f in zip(iterates, factors)]
+        inverses = [halves(folded_product(f, z)) for f, z in zip(factors, inverses)]
     partials = [halves(folded_product(z, x)) for z, x in zip(inverses, perts)]
     results = []
     for factor, part, frob, pull, mean_g in zip(factors, partials, frobs, pulls, means):
@@ -506,9 +506,9 @@
     halo = lax.ppermute(message, ("member", "lat"), halo_pairs(groups, bands))
 
     dsum, vsum = per_cell(*tables, lon)
-    inner, *sent = forecast_inner(bands, crossed, own, partner, zonal, merid)
+    inner, done = forecast_inner(bands, own, partner, zonal, merid)
     sent = forecast_edge(
-        bands, crossed, own, partner, halo, zonal, merid, inner, sent, dsum, vsum
+        bands, crossed, own, partner, halo, zonal, merid, inner, done, dsum, vsum
     )
     same_core = [list(range(core, groups, 2)) for core in range(2)]
 

time: 27.2 us -> 27.1 us (level)
  transfers between devices with their start and end apart: 12 -> 12, of which waited for: 9 -> 9; matrix products, arithmetic and copies ran while one was open for 0% -> 0% of each run, Pallas kernels for 8% -> 7%
where the time goes in v9:
time: 27.1 us; the launch traced here: 27 us
  waiting for transfers between devices  11.8 us (44%)
  starting transfers between devices  10.6 us (39%)
  Pallas kernels  4.52 us (17%)
    ppermute x11, waiting for transfers between devices, swap(): return lax.ppermute(x, 'member', [(i, i ^ distance) for i in range(groups)])  9.58 us
    ppermute x11, starting transfers between devices, swap(): return lax.ppermute(x, 'member', [(i, i ^ distance) for i in range(groups)])  7.62 us
    ppermute x1, starting transfers between devices, body(): halo = lax.ppermute(message, ('member', 'lat'), halo_pairs(groups, bands))  3 us
    ppermute x1, waiting for transfers between devices, body(): halo = lax.ppermute(message, ('member', 'lat'), halo_pairs(groups, bands))  2.17 us
    pallas_call x1, Pallas kernels, analysis(): pl.pallas_call(kernel, out_shape=(jax.ShapeDtypeStruct((share, lon), jnp....  1.53 us
    pallas_call x1, Pallas kernels, stage(): pl.pallas_call(functools.partial(stage_kernel, bands), out_shape=tuple((j...  1.01 us
    pallas_call x1, Pallas kernels, place_rows(): pl.pallas_call(functools.partial(place_rows_kernel, bands, crossed), out_...  0.76 us
    pallas_call x1, Pallas kernels, per_cell(): pl.pallas_call(cells_kernel, out_shape=(shape, shape), in_specs=whole(3),...  0.63 us
  transfers between devices with their start and end apart: 12, of which 9 were waited for; matrix products, arithmetic and copies ran while one was open for 0% of the time, Pallas kernels for 7%

profile of v9, /device:TPU:0, one launch (start us, length us, event | category | flops | bytes accessed | tf_op | source)
XLA Modules:
  0.0 27.0 jit_solution(6275901503572719239)
XLA Ops:
  0.0 0.5 %collective-permute-start = (f32[4,8,8,256]{3,2,1,0:T(8,128)}, f32[4,8,8,256]{3,2,1,0:T(8,128)S(1)}, u32[]{:S(2)}, u32[]{:S(2)}) collective-permute-start(f32[4,8,8,256]{3,2,1,0:T(8,128)} %refs_0_.1), channel_id=1, source_target_pairs={{0,4},{4,0},{8,12},{12,8},{16,20},{20,16},{24,28},{28,24},{1,5},{5... | collective-permute-start | bytes 786440 | tf_op jit(solution)/shard_map/ppermute | solution.py:44
  0.5 1.0 %stage.1 = (f32[4,8,8,256]{3,2,1,0:T(8,128)S(1)}, f32[8,8,256]{2,1,0:T(8,128)S(1)}, f32[8,8,256]{2,1,0:T(8,128)S(1)}, s32[8,128]{1,0:T(8,128)S(1)}, f32[8,128]{1,0:T(8,128)S(1)}, /*index=5*/f32[8,128]{1,0:T(8,128)S(1)}) custom-call(f32[4,8,8,256]{3,2,1,0:T(8,128)} %refs_0_.1, f32[8,8,256]{2,1,0:T(8,128)} %refs_1_.1, f32[8,8,256]{2,1,0:T(8,128)} %refs_2_.1, ...), custom_call_target="tpu_custom_call" | custom-call | bytes 2097152 | tf_op jit(solution)/shard_map/stage/pallas_call | solution.py:67
  1.5 0.4 %collective-permute-done.partner_ref = f32[4,8,8,256]{3,2,1,0:T(8,128)S(1)} collective-permute-done((f32[4,8,8,256]{3,2,1,0:T(8,128)}, f32[4,8,8,256]{3,2,1,0:T(8,128)S(1)}, u32[]{:S(2)}, u32[]{:S(2)}) %collective-permute-start) | collective-permute-done | bytes 262176 | tf_op jit(solution)/shard_map/ppermute | solution.py:44
  1.9 3.0 %collective-permute-start.1 = (f32[18,8,256]{2,1,0:T(8,128)S(1)}, f32[18,8,256]{2,1,0:T(8,128)S(1)}, u32[]{:S(2)}, u32[]{:S(2)}) collective-permute-start(f32[18,8,256]{2,1,0:T(8,128)S(1)} %edges.1), channel_id=1, source_target_pairs={{0,1},{1,0},{2,3},{3,2},{4,12},{5,6},{6,5},{7,15},{8,9},{9,8},{10,... | collective-permute-start | bytes 442376 | tf_op jit(solution)/shard_map/ppermute | solution.py:506
  4.9 0.6 %per_cell.1 = (f32[8,256]{1,0:T(8,128)S(1)}, f32[8,256]{1,0:T(8,128)S(1)}) custom-call(s32[8,128]{1,0:T(8,128)S(1)} %get-tuple-element.28.cell_ref, f32[8,128]{1,0:T(8,128)S(1)} %get-tuple-element.29.value_ref, f32[8,128]{1,0:T(8,128)S(1)} %get-tuple-element.30.weight_ref), custom_call_target="tpu_custom_call" | custom-call | flops 1048576 | bytes 28672 | tf_op jit(solution)/shard_map/per_cell/pallas_call | solution.py:244
  5.5 0.3 %forecast_inner.1 = (f32[4,8,8,256]{3,2,1,0:T(8,128)S(1)}, f32[2,8,8,256]{3,2,1,0:T(8,128)S(1)}) custom-call(f32[4,8,8,256]{3,2,1,0:T(8,128)S(1)} %get-tuple-element.23.own_ref, f32[4,8,8,256]{3,2,1,0:T(8,128)S(1)} %collective-permute-done.partner_ref, f32[8,8,256]{2,1,0:T(8,128)S(1)} %get-tuple-element.24.zonal_ref, ...), custom_call_target="tpu_custom_call" | custom-call | flops 1048576 | bytes 524288 | tf_op jit(solution)/shard_map/forecast_inner/pallas_call | solution.py:191
  5.8 2.2 %collective-permute-done.1.halo_ref = f32[18,8,256]{2,1,0:T(8,128)S(1)} collective-permute-done((f32[18,8,256]{2,1,0:T(8,128)S(1)}, f32[18,8,256]{2,1,0:T(8,128)S(1)}, u32[]{:S(2)}, u32[]{:S(2)}) %collective-permute-start.1) | collective-permute-done | bytes 147488 | tf_op jit(solution)/shard_map/ppermute | solution.py:506
  8.0 0.3 forecast_edge.1
  8.3 2.0 %collective-permute-start.2 = (f32[8,8,256]{2,1,0:T(8,128)S(1)}, f32[8,8,256]{2,1,0:T(8,128)S(1)}, u32[]{:S(2)}, u32[]{:S(2)}) collective-permute-start(f32[8,8,256]{2,1,0:T(8,128)S(1)} %get-tuple-element.34), channel_id=1, source_target_pairs={{0,8},{4,12},{8,0},{12,4},{16,24},{20,28},{24,16},{28,20},{1,9},{5... | collective-permute-start | bytes 196616 | tf_op jit(solution)/shard_map/ppermute | solution.py:44
  10.3 1.5 %collective-permute-start.3 = (f32[8,8,256]{2,1,0:T(8,128)S(1)}, f32[8,8,256]{2,1,0:T(8,128)S(1)}, u32[]{:S(2)}, u32[]{:S(2)}) collective-permute-start(f32[8,8,256]{2,1,0:T(8,128)S(1)} %get-tuple-element.35), channel_id=1, source_target_pairs={{0,16},{4,20},{8,24},{12,28},{16,0},{20,4},{24,8},{28,12},{1,17},{... | collective-permute-start | bytes 196616 | tf_op jit(solution)/shard_map/ppermute | solution.py:44
  11.8 0.0 collective-permute-start.4
  11.8 0.8 %collective-permute-done.2 = f32[8,8,256]{2,1,0:T(8,128)S(1)} collective-permute-done((f32[8,8,256]{2,1,0:T(8,128)S(1)}, f32[8,8,256]{2,1,0:T(8,128)S(1)}, u32[]{:S(2)}, u32[]{:S(2)}) %collective-permute-start.2) | collective-permute-done | bytes 65568 | tf_op jit(solution)/shard_map/ppermute | solution.py:44
  12.6 2.6 %collective-permute-done.3 = f32[8,8,256]{2,1,0:T(8,128)S(1)} collective-permute-done((f32[8,8,256]{2,1,0:T(8,128)S(1)}, f32[8,8,256]{2,1,0:T(8,128)S(1)}, u32[]{:S(2)}, u32[]{:S(2)}) %collective-permute-start.3) | collective-permute-done | bytes 65568 | tf_op jit(solution)/shard_map/ppermute | solution.py:44
  15.2 1.7 %collective-permute-done.4 = f32[8,8,256]{2,1,0:T(8,128)S(1)} collective-permute-done((f32[8,8,256]{2,1,0:T(8,128)S(1)}, f32[8,8,256]{2,1,0:T(8,128)S(1)}, u32[]{:S(2)}, u32[]{:S(2)}) %collective-permute-start.4) | collective-permute-done | bytes 65568 | tf_op jit(solution)/shard_map/ppermute | solution.py:44
  17.0 1.5 %analysis.1 = (f32[64,256]{1,0:T(8,128)S(1)}, f32[64,256]{1,0:T(8,128)S(1)}, f32[64,256]{1,0:T(8,128)S(1)}, f32[64,256]{1,0:T(8,128)S(1)}) custom-call(f32[64,256]{1,0:T(8,128)S(1)} %bitcast.12, f32[64,256]{1,0:T(8,128)S(1)} %bitcast.14, f32[64,256]{1,0:T(8,128)S(1)} %bitcast.16, f32[64,256]{1,0:T(8,128)S(1)} %bitcast.17, ...), custom_call_target="tpu_custom_call" | custom-call | flops 805306368 | bytes 524288 | tf_op jit(solution)/shard_map/analysis/pallas_call | solution.py:441
  18.5 0.6 %collective-permute-start.8 = (f32[8,8,256]{2,1,0:T(8,128)S(1)}, f32[8,8,256]{2,1,0:T(8,128)S(1)}, u32[]{:S(2)}, u32[]{:S(2)}) collective-permute-start(f32[8,8,256]{2,1,0:T(8,128)S(1)} %bitcast.15), channel_id=1, source_target_pairs={{0,16},{4,20},{8,24},{12,28},{16,0},{20,4},{24,8},{28,12},{1,17},{... | collective-permute-start | bytes 196616 | tf_op jit(solution)/shard_map/ppermute | solution.py:44
  19.1 0.1 collective-permute-start.6
  19.2 2.9 %collective-permute-start.10 = (f32[8,8,256]{2,1,0:T(8,128)S(1)}, f32[8,8,256]{2,1,0:T(8,128)S(1)}, u32[]{:S(2)}, u32[]{:S(2)}) collective-permute-start(f32[8,8,256]{2,1,0:T(8,128)S(1)} %bitcast.11), channel_id=1, source_target_pairs={{0,24},{4,28},{8,16},{12,20},{16,8},{20,12},{24,0},{28,4},{1,25},{... | collective-permute-start | bytes 196616 | tf_op jit(solution)/shard_map/ppermute | solution.py:44
  22.1 0.0 collective-permute-start.5
  22.1 0.8 %collective-permute-done.8.refs_6_ = f32[8,8,256]{2,1,0:T(8,128)S(1)} collective-permute-done((f32[8,8,256]{2,1,0:T(8,128)S(1)}, f32[8,8,256]{2,1,0:T(8,128)S(1)}, u32[]{:S(2)}, u32[]{:S(2)}) %collective-permute-start.8) | collective-permute-done | bytes 65568 | tf_op jit(solution)/shard_map/ppermute | solution.py:44
  22.8 0.0 collective-permute-start.9
  22.8 0.5 %collective-permute-done.6.refs_5_ = f32[8,8,256]{2,1,0:T(8,128)S(1)} collective-permute-done((f32[8,8,256]{2,1,0:T(8,128)S(1)}, f32[8,8,256]{2,1,0:T(8,128)S(1)}, u32[]{:S(2)}, u32[]{:S(2)}) %collective-permute-start.6) | collective-permute-done | bytes 65568 | tf_op jit(solution)/shard_map/ppermute | solution.py:44
  23.3 0.0 collective-permute-start.7
  23.3 1.6 %collective-permute-done.10.refs_7_ = f32[8,8,256]{2,1,0:T(8,128)S(1)} collective-permute-done((f32[8,8,256]{2,1,0:T(8,128)S(1)}, f32[8,8,256]{2,1,0:T(8,128)S(1)}, u32[]{:S(2)}, u32[]{:S(2)}) %collective-permute-start.10) | collective-permute-done | bytes 65568 | tf_op jit(solution)/shard_map/ppermute | solution.py:44
  25.0 0.0 collective-permute-start.11
  25.0 0.0 collective-permute-done.5.refs_0_
  25.0 0.0 collective-permute-done.9.refs_2_
  25.0 0.0 collective-permute-done.7.refs_1_
  25.0 1.2 %collective-permute-done.11.refs_3_ = f32[4,8,256]{2,1,0:T(8,128)S(1)} collective-permute-done((f32[4,8,256]{2,1,0:T(8,128)S(1)}, f32[4,8,256]{2,1,0:T(8,128)S(1)}, u32[]{:S(2)}, u32[]{:S(2)}) %collective-permute-start.11) | collective-permute-done | bytes 32800 | tf_op jit(solution)/shard_map/ppermute | solution.py:44
  26.2 0.8 %place_rows.1 = f32[4,8,8,256]{3,2,1,0:T(8,128)} custom-call(f32[4,8,256]{2,1,0:T(8,128)S(1)} %collective-permute-done.5.refs_0_, f32[4,8,256]{2,1,0:T(8,128)S(1)} %collective-permute-done.7.refs_1_, f32[4,8,256]{2,1,0:T(8,128)S(1)} %collective-permute-done.9.refs_2_, f32[4,8,256]{2,1,0:T(8,128)S(1)} %collective-permute-done.11.refs_3_, ...), custom_call_target="tpu_custom_call" | custom-call | tf_op jit(solution)/shard_map/place_rows/pallas_call | solution.py:476
  (5 shorter events, 0.0 us)
Async XLA Ops:
  0.0 1.9 %collective-permute-start = (f32[4,8,8,256]{3,2,1,0:T(8,128)}, f32[4,8,8,256]{3,2,1,0:T(8,128)S(1)}, u32[]{:S(2)}, u32[]{:S(2)}) collective-permute-start(f32[4,8,8,256]{3,2,1,0:T(8,128)} %refs_0_.1), channel_id=1, source_target_pairs={{0,4},{4,0},{8,12},{12,8},{16,20},{20,16},{24,28},{28,24},{1,5},{5... | collective-permute-start | bytes 786440 | tf_op jit(solution)/shard_map/ppermute | solution.py:44
  1.9 6.1 %collective-permute-start.1 = (f32[18,8,256]{2,1,0:T(8,128)S(1)}, f32[18,8,256]{2,1,0:T(8,128)S(1)}, u32[]{:S(2)}, u32[]{:S(2)}) collective-permute-start(f32[18,8,256]{2,1,0:T(8,128)S(1)} %edges.1), channel_id=1, source_target_pairs={{0,1},{1,0},{2,3},{3,2},{4,12},{5,6},{6,5},{7,15},{8,9},{9,8},{10,... | collective-permute-start | bytes 442376 | tf_op jit(solution)/shard_map/ppermute | solution.py:506
  8.3 4.3 %collective-permute-start.2 = (f32[8,8,256]{2,1,0:T(8,128)S(1)}, f32[8,8,256]{2,1,0:T(8,128)S(1)}, u32[]{:S(2)}, u32[]{:S(2)}) collective-permute-start(f32[8,8,256]{2,1,0:T(8,128)S(1)} %get-tuple-element.34), channel_id=1, source_target_pairs={{0,8},{4,12},{8,0},{12,4},{16,24},{20,28},{24,16},{28,20},{1,9},{5... | collective-permute-start | bytes 196616 | tf_op jit(solution)/shard_map/ppermute | solution.py:44
  10.3 5.0 %collective-permute-start.3 = (f32[8,8,256]{2,1,0:T(8,128)S(1)}, f32[8,8,256]{2,1,0:T(8,128)S(1)}, u32[]{:S(2)}, u32[]{:S(2)}) collective-permute-start(f32[8,8,256]{2,1,0:T(8,128)S(1)} %get-tuple-element.35), channel_id=1, source_target_pairs={{0,16},{4,20},{8,24},{12,28},{16,0},{20,4},{24,8},{28,12},{1,17},{... | collective-permute-start | bytes 196616 | tf_op jit(solution)/shard_map/ppermute | solution.py:44
  11.8 5.2 %collective-permute-start.4 = (f32[8,8,256]{2,1,0:T(8,128)S(1)}, f32[8,8,256]{2,1,0:T(8,128)S(1)}, u32[]{:S(2)}, u32[]{:S(2)}) collective-permute-start(f32[8,8,256]{2,1,0:T(8,128)S(1)} %get-tuple-element.36), channel_id=1, source_target_pairs={{0,24},{4,28},{8,16},{12,20},{16,8},{20,12},{24,0},{28,4},{1,25},{... | collective-permute-start | bytes 196616 | tf_op jit(solution)/shard_map/ppermute | solution.py:44
  18.5 4.3 %collective-permute-start.8 = (f32[8,8,256]{2,1,0:T(8,128)S(1)}, f32[8,8,256]{2,1,0:T(8,128)S(1)}, u32[]{:S(2)}, u32[]{:S(2)}) collective-permute-start(f32[8,8,256]{2,1,0:T(8,128)S(1)} %bitcast.15), channel_id=1, source_target_pairs={{0,16},{4,20},{8,24},{12,28},{16,0},{20,4},{24,8},{28,12},{1,17},{... | collective-permute-start | bytes 196616 | tf_op jit(solution)/shard_map/ppermute | solution.py:44
  19.1 4.3 %collective-permute-start.6 = (f32[8,8,256]{2,1,0:T(8,128)S(1)}, f32[8,8,256]{2,1,0:T(8,128)S(1)}, u32[]{:S(2)}, u32[]{:S(2)}) collective-permute-start(f32[8,8,256]{2,1,0:T(8,128)S(1)} %bitcast.13), channel_id=1, source_target_pairs={{0,8},{4,12},{8,0},{12,4},{16,24},{20,28},{24,16},{28,20},{1,9},{5... | collective-permute-start | bytes 196616 | tf_op jit(solution)/shard_map/ppermute | solution.py:44
  19.2 5.8 %collective-permute-start.10 = (f32[8,8,256]{2,1,0:T(8,128)S(1)}, f32[8,8,256]{2,1,0:T(8,128)S(1)}, u32[]{:S(2)}, u32[]{:S(2)}) collective-permute-start(f32[8,8,256]{2,1,0:T(8,128)S(1)} %bitcast.11), channel_id=1, source_target_pairs={{0,24},{4,28},{8,16},{12,20},{16,8},{20,12},{24,0},{28,4},{1,25},{... | collective-permute-start | bytes 196616 | tf_op jit(solution)/shard_map/ppermute | solution.py:44
  22.1 2.9 %collective-permute-start.5 = (f32[4,8,256]{2,1,0:T(8,128)S(1)}, f32[4,8,256]{2,1,0:T(8,128)S(1)}, u32[]{:S(2)}, u32[]{:S(2)}) collective-permute-start(f32[4,8,256]{2,1,0:T(8,128)S(1)} %slice_bitcast_fusion), channel_id=1, source_target_pairs={{0,4},{4,0},{8,12},{12,8},{16,20},{20,16},{24,28},{28,24},{1,5},{5... | collective-permute-start | bytes 98312 | tf_op jit(solution)/shard_map/ppermute | solution.py:44
  22.8 2.2 %collective-permute-start.9 = (f32[4,8,256]{2,1,0:T(8,128)S(1)}, f32[4,8,256]{2,1,0:T(8,128)S(1)}, u32[]{:S(2)}, u32[]{:S(2)}) collective-permute-start(f32[4,8,256]{2,1,0:T(8,128)S(1)} %slice.21), channel_id=1, source_target_pairs={{0,4},{4,0},{8,12},{12,8},{16,20},{20,16},{24,28},{28,24},{1,5},{5... | collective-permute-start | bytes 98312 | tf_op jit(solution)/shard_map/ppermute | solution.py:44
  23.3 1.7 %collective-permute-start.7 = (f32[4,8,256]{2,1,0:T(8,128)S(1)}, f32[4,8,256]{2,1,0:T(8,128)S(1)}, u32[]{:S(2)}, u32[]{:S(2)}) collective-permute-start(f32[4,8,256]{2,1,0:T(8,128)S(1)} %slice.20), channel_id=1, source_target_pairs={{0,4},{4,0},{8,12},{12,8},{16,20},{20,16},{24,28},{28,24},{1,5},{5... | collective-permute-start | bytes 98312 | tf_op jit(solution)/shard_map/ppermute | solution.py:44
  25.0 1.2 %collective-permute-start.11 = (f32[4,8,256]{2,1,0:T(8,128)S(1)}, f32[4,8,256]{2,1,0:T(8,128)S(1)}, u32[]{:S(2)}, u32[]{:S(2)}) collective-permute-start(f32[4,8,256]{2,1,0:T(8,128)S(1)} %slice.22), channel_id=1, source_target_pairs={{0,4},{4,0},{8,12},{12,8},{16,20},{20,16},{24,28},{28,24},{1,5},{5... | collective-permute-start | bytes 98312 | tf_op jit(solution)/shard_map/ppermute | solution.py:44

commit v10 on v9

--- a/solution.py
+++ b/solution.py
@@ -46,7 +46,7 @@
 
 def stage_kernel(bands, *refs):
     sources, targets, sems = refs[:6], refs[6:12], refs[12]
-    chip, high, at_edge = place(bands)
+    chip, high, _ = place(bands)
     rows, levels = sources[0].shape[1:3]
     per_row = levels // sources[3].shape[1]
     mine = row_at(high, rows, lax.div(chip, per_row)) * per_row + lax.rem(chip, per_row)
@@ -77,8 +77,8 @@
 
 
 def edges_kernel(bands, own_ref, partner_ref, zonal_ref, merid_ref, out_ref):
-    members, rows, levels, lon = own_ref.shape
-    chip, high, at_edge = place(bands)
+    members, rows, _, _ = own_ref.shape
+    _, high, _ = place(bands)
     edge = row_at(high, rows, 0)
     for m in range(2 * members):
         ref = own_ref if m < members else partner_ref
@@ -89,7 +89,7 @@
 
 
 def edge_message(bands, own, partner, zonal, merid):
-    members, rows, levels, lon = own.shape
+    members, _, levels, lon = own.shape
     return pl.pallas_call(
         functools.partial(edges_kernel, bands),
         out_shape=jax.ShapeDtypeStruct((4 * members + 2, levels, lon), jnp.float32),
@@ -119,9 +119,9 @@
 
 
 def inner_kernel(bands, own_ref, partner_ref, zonal_ref, merid_ref, first_ref, done_ref):
-    members, rows, levels, lon = own_ref.shape
+    members, rows, _, _ = own_ref.shape
     half = rows // 2
-    chip, high, at_edge = place(bands)
+    _, high, _ = place(bands)
     wind = [wind_row(high, rows, e, zonal_ref, merid_ref) for e in range(1, half + 1)]
     for m in range(2 * members):
         ref, k = (own_ref if m < members else partner_ref), m % members
@@ -150,7 +150,7 @@
     vsum_ref,
     *refs,
 ):
-    members, rows, levels, lon = own_ref.shape
+    members, rows, _, _ = own_ref.shape
     half = rows // 2
     out_refs, edge_ref = refs[:half], refs[half]
     chip, high, at_edge = place(bands)
@@ -272,7 +272,7 @@
 def analysis_kernel(regions, parts, *refs):
     ens_refs, (dsum_ref, vsum_ref) = refs[:parts], refs[parts : parts + 2]
     out_refs = refs[parts + 2 :]
-    share, lon = ens_refs[0].shape
+    share, _ = ens_refs[0].shape
     size = share * parts
     count = size // regions
 
@@ -456,7 +456,7 @@
     half = out_ref.shape[1] // 2
     got_refs, half_refs = refs[:half], refs[half : 2 * half]
     members = out_ref.shape[0]
-    chip, high, at_edge = place(bands)
+    chip, high, _ = place(bands)
     copies = []
     for t, ref in enumerate(half_refs):
         mine = row_at(high, 2 * half, row_of(chip, t, crossed))
@@ -514,7 +514,10 @@
 
     def exchange(blocks):
         if crossed:
-            return [blocks[0]] + [swap(b, groups, 2 * t) for t, b in enumerate(blocks) if t]
+            moved = [blocks[0]]
+            for t in range(1, chips):
+                moved.append(swap(blocks[t], groups, 2 * t))
+            return moved
         return [
             lax.all_to_all(
                 blocks[0], "member", 0, 0, tiled=True, axis_index_groups=same_core
@@ -531,7 +534,9 @@
     if not crossed:
         field = back[0].transpose(1, 0, 2, 3).reshape(2 * members, half, levels, lon)
         back = [field[:, t] for t in range(half)]
-    got = [swap(b[members:], groups, 1) for b in back]
+    got = []
+    for block in back:
+        got.append(swap(block[members:], groups, 1))
     return place_rows(bands, crossed, got, back, state.shape)
 
 
@@ -545,4 +550,5 @@
         P("lat", None, None),
     )
     out_specs = P("member", "lat", None, None)
+
     return jax.shard_map(body, mesh=mesh, in_specs=in_specs, out_specs=out_specs, check_vma=False)

time: 27.1 us -> 27.1 us (level)
  no operation moved by 1% of the time
where the time goes in v10:
time: 27.1 us; the launch traced here: 27 us
  waiting for transfers between devices  11.8 us (44%)
  starting transfers between devices  10.6 us (39%)
  Pallas kernels  4.52 us (17%)
    ppermute x11, waiting for transfers between devices, swap(): return lax.ppermute(x, 'member', [(i, i ^ distance) for i in range(groups)])  9.58 us
    ppermute x11, starting transfers between devices, swap(): return lax.ppermute(x, 'member', [(i, i ^ distance) for i in range(groups)])  7.62 us
    ppermute x1, starting transfers between devices, body(): halo = lax.ppermute(message, ('member', 'lat'), halo_pairs(groups, bands))  3 us
    ppermute x1, waiting for transfers between devices, body(): halo = lax.ppermute(message, ('member', 'lat'), halo_pairs(groups, bands))  2.17 us
    pallas_call x1, Pallas kernels, analysis(): pl.pallas_call(kernel, out_shape=(jax.ShapeDtypeStruct((share, lon), jnp....  1.53 us
    pallas_call x1, Pallas kernels, stage(): pl.pallas_call(functools.partial(stage_kernel, bands), out_shape=tuple((j...  1.01 us
    pallas_call x1, Pallas kernels, place_rows(): pl.pallas_call(functools.partial(place_rows_kernel, bands, crossed), out_...  0.76 us
    pallas_call x1, Pallas kernels, per_cell(): pl.pallas_call(cells_kernel, out_shape=(shape, shape), in_specs=whole(3),...  0.63 us
  transfers between devices with their start and end apart: 12, of which 9 were waited for; matrix products, arithmetic and copies ran while one was open for 0% of the time, Pallas kernels for 7%

profile of v10, /device:TPU:0, one launch (start us, length us, event | category | flops | bytes accessed | tf_op | source)
XLA Modules:
  0.0 27.0 jit_solution(6275901503572719239)
XLA Ops:
  0.0 0.5 %collective-permute-start = (f32[4,8,8,256]{3,2,1,0:T(8,128)}, f32[4,8,8,256]{3,2,1,0:T(8,128)S(1)}, u32[]{:S(2)}, u32[]{:S(2)}) collective-permute-start(f32[4,8,8,256]{3,2,1,0:T(8,128)} %refs_0_.1), channel_id=1, source_target_pairs={{0,4},{4,0},{8,12},{12,8},{16,20},{20,16},{24,28},{28,24},{1,5},{5... | collective-permute-start | bytes 786440 | tf_op jit(solution)/shard_map/ppermute | solution.py:44
  0.5 1.0 %stage.1 = (f32[4,8,8,256]{3,2,1,0:T(8,128)S(1)}, f32[8,8,256]{2,1,0:T(8,128)S(1)}, f32[8,8,256]{2,1,0:T(8,128)S(1)}, s32[8,128]{1,0:T(8,128)S(1)}, f32[8,128]{1,0:T(8,128)S(1)}, /*index=5*/f32[8,128]{1,0:T(8,128)S(1)}) custom-call(f32[4,8,8,256]{3,2,1,0:T(8,128)} %refs_0_.1, f32[8,8,256]{2,1,0:T(8,128)} %refs_1_.1, f32[8,8,256]{2,1,0:T(8,128)} %refs_2_.1, ...), custom_call_target="tpu_custom_call" | custom-call | bytes 2097152 | tf_op jit(solution)/shard_map/stage/pallas_call | solution.py:67
  1.5 0.4 %collective-permute-done.partner_ref = f32[4,8,8,256]{3,2,1,0:T(8,128)S(1)} collective-permute-done((f32[4,8,8,256]{3,2,1,0:T(8,128)}, f32[4,8,8,256]{3,2,1,0:T(8,128)S(1)}, u32[]{:S(2)}, u32[]{:S(2)}) %collective-permute-start) | collective-permute-done | bytes 262176 | tf_op jit(solution)/shard_map/ppermute | solution.py:44
  1.9 3.0 %collective-permute-start.1 = (f32[18,8,256]{2,1,0:T(8,128)S(1)}, f32[18,8,256]{2,1,0:T(8,128)S(1)}, u32[]{:S(2)}, u32[]{:S(2)}) collective-permute-start(f32[18,8,256]{2,1,0:T(8,128)S(1)} %edges.1), channel_id=1, source_target_pairs={{0,1},{1,0},{2,3},{3,2},{4,12},{5,6},{6,5},{7,15},{8,9},{9,8},{10,... | collective-permute-start | bytes 442376 | tf_op jit(solution)/shard_map/ppermute | solution.py:506
  4.9 0.6 %per_cell.1 = (f32[8,256]{1,0:T(8,128)S(1)}, f32[8,256]{1,0:T(8,128)S(1)}) custom-call(s32[8,128]{1,0:T(8,128)S(1)} %get-tuple-element.28.cell_ref, f32[8,128]{1,0:T(8,128)S(1)} %get-tuple-element.29.value_ref, f32[8,128]{1,0:T(8,128)S(1)} %get-tuple-element.30.weight_ref), custom_call_target="tpu_custom_call" | custom-call | flops 1048576 | bytes 28672 | tf_op jit(solution)/shard_map/per_cell/pallas_call | solution.py:244
  5.5 0.3 %forecast_inner.1 = (f32[4,8,8,256]{3,2,1,0:T(8,128)S(1)}, f32[2,8,8,256]{3,2,1,0:T(8,128)S(1)}) custom-call(f32[4,8,8,256]{3,2,1,0:T(8,128)S(1)} %get-tuple-element.23.own_ref, f32[4,8,8,256]{3,2,1,0:T(8,128)S(1)} %collective-permute-done.partner_ref, f32[8,8,256]{2,1,0:T(8,128)S(1)} %get-tuple-element.24.zonal_ref, ...), custom_call_target="tpu_custom_call" | custom-call | flops 1048576 | bytes 524288 | tf_op jit(solution)/shard_map/forecast_inner/pallas_call | solution.py:191
  5.8 2.2 %collective-permute-done.1.halo_ref = f32[18,8,256]{2,1,0:T(8,128)S(1)} collective-permute-done((f32[18,8,256]{2,1,0:T(8,128)S(1)}, f32[18,8,256]{2,1,0:T(8,128)S(1)}, u32[]{:S(2)}, u32[]{:S(2)}) %collective-permute-start.1) | collective-permute-done | bytes 147488 | tf_op jit(solution)/shard_map/ppermute | solution.py:506
  8.0 0.3 forecast_edge.1
  8.3 2.0 %collective-permute-start.2 = (f32[8,8,256]{2,1,0:T(8,128)S(1)}, f32[8,8,256]{2,1,0:T(8,128)S(1)}, u32[]{:S(2)}, u32[]{:S(2)}) collective-permute-start(f32[8,8,256]{2,1,0:T(8,128)S(1)} %get-tuple-element.34), channel_id=1, source_target_pairs={{0,8},{4,12},{8,0},{12,4},{16,24},{20,28},{24,16},{28,20},{1,9},{5... | collective-permute-start | bytes 196616 | tf_op jit(solution)/shard_map/ppermute | solution.py:44
  10.3 1.5 %collective-permute-start.3 = (f32[8,8,256]{2,1,0:T(8,128)S(1)}, f32[8,8,256]{2,1,0:T(8,128)S(1)}, u32[]{:S(2)}, u32[]{:S(2)}) collective-permute-start(f32[8,8,256]{2,1,0:T(8,128)S(1)} %get-tuple-element.35), channel_id=1, source_target_pairs={{0,16},{4,20},{8,24},{12,28},{16,0},{20,4},{24,8},{28,12},{1,17},{... | collective-permute-start | bytes 196616 | tf_op jit(solution)/shard_map/ppermute | solution.py:44
  11.8 0.0 collective-permute-start.4
  11.8 0.8 %collective-permute-done.2 = f32[8,8,256]{2,1,0:T(8,128)S(1)} collective-permute-done((f32[8,8,256]{2,1,0:T(8,128)S(1)}, f32[8,8,256]{2,1,0:T(8,128)S(1)}, u32[]{:S(2)}, u32[]{:S(2)}) %collective-permute-start.2) | collective-permute-done | bytes 65568 | tf_op jit(solution)/shard_map/ppermute | solution.py:44
  12.6 2.6 %collective-permute-done.3 = f32[8,8,256]{2,1,0:T(8,128)S(1)} collective-permute-done((f32[8,8,256]{2,1,0:T(8,128)S(1)}, f32[8,8,256]{2,1,0:T(8,128)S(1)}, u32[]{:S(2)}, u32[]{:S(2)}) %collective-permute-start.3) | collective-permute-done | bytes 65568 | tf_op jit(solution)/shard_map/ppermute | solution.py:44
  15.2 1.7 %collective-permute-done.4 = f32[8,8,256]{2,1,0:T(8,128)S(1)} collective-permute-done((f32[8,8,256]{2,1,0:T(8,128)S(1)}, f32[8,8,256]{2,1,0:T(8,128)S(1)}, u32[]{:S(2)}, u32[]{:S(2)}) %collective-permute-start.4) | collective-permute-done | bytes 65568 | tf_op jit(solution)/shard_map/ppermute | solution.py:44
  17.0 1.5 %analysis.1 = (f32[64,256]{1,0:T(8,128)S(1)}, f32[64,256]{1,0:T(8,128)S(1)}, f32[64,256]{1,0:T(8,128)S(1)}, f32[64,256]{1,0:T(8,128)S(1)}) custom-call(f32[64,256]{1,0:T(8,128)S(1)} %bitcast.12, f32[64,256]{1,0:T(8,128)S(1)} %bitcast.14, f32[64,256]{1,0:T(8,128)S(1)} %bitcast.16, f32[64,256]{1,0:T(8,128)S(1)} %bitcast.17, ...), custom_call_target="tpu_custom_call" | custom-call | flops 805306368 | bytes 524288 | tf_op jit(solution)/shard_map/analysis/pallas_call | solution.py:441
  18.5 0.6 %collective-permute-start.8 = (f32[8,8,256]{2,1,0:T(8,128)S(1)}, f32[8,8,256]{2,1,0:T(8,128)S(1)}, u32[]{:S(2)}, u32[]{:S(2)}) collective-permute-start(f32[8,8,256]{2,1,0:T(8,128)S(1)} %bitcast.15), channel_id=1, source_target_pairs={{0,16},{4,20},{8,24},{12,28},{16,0},{20,4},{24,8},{28,12},{1,17},{... | collective-permute-start | bytes 196616 | tf_op jit(solution)/shard_map/ppermute | solution.py:44
  19.1 0.1 collective-permute-start.6
  19.2 2.9 %collective-permute-start.10 = (f32[8,8,256]{2,1,0:T(8,128)S(1)}, f32[8,8,256]{2,1,0:T(8,128)S(1)}, u32[]{:S(2)}, u32[]{:S(2)}) collective-permute-start(f32[8,8,256]{2,1,0:T(8,128)S(1)} %bitcast.11), channel_id=1, source_target_pairs={{0,24},{4,28},{8,16},{12,20},{16,8},{20,12},{24,0},{28,4},{1,25},{... | collective-permute-start | bytes 196616 | tf_op jit(solution)/shard_map/ppermute | solution.py:44
  22.1 0.0 collective-permute-start.5
  22.1 0.8 %collective-permute-done.8.refs_6_ = f32[8,8,256]{2,1,0:T(8,128)S(1)} collective-permute-done((f32[8,8,256]{2,1,0:T(8,128)S(1)}, f32[8,8,256]{2,1,0:T(8,128)S(1)}, u32[]{:S(2)}, u32[]{:S(2)}) %collective-permute-start.8) | collective-permute-done | bytes 65568 | tf_op jit(solution)/shard_map/ppermute | solution.py:44
  22.8 0.0 collective-permute-start.9
  22.8 0.5 %collective-permute-done.6.refs_5_ = f32[8,8,256]{2,1,0:T(8,128)S(1)} collective-permute-done((f32[8,8,256]{2,1,0:T(8,128)S(1)}, f32[8,8,256]{2,1,0:T(8,128)S(1)}, u32[]{:S(2)}, u32[]{:S(2)}) %collective-permute-start.6) | collective-permute-done | bytes 65568 | tf_op jit(solution)/shard_map/ppermute | solution.py:44
  23.3 0.0 collective-permute-start.7
  23.3 1.6 %collective-permute-done.10.refs_7_ = f32[8,8,256]{2,1,0:T(8,128)S(1)} collective-permute-done((f32[8,8,256]{2,1,0:T(8,128)S(1)}, f32[8,8,256]{2,1,0:T(8,128)S(1)}, u32[]{:S(2)}, u32[]{:S(2)}) %collective-permute-start.10) | collective-permute-done | bytes 65568 | tf_op jit(solution)/shard_map/ppermute | solution.py:44
  25.0 0.0 collective-permute-start.11
  25.0 0.0 collective-permute-done.5.refs_0_
  25.0 0.0 collective-permute-done.9.refs_2_
  25.0 0.0 collective-permute-done.7.refs_1_
  25.0 1.2 %collective-permute-done.11.refs_3_ = f32[4,8,256]{2,1,0:T(8,128)S(1)} collective-permute-done((f32[4,8,256]{2,1,0:T(8,128)S(1)}, f32[4,8,256]{2,1,0:T(8,128)S(1)}, u32[]{:S(2)}, u32[]{:S(2)}) %collective-permute-start.11) | collective-permute-done | bytes 32800 | tf_op jit(solution)/shard_map/ppermute | solution.py:44
  26.2 0.8 %place_rows.1 = f32[4,8,8,256]{3,2,1,0:T(8,128)} custom-call(f32[4,8,256]{2,1,0:T(8,128)S(1)} %collective-permute-done.5.refs_0_, f32[4,8,256]{2,1,0:T(8,128)S(1)} %collective-permute-done.7.refs_1_, f32[4,8,256]{2,1,0:T(8,128)S(1)} %collective-permute-done.9.refs_2_, f32[4,8,256]{2,1,0:T(8,128)S(1)} %collective-permute-done.11.refs_3_, ...), custom_call_target="tpu_custom_call" | custom-call | tf_op jit(solution)/shard_map/place_rows/pallas_call | solution.py:476
  (5 shorter events, 0.0 us)
Async XLA Ops:
  0.0 1.9 %collective-permute-start = (f32[4,8,8,256]{3,2,1,0:T(8,128)}, f32[4,8,8,256]{3,2,1,0:T(8,128)S(1)}, u32[]{:S(2)}, u32[]{:S(2)}) collective-permute-start(f32[4,8,8,256]{3,2,1,0:T(8,128)} %refs_0_.1), channel_id=1, source_target_pairs={{0,4},{4,0},{8,12},{12,8},{16,20},{20,16},{24,28},{28,24},{1,5},{5... | collective-permute-start | bytes 786440 | tf_op jit(solution)/shard_map/ppermute | solution.py:44
  1.9 6.1 %collective-permute-start.1 = (f32[18,8,256]{2,1,0:T(8,128)S(1)}, f32[18,8,256]{2,1,0:T(8,128)S(1)}, u32[]{:S(2)}, u32[]{:S(2)}) collective-permute-start(f32[18,8,256]{2,1,0:T(8,128)S(1)} %edges.1), channel_id=1, source_target_pairs={{0,1},{1,0},{2,3},{3,2},{4,12},{5,6},{6,5},{7,15},{8,9},{9,8},{10,... | collective-permute-start | bytes 442376 | tf_op jit(solution)/shard_map/ppermute | solution.py:506
  8.3 4.3 %collective-permute-start.2 = (f32[8,8,256]{2,1,0:T(8,128)S(1)}, f32[8,8,256]{2,1,0:T(8,128)S(1)}, u32[]{:S(2)}, u32[]{:S(2)}) collective-permute-start(f32[8,8,256]{2,1,0:T(8,128)S(1)} %get-tuple-element.34), channel_id=1, source_target_pairs={{0,8},{4,12},{8,0},{12,4},{16,24},{20,28},{24,16},{28,20},{1,9},{5... | collective-permute-start | bytes 196616 | tf_op jit(solution)/shard_map/ppermute | solution.py:44
  10.3 5.0 %collective-permute-start.3 = (f32[8,8,256]{2,1,0:T(8,128)S(1)}, f32[8,8,256]{2,1,0:T(8,128)S(1)}, u32[]{:S(2)}, u32[]{:S(2)}) collective-permute-start(f32[8,8,256]{2,1,0:T(8,128)S(1)} %get-tuple-element.35), channel_id=1, source_target_pairs={{0,16},{4,20},{8,24},{12,28},{16,0},{20,4},{24,8},{28,12},{1,17},{... | collective-permute-start | bytes 196616 | tf_op jit(solution)/shard_map/ppermute | solution.py:44
  11.8 5.2 %collective-permute-start.4 = (f32[8,8,256]{2,1,0:T(8,128)S(1)}, f32[8,8,256]{2,1,0:T(8,128)S(1)}, u32[]{:S(2)}, u32[]{:S(2)}) collective-permute-start(f32[8,8,256]{2,1,0:T(8,128)S(1)} %get-tuple-element.36), channel_id=1, source_target_pairs={{0,24},{4,28},{8,16},{12,20},{16,8},{20,12},{24,0},{28,4},{1,25},{... | collective-permute-start | bytes 196616 | tf_op jit(solution)/shard_map/ppermute | solution.py:44
  18.5 4.3 %collective-permute-start.8 = (f32[8,8,256]{2,1,0:T(8,128)S(1)}, f32[8,8,256]{2,1,0:T(8,128)S(1)}, u32[]{:S(2)}, u32[]{:S(2)}) collective-permute-start(f32[8,8,256]{2,1,0:T(8,128)S(1)} %bitcast.15), channel_id=1, source_target_pairs={{0,16},{4,20},{8,24},{12,28},{16,0},{20,4},{24,8},{28,12},{1,17},{... | collective-permute-start | bytes 196616 | tf_op jit(solution)/shard_map/ppermute | solution.py:44
  19.1 4.3 %collective-permute-start.6 = (f32[8,8,256]{2,1,0:T(8,128)S(1)}, f32[8,8,256]{2,1,0:T(8,128)S(1)}, u32[]{:S(2)}, u32[]{:S(2)}) collective-permute-start(f32[8,8,256]{2,1,0:T(8,128)S(1)} %bitcast.13), channel_id=1, source_target_pairs={{0,8},{4,12},{8,0},{12,4},{16,24},{20,28},{24,16},{28,20},{1,9},{5... | collective-permute-start | bytes 196616 | tf_op jit(solution)/shard_map/ppermute | solution.py:44
  19.2 5.8 %collective-permute-start.10 = (f32[8,8,256]{2,1,0:T(8,128)S(1)}, f32[8,8,256]{2,1,0:T(8,128)S(1)}, u32[]{:S(2)}, u32[]{:S(2)}) collective-permute-start(f32[8,8,256]{2,1,0:T(8,128)S(1)} %bitcast.11), channel_id=1, source_target_pairs={{0,24},{4,28},{8,16},{12,20},{16,8},{20,12},{24,0},{28,4},{1,25},{... | collective-permute-start | bytes 196616 | tf_op jit(solution)/shard_map/ppermute | solution.py:44
  22.1 2.9 %collective-permute-start.5 = (f32[4,8,256]{2,1,0:T(8,128)S(1)}, f32[4,8,256]{2,1,0:T(8,128)S(1)}, u32[]{:S(2)}, u32[]{:S(2)}) collective-permute-start(f32[4,8,256]{2,1,0:T(8,128)S(1)} %slice_bitcast_fusion), channel_id=1, source_target_pairs={{0,4},{4,0},{8,12},{12,8},{16,20},{20,16},{24,28},{28,24},{1,5},{5... | collective-permute-start | bytes 98312 | tf_op jit(solution)/shard_map/ppermute | solution.py:44
  22.8 2.2 %collective-permute-start.9 = (f32[4,8,256]{2,1,0:T(8,128)S(1)}, f32[4,8,256]{2,1,0:T(8,128)S(1)}, u32[]{:S(2)}, u32[]{:S(2)}) collective-permute-start(f32[4,8,256]{2,1,0:T(8,128)S(1)} %slice.21), channel_id=1, source_target_pairs={{0,4},{4,0},{8,12},{12,8},{16,20},{20,16},{24,28},{28,24},{1,5},{5... | collective-permute-start | bytes 98312 | tf_op jit(solution)/shard_map/ppermute | solution.py:44
  23.3 1.7 %collective-permute-start.7 = (f32[4,8,256]{2,1,0:T(8,128)S(1)}, f32[4,8,256]{2,1,0:T(8,128)S(1)}, u32[]{:S(2)}, u32[]{:S(2)}) collective-permute-start(f32[4,8,256]{2,1,0:T(8,128)S(1)} %slice.20), channel_id=1, source_target_pairs={{0,4},{4,0},{8,12},{12,8},{16,20},{20,16},{24,28},{28,24},{1,5},{5... | collective-permute-start | bytes 98312 | tf_op jit(solution)/shard_map/ppermute | solution.py:44
  25.0 1.2 %collective-permute-start.11 = (f32[4,8,256]{2,1,0:T(8,128)S(1)}, f32[4,8,256]{2,1,0:T(8,128)S(1)}, u32[]{:S(2)}, u32[]{:S(2)}) collective-permute-start(f32[4,8,256]{2,1,0:T(8,128)S(1)} %slice.22), channel_id=1, source_target_pairs={{0,4},{4,0},{8,12},{12,8},{16,20},{20,16},{24,28},{28,24},{1,5},{5... | collective-permute-start | bytes 98312 | tf_op jit(solution)/shard_map/ppermute | solution.py:44
